TPU v7x, 512 devices: a whole 4x8x8 slice. The times are simulated.
512 devices in a mesh: shard: 128 (over y, z, core), tensor: 4 (over x).
Axes of the slice: x: 4, y: 8, z: 8, core: 2. Of those that a mesh axis runs over, the one named last changes fastest.
Arguments:
- grad_query: bfloat16 [128, 1024, 512], P('shard', None, 'tensor'), may hold values from -8 to 8
- error_query: float32 [128, 1024, 512], P('shard', None, 'tensor'), may hold values from -3 to 3
- grad_output: bfloat16 [128, 512, 1024], P('shard', 'tensor'), may hold values from -8 to 8
- error_output: float32 [128, 512, 1024], P('shard', 'tensor'), may hold values from -3 to 3
- start_query: float32 [512, 32], P('tensor'), may hold values from -6 to 6
- start_output: float32 [1024, 32], replicated, may hold values from -6 to 6
- weight_query: float32 [1024, 512], P('shard', 'tensor'), may hold values from -0.1875 to 0.1875
- weight_output: float32 [512, 1024], P('tensor', 'shard'), may hold values from -0.25 to 0.25
- moment_query: float32 [1024, 512], P('shard', 'tensor'), may hold values from -1.2 to 1.2
- moment_output: float32 [512, 1024], P('tensor', 'shard'), may hold values from -1.2 to 1.2
- grad_vector: bfloat16 [128, 3584], P('shard'), may hold values from -12 to 12
- moment_vector: float32 [3584], P('shard'), may hold values from -1.2 to 1.2
- weight_vector: float32 [3584], P('shard'), may hold values from 0.5 to 1.5
Outputs:
- new_error_query: float32 [128, 1024, 512], P('shard', None, 'tensor')
- new_error_output: float32 [128, 512, 1024], P('shard', 'tensor')
- new_moment_query: float32 [1024, 512], P('shard', 'tensor')
- new_moment_output: float32 [512, 1024], P('tensor', 'shard')
- new_weight_query: float32 [1024, 512], P(None, 'tensor')
- new_weight_output: float32 [512, 1024], P('tensor')
- new_moment_vector: float32 [3584], P('shard')
- new_weight_vector: float32 [3584], replicated
All inputs are finite; a program needn't handle non-finite values.
Results may differ from a plain program's by a relative error of at most 0.0003.
Values sent between devices are 32-bit elements; how exact they have to be, the bound alone decides.
No kernel may reach another device: no remote copies, remote signals or barrier semaphores. Data moves between devices by JAX's collectives and lax.ppermute only.
A program may use at most 64 MiB of HBM per device.

v0:
```python
import jax
import jax.numpy as jnp
from jax import lax
from jax.sharding import PartitionSpec as P

ROUNDS = 2


highest = lax.Precision.HIGHEST


def product(left, right):
    return jnp.dot(left, right, precision=highest, preferred_element_type=jnp.float32)


def product_inner(left, right):
    return lax.dot_general(
        left, right, (((0,), (0,)), ((), ())), precision=highest, preferred_element_type=jnp.float32
    )


def solve_rows(gram, factor):
    lower = jnp.linalg.cholesky(gram)
    return jax.scipy.linalg.solve_triangular(lower, factor.T, lower=True).T


def orthonormal(factor):
    return solve_rows(product_inner(factor, factor), factor)


def orthonormal_rows(factor):
    gram = lax.psum(product_inner(factor, factor), "tensor")
    return solve_rows(gram, factor)


def local(
    grad_query,
    error_query,
    grad_output,
    error_output,
    start_query,
    start_output,
    weight_query,
    weight_output,
    moment_query,
    moment_output,
    grad_vector,
    moment_vector,
    weight_vector,
):
    replicas = lax.axis_size("shard")
    shard_index = lax.axis_index("shard")
    total_query = grad_query[0].astype(jnp.float32) + error_query[0]
    total_output = grad_output[0].astype(jnp.float32) + error_output[0]
    factor_query = start_query
    factor_output = start_output
    for turn in range(ROUNDS):
        part_query = product(total_query, factor_query)
        part_output = product(total_output, factor_output)
        sum_query = lax.psum(part_query, ("shard", "tensor"))
        sum_output = lax.psum(part_output, "shard")
        left_query = orthonormal(sum_query)
        left_output = orthonormal_rows(sum_output)
        right_query_part = product_inner(total_query, left_query)
        right_output_part = product_inner(total_output, left_output)
        factor_query = lax.psum(right_query_part, "shard")
        factor_output = lax.psum(right_output_part, ("shard", "tensor"))
    approx_query = product(left_query, factor_query.T) / replicas
    approx_output = product(left_output, factor_output.T) / replicas
    new_error_query = (total_query - approx_query)[None]
    new_error_output = (total_output - approx_output)[None]
    rows_block = moment_query.shape[0]
    block_query = lax.dynamic_slice_in_dim(approx_query, shard_index * rows_block, rows_block, 0)
    cols_block = moment_output.shape[1]
    block_output = lax.dynamic_slice_in_dim(approx_output, shard_index * cols_block, cols_block, 1)
    new_moment_query = 0.9 * moment_query + block_query
    new_moment_output = 0.9 * moment_output + block_output
    stepped_query = weight_query - 0.01 * new_moment_query
    stepped_output = weight_output - 0.01 * new_moment_output
    local_vector = grad_vector[0].astype(jnp.float32)
    vector_block = moment_vector.shape[0]
    vector_whole = lax.psum(local_vector, "shard")
    vector_part = lax.dynamic_slice_in_dim(
        vector_whole, shard_index * vector_block, vector_block, 0
    )
    vector_mean = vector_part / replicas
    new_moment_vector = 0.9 * moment_vector + vector_mean
    stepped_vector = weight_vector - 0.01 * new_moment_vector
    new_weight_query, new_weight_output, new_weight_vector = (
        lax.all_gather(stepped_query, "shard", axis=0, tiled=True),
        lax.all_gather(stepped_output, "shard", axis=1, tiled=True),
        lax.all_gather(stepped_vector, "shard", axis=0, tiled=True),
    )
    return (
        new_error_query,
        new_error_output,
        new_moment_query,
        new_moment_output,
        new_weight_query,
        new_weight_output,
        new_moment_vector,
        new_weight_vector,
    )


def solution(mesh):
    in_specs = (
        P("shard", None, "tensor"),
        P("shard", None, "tensor"),
        P("shard", "tensor", None),
        P("shard", "tensor", None),
        P("tensor", None),
        P(),
        P("shard", "tensor"),
        P("tensor", "shard"),
        P("shard", "tensor"),
        P("tensor", "shard"),
        P("shard", None),
        P("shard"),
        P("shard"),
    )
    out_specs = (
        P("shard", None, "tensor"),
        P("shard", "tensor", None),
        P("shard", "tensor"),
        P("tensor", "shard"),
        P(None, "tensor"),
        P("tensor", None),
        P("shard"),
        P(),
    )
    return jax.shard_map(local, mesh=mesh, in_specs=in_specs, out_specs=out_specs, check_vma=False)
```

profile of v0, /device:TPU:1, one launch (start us, length us, event | category | flops | bytes accessed | tf_op | source)
XLA Modules:
  0.0 2203.4 jit_solution(7634404734054702130)
XLA Ops:
  7.2 1.2 copy.45
  8.6 0.4 fusion.6
  9.1 498.1 %psum.81 = f32[128,32]{0,1:T(8,128)S(1)} all-reduce(f32[128,32]{0,1:T(8,128)S(1)} %fusion.6), channel_id=1, replica_groups=mesh['shard'=128,'tensor'=4] {'shard'}, use_global_device_ids=true, to_apply=%region_6.9 | all-reduce | flops 4096 | bytes 32768 | tf_op jit(solution)/shard_map/psum | solution.py:61
  507.3 13.2 psum.82
  520.6 2.9 cholesky.96
  523.6 0.6 compare_reduce_fusion.1
  524.2 0.7 fusion.24
  524.9 2.4 custom-call.12
  527.6 1.3 fusion.4
  528.9 1.3 fusion.15
  530.3 1.3 dynamic-slice
  532.3 265.7 %all-reduce.10.cloned.1.call-done = (f32[1024,32]{0,1:T(8,128)}, f32[1024,32]{0,1:T(8,128)}) async-done(((f32[1024,32]{0,1:T(8,128)}, f32[1024,32]{0,1:T(8,128)}), (f32[1024,32]{0,1:T(8,128)}, f32[1024,32]{0,1:T(8,128)})) %all-reduce.10.cloned.1.call-update) | async-done | bytes 262160 | tf_op jit(solution)/shard_map/psum | solution.py:60
  798.0 1.4 fusion.2
  799.7 2.9 cholesky.74
  802.7 0.6 compare_reduce_fusion.3
  803.3 0.7 fusion.22
  804.0 2.4 custom-call.10
  806.4 0.3 fusion.20
  806.8 0.4 fusion.13
  807.2 487.8 %all-reduce.4 = (f32[128,32]{0,1:T(8,128)S(1)}, f32[128,32]{0,1:T(8,128)S(1)}, f32[3584]{0:T(1024)S(1)}) all-reduce(f32[128,32]{0,1:T(8,128)S(1)} %fusion.13, f32[128,32]{0,1:T(8,128)S(1)} %fusion.2, f32[3584]{0:T(1024)S(1)} %convert_reduce_fusion), channel_id=1, replica_groups=mesh['shard'=128,'tensor'=4] {'shard'}, use_global_device_ids=true, to_apply=%region_3.6 | all-reduce | flops 11776 | bytes 94208 | tf_op jit(solution)/shard_map/psum | solution.py:66
  1295.2 12.4 psum.85
  1307.6 2.9 cholesky.107
  1310.6 0.6 compare_reduce_fusion
  1311.2 0.7 fusion.25
  1311.9 2.4 custom-call.13
  1314.6 1.3 fusion.11
  1315.9 1.3 fusion
  1317.3 0.6 copy-done.13
  1317.9 0.6 subtract_dynamic-update-slice_fusion
  1318.5 270.5 %all-reduce.8.cloned.1.call-done = (f32[1024,32]{0,1:T(8,128)}, f32[1024,32]{0,1:T(8,128)}) async-done(((f32[1024,32]{0,1:T(8,128)}, f32[1024,32]{0,1:T(8,128)}), (f32[1024,32]{0,1:T(8,128)}, f32[1024,32]{0,1:T(8,128)})) %all-reduce.8.cloned.1.call-update) | async-done | bytes 262160 | tf_op jit(solution)/shard_map/psum | solution.py:60
  1589.0 1.2 fusion.41
  1590.3 2.9 cholesky.85
  1593.3 0.6 compare_reduce_fusion.2
  1593.9 0.7 fusion.23
  1594.6 2.4 custom-call.11
  1597.0 0.3 fusion.18
  1597.4 0.4 fusion.9
  1597.8 487.8 %all-reduce.3 = (f32[128,32]{0,1:T(8,128)S(1)}, f32[3584]{0:T(1024)}) all-reduce(f32[128,32]{0,1:T(8,128)S(1)} %fusion.9, f32[3584]{0:T(1024)S(1)} %get-tuple-element.48), channel_id=1, replica_groups=mesh['shard'=128,'tensor'=4] {'shard'}, use_global_device_ids=true, to_apply=%region_5.8 | all-reduce | flops 7680 | bytes 61440 | tf_op jit(solution)/shard_map/psum | solution.py:66
  2085.6 1.0 convolution_multiply_fusion.1
  2086.6 0.9 fusion.17
  2087.5 1.0 convolution_multiply_fusion
  2088.6 1.0 copy.52
  2089.6 0.6 multiply_subtract_fusion
  2090.2 53.0 %all_gather.10 = f32[128,1024]{0,1:T(8,128)S(1)} all-gather(f32[128,8]{0,1:T(8,128)S(1)} %get-tuple-element.44), channel_id=1, replica_groups=mesh['shard'=128,'tensor'=4] {'shard'}, dimensions={1}, use_global_device_ids=true | all-gather | bytes 528384 | tf_op jit(solution)/shard_map/all_gather | solution.py:91
  2143.3 1.0 copy.53
  2144.3 0.6 multiply_subtract_fusion.1
  2144.9 50.9 %all_gather.9 = f32[1024,128]{1,0:T(8,128)S(1)} all-gather(f32[8,128]{1,0:T(8,128)S(1)} %get-tuple-element.46), channel_id=1, replica_groups=mesh['shard'=128,'tensor'=4] {'shard'}, dimensions={0}, use_global_device_ids=true | all-gather | bytes 528384 | tf_op jit(solution)/shard_map/all_gather | solution.py:90
  2195.8 0.8 copy.63
  (54 shorter events, 2.0 us)
Async XLA Ops:
  7.2 1.5 copy-start
  7.2 1.2 copy-start.5
  7.2 790.8 %all-reduce.10.cloned.1.call-start = ((), (), s32[]{:S(2)}) async-start(), calls=%async_computation.1 | async-start | bytes 524288 | tf_op jit(solution)/shard_map/psum | solution.py:60
  520.6 8.3 copy-start.1
  527.6 1.3 copy-start.2
  527.6 1.3 copy-start.7
  530.3 1058.7 %all-reduce.8.cloned.1.call-start = ((), (), s32[]{:S(2)}) async-start(), calls=%async_computation | async-start | bytes 524288 | tf_op jit(solution)/shard_map/psum | solution.py:60
  530.3 1.9 copy-start.8
  798.0 1.4 copy-start.3
  1317.2 0.7 copy-start.13
  1317.2 0.7 copy-start.14
  1590.2 6.8 copy-start.4
  2086.6 0.9 copy-start.6
  2088.6 1.0 copy-start.9
  2088.6 1.0 copy-start.10
  2143.3 1.0 copy-start.11
  2143.3 1.0 copy-start.12
Sparse Core Ops, SparseCore 0:
  530.4 267.5 all-reduce.9
  1317.3 271.6 all-reduce.7
where the time goes:
time: 2200 us
  blocking collectives  1600 us (73%)
  waiting for transfers between devices  536 us (24%)
  other arithmetic  29.5 us (1%)
    psum x2, blocking collectives, local(): factor_query = lax.psum(right_query_part, 'shard')  976 us
    psum x2, waiting for transfers between devices, local(): sum_query = lax.psum(part_query, ('shard', 'tensor'))  536 us
    psum x1, blocking collectives, local(): sum_output = lax.psum(part_output, 'shard')  498 us
    all_gather x1, blocking collectives, local(): lax.all_gather(stepped_output, 'shard', axis=1, tiled=True)  53 us
    all_gather x1, blocking collectives, local(): lax.all_gather(stepped_query, 'shard', axis=0, tiled=True)  50.9 us
  transfers between devices with their start and end apart: 2, of which 2 were waited for; matrix products, arithmetic and copies ran while one was open for 0% of the time, Pallas kernels for 0%

commit v1 on v0

v1 whole, which is shorter than its diff:
```python
import jax
import jax.numpy as jnp
import numpy as np
from jax import lax
from jax.sharding import PartitionSpec as P

ROUNDS = 2
LANES = 128

highest = lax.Precision.HIGHEST


def dot(left, right, dims):
    return lax.dot_general(left, right, (dims, ((), ())), precision=highest, preferred_element_type=jnp.float32)


def ring_size(shards):
    ring = int(round((shards // 2) ** 0.5))
    assert 2 * ring * ring == shards
    return ring


def groups(ring):
    along_y = [[[(2 * (ring * y + z)) + c for y in range(ring)] for z in range(ring)] for c in range(2)]
    along_z = [[[(2 * (ring * y + z)) + c for z in range(ring)] for y in range(ring)] for c in range(2)]
    return along_y[0] + along_z[1], along_z[0] + along_y[1]


def swap_cores(value, shards):
    return lax.ppermute(value, "shard", [(s, s ^ 1) for s in range(shards)])


def exchange(value, group):
    return lax.all_to_all(value, "shard", 0, 0, axis_index_groups=group, tiled=True)


def share(value, group, size):
    return exchange(jnp.broadcast_to(value[None], (size, *value.shape)), group)


def inverse_lower(gram):
    lower = jnp.linalg.cholesky(gram)
    eye = jnp.eye(gram.shape[0], dtype=gram.dtype)
    return jax.scipy.linalg.solve_triangular(lower, eye, lower=True)


def local(
    grad_query,
    error_query,
    grad_output,
    error_output,
    start_query,
    start_output,
    weight_query,
    weight_output,
    moment_query,
    moment_output,
    grad_vector,
    moment_vector,
    weight_vector,
):
    shards = lax.axis_size("shard")
    tensors = lax.axis_size("tensor")
    index = lax.axis_index("shard")
    ring = ring_size(shards)
    first, second = groups(ring)
    even = (index % 2) == 0
    width = start_query.shape[0]
    height = start_output.shape[0]
    rank = start_query.shape[1]
    block = height // ring
    rows = height // shards
    vec = grad_vector.shape[1]
    piece = vec // ring
    small = vec // shards
    assert width == LANES and rows % 8 == 0 or rows * shards == height
    vec_rows = -(-piece // (8 * LANES)) * 8

    total_query = grad_query[0].astype(jnp.float32) + error_query[0]
    total_output = grad_output[0].astype(jnp.float32) + error_output[0]
    query_blocks = total_query.reshape(ring, block, width)
    output_blocks = total_output.reshape(width, ring, block).transpose(1, 0, 2)
    vector_blocks = jnp.pad(
        grad_vector[0].astype(jnp.float32).reshape(ring, piece), ((0, 0), (0, vec_rows * LANES - piece))
    ).reshape(ring, vec_rows, LANES)

    kept_query = weight_query - 0.009 * moment_query
    kept_output = (weight_output - 0.009 * moment_output).T
    kept_vector = jnp.pad(weight_vector - 0.009 * moment_vector, (0, LANES - small))

    mine = jnp.where(even, query_blocks, output_blocks)
    theirs = jnp.where(even, output_blocks, query_blocks)
    own_kept = jnp.where(even, kept_query, kept_output)
    other_kept = jnp.where(even, kept_output, kept_query)
    sent = jnp.concatenate([
        jnp.concatenate([theirs, vector_blocks], axis=1).reshape(-1, LANES),
        other_kept,
        jnp.pad(kept_vector[None], ((0, 7), (0, 0))),
    ])
    got = swap_cores(sent, shards)
    tall = ring * (block + vec_rows)
    summed = jnp.concatenate([mine, vector_blocks], axis=1) + got[:tall].reshape(ring, block + vec_rows, LANES)
    got_kept = got[tall:tall + rows]
    got_vector = got[tall + rows, :small]
    own_vector = kept_vector[:small]
    pair_kept = jnp.where(even, jnp.concatenate([own_kept, got_kept]), jnp.concatenate([got_kept, own_kept]))
    pair_vector = jnp.where(even, jnp.concatenate([own_vector, got_vector]), jnp.concatenate([got_vector, own_vector]))
    pair_vector = jnp.pad(pair_vector[None], ((0, 7), (0, LANES - 2 * small)))

    part = exchange(summed, first).sum(0)
    every = share(jnp.concatenate([part, pair_kept, pair_vector]), second, ring)
    whole = every[:, :block + vec_rows].sum(0)
    square = jnp.where(even, whole[:block], whole[:block].T)
    kept_rows = every[:, block + vec_rows:block + vec_rows + 2 * rows].reshape(block, LANES)
    kept_vectors = every[:, block + vec_rows + 2 * rows]
    every = share(jnp.concatenate([square, whole[block:], kept_rows, kept_vectors]), first, ring)
    matrix = every[:, :block].reshape(height, width)
    vector_sum = every[:, block:block + vec_rows].reshape(ring, -1)[:, :piece].reshape(vec)
    kept_all = every[:, block + vec_rows:2 * block + vec_rows].reshape(ring, ring, 2 * rows, LANES)
    kept_all = jnp.where(even, kept_all, kept_all.transpose(1, 0, 2, 3)).reshape(height, LANES)
    kept_vectors = every[:, 2 * block + vec_rows:][:, :, :2 * small]
    kept_vectors = jnp.where(even, kept_vectors, kept_vectors.transpose(1, 0, 2)).reshape(vec)
    kept_other = swap_cores(kept_all, shards)

    narrow = jnp.where(even, start_query.T, dot(start_output, matrix, ((0,), (0,))))
    for turn in range(ROUNDS):
        wide = dot(narrow, matrix, ((1,), (1,)))
        gram = jnp.pad(dot(narrow, narrow, ((1,), (1,))), ((0, 0), (0, LANES - rank)))
        sent = jnp.concatenate([wide, gram], axis=1)
        got = lax.all_to_all(jnp.broadcast_to(sent[None], (tensors, *sent.shape)), "tensor", 0, 0, tiled=True).sum(0)
        wide = got[:, :height]
        gram = jnp.where(even, dot(wide, wide, ((1,), (1,))), got[:, height:height + rank])
        inverse = inverse_lower(gram)
        wide = dot(inverse, wide, ((1,), (0,)))
        scaled = dot(inverse, narrow, ((1,), (0,)))
        narrow = dot(wide, matrix, ((1,), (0,)))
    mine = jnp.concatenate([wide, jnp.where(even, narrow, scaled)], axis=1)
    other = swap_cores(mine, shards)
    of_query = jnp.where(even, mine, other)
    of_output = jnp.where(even, other, mine)
    approx_query = dot(of_query[:, :height], of_query[:, height:], ((0,), (0,))) / shards
    approx_output = dot(of_output[:, height:], of_output[:, :height], ((0,), (0,))) / shards
    kept_query = jnp.where(even, kept_all, kept_other)
    kept_output = jnp.where(even, kept_other, kept_all).T

    new_error_query = (total_query - approx_query)[None]
    new_error_output = (total_output - approx_output)[None]
    block_query = lax.dynamic_slice_in_dim(approx_query, index * rows, rows, 0)
    block_output = lax.dynamic_slice_in_dim(approx_output, index * rows, rows, 1)
    new_moment_query = 0.9 * moment_query + block_query
    new_moment_output = 0.9 * moment_output + block_output
    new_weight_query = kept_query - 0.01 * approx_query
    new_weight_output = kept_output - 0.01 * approx_output
    vector_mean = vector_sum / shards
    new_moment_vector = 0.9 * moment_vector + lax.dynamic_slice_in_dim(vector_mean, index * small, small, 0)
    new_weight_vector = kept_vectors - 0.01 * vector_mean
    return (
        new_error_query,
        new_error_output,
        new_moment_query,
        new_moment_output,
        new_weight_query,
        new_weight_output,
        new_moment_vector,
        new_weight_vector,
    )


def solution(mesh):
    in_specs = (
        P("shard", None, "tensor"),
        P("shard", None, "tensor"),
        P("shard", "tensor", None),
        P("shard", "tensor", None),
        P("tensor", None),
        P(),
        P("shard", "tensor"),
        P("tensor", "shard"),
        P("shard", "tensor"),
        P("tensor", "shard"),
        P("shard", None),
        P("shard"),
        P("shard"),
    )
    out_specs = (
        P("shard", None, "tensor"),
        P("shard", "tensor", None),
        P("shard", "tensor"),
        P("tensor", "shard"),
        P(None, "tensor"),
        P("tensor", None),
        P("shard"),
        P(),
    )
    return jax.shard_map(local, mesh=mesh, in_specs=in_specs, out_specs=out_specs, check_vma=False)
```

time: 2200 us -> 143 us (0.07)
  blocking collectives: 1600 us -> 20.2 us
  waiting for transfers between devices: 536 us -> 39.2 us
  starting transfers between devices: 0.08 us -> 40 us
    psum x5 -> x0, blocking collectives: 1500 us -> none  [the longest x2 976 us: local(): factor_query = lax.psum(right_query_part, 'shard')]
    psum x2 -> x0, waiting for transfers between devices: 536 us -> none  [local(): sum_query = lax.psum(part_query, ('shard', 'tensor'))]
    all_gather x2 -> x0, blocking collectives: 104 us -> none  [the longest x1 53 us: local(): lax.all_gather(stepped_output, 'shard', axis=1, tiled=True)]
    all_to_all x0 -> x4, waiting for transfers between devices: none -> 37.7 us  [the longest x2 30.4 us: exchange(): lax.all_to_all(value, 'shard', 0, 0, axis_index_groups=group, tiled=True)]
    ppermute x0 -> x3, starting transfers between devices: none -> 23.1 us  [swap_cores(): return lax.ppermute(value, 'shard', [(s, s ^ 1) for s in range(shards)])]
  transfers between devices with their start and end apart: 2 -> 7, of which waited for: 2 -> 4; matrix products, arithmetic and copies ran while one was open for 0% -> 18% of each run, Pallas kernels for 0% -> 0%
where the time goes in v1:
time: 143 us
  starting transfers between devices  40 us (28%)
  waiting for transfers between devices  39.2 us (27%)
  other arithmetic  22.8 us (16%)
  blocking collectives  20.2 us (14%)
  local copies, waits for them, and re-layouts  10 us (7%)
  matrix products  9.04 us (6%)
    all_to_all x2, waiting for transfers between devices, exchange(): lax.all_to_all(value, 'shard', 0, 0, axis_index_groups=group, tiled=True)  30.4 us
    ppermute x3, starting transfers between devices, swap_cores(): return lax.ppermute(value, 'shard', [(s, s ^ 1) for s in range(shards)])  23.1 us
    all_to_all x1, blocking collectives, exchange(): lax.all_to_all(value, 'shard', 0, 0, axis_index_groups=group, tiled=True)  20.2 us
    all_to_all x2, starting transfers between devices, local(): lax.all_to_all(jnp.broadcast_to(sent[None], (tensors, *sent.shape)), 'ten...  8.67 us
    all_to_all x2, starting transfers between devices, exchange(): lax.all_to_all(value, 'shard', 0, 0, axis_index_groups=group, tiled=True)  8.22 us
    another operation x6, other arithmetic, inverse_lower(): lower = jnp.linalg.cholesky(gram)  7.9 us
    dot_general x14, matrix products, dot(): lax.dot_general(left, right, (dims, ((), ())), precision=highest, preferr...  7.88 us
    all_to_all x2, waiting for transfers between devices, local(): lax.all_to_all(jnp.broadcast_to(sent[None], (tensors, *sent.shape)), 'ten...  7.28 us
  transfers between devices with their start and end apart: 7, of which 4 were waited for; matrix products, arithmetic and copies ran while one was open for 18% of the time, Pallas kernels for 0%

profile of v1, /device:TPU:1, one launch (start us, length us, event | category | flops | bytes accessed | tf_op | source)
XLA Modules:
  0.0 142.6 jit_solution(5334632397028994844)
XLA Ops:
  0.7 1.3 copy.181
  2.5 0.4 copy-done.9
  3.5 0.5 copy-done.5
  4.1 8.8 %collective-permute-start = (f32[1104,128]{1,0:T(8,128)S(1)}, f32[1104,128]{1,0:T(8,128)S(1)}, u32[]{:S(2)}, u32[]{:S(2)}) collective-permute-start(f32[1104,128]{1,0:T(8,128)S(1)} %select_maximum_fusion), channel_id=1, source_target_pairs={{0,4},{4,0},{8,12},{12,8},{16,20},{20,16},{24,28},{28,24},{32,36},... | collective-permute-start | bytes 1695752 | tf_op jit(solution)/shard_map/ppermute | solution.py:30
  12.9 1.6 %collective-permute-done = f32[1104,128]{1,0:T(8,128)S(1)} collective-permute-done((f32[1104,128]{1,0:T(8,128)S(1)}, f32[1104,128]{1,0:T(8,128)S(1)}, u32[]{:S(2)}, u32[]{:S(2)}) %collective-permute-start) | collective-permute-done | bytes 565280 | tf_op jit(solution)/shard_map/ppermute | solution.py:30
  14.5 0.9 fusion
  15.4 4.7 %all-to-all-start = ((f32[8,136,128]{2,1,0:T(8,128)}), f32[8,136,128]{2,1,0:T(8,128)S(1)}, u32[]{:S(2)}, u32[]{:S(2)}) async-start(f32[8,136,128]{2,1,0:T(8,128)} %fusion), calls=%async_computation | async-start | bytes 1114112 | tf_op jit(solution)/shard_map/all_to_all | solution.py:34
  20.6 12.0 %all-to-all-done = f32[8,136,128]{2,1,0:T(8,128)S(1)} async-done(((f32[8,136,128]{2,1,0:T(8,128)}), f32[8,136,128]{2,1,0:T(8,128)S(1)}, u32[]{:S(2)}, u32[]{:S(2)}) %all-to-all-start) | async-done | bytes 557088 | tf_op jit(solution)/shard_map/all_to_all | solution.py:34
  33.0 20.2 %all_to_all.25 = f32[8,160,128]{2,1,0:T(8,128)S(1)} all-to-all(f32[8,160,128]{2,1,0:T(8,128)S(1)} %broadcast_in_dim.16), channel_id=1, replica_groups={{0,8,16,24,32,40,48,56},{64,72,80,88,96,104,112,120},{128,136,144,152,1..., dimensions={0} | all-to-all | bytes 1310720 | tf_op jit(solution)/shard_map/all_to_all | solution.py:34
  53.3 1.1 broadcast_in_dim.17
  54.4 3.6 %all-to-all-start.2 = ((f32[8,272,128]{2,1,0:T(8,128)}), f32[8,272,128]{2,1,0:T(8,128)S(1)}, u32[]{:S(2)}, u32[]{:S(2)}) async-start(f32[8,272,128]{2,1,0:T(8,128)} %broadcast_in_dim.17), calls=%async_computation.2 | async-start | bytes 2228224 | tf_op jit(solution)/shard_map/all_to_all | solution.py:34
  58.0 18.4 %all-to-all-done.2 = f32[8,272,128]{2,1,0:T(8,128)S(1)} async-done(((f32[8,272,128]{2,1,0:T(8,128)}), f32[8,272,128]{2,1,0:T(8,128)S(1)}, u32[]{:S(2)}, u32[]{:S(2)}) %all-to-all-start.2) | async-done | bytes 1114144 | tf_op jit(solution)/shard_map/all_to_all | solution.py:34
  76.4 0.9 fusion.27
  77.3 0.4 convolution_select_fusion.3
  77.7 0.6 fusion.36
  78.5 0.9 broadcast_in_dim.18
  79.4 4.1 %all-to-all-start.3 = ((f32[4,32,1152]{2,1,0:T(8,128)}), f32[4,32,1152]{2,1,0:T(8,128)}, u32[]{:S(2)}, u32[]{:S(2)}) async-start(f32[4,32,1152]{2,1,0:T(8,128)} %broadcast_in_dim.18), calls=%async_computation.3 | async-start | bytes 1179648 | tf_op jit(solution)/shard_map/all_to_all | solution.py:130
  83.6 1.3 bitcast_select_fusion
  84.9 6.4 %collective-permute-start.2 = (f32[1024,128]{1,0:T(8,128)S(1)}, f32[1024,128]{1,0:T(8,128)}, u32[]{:S(2)}, u32[]{:S(2)}) collective-permute-start(f32[1024,128]{1,0:T(8,128)S(1)} %bitcast.95), channel_id=1, source_target_pairs={{0,4},{4,0},{8,12},{12,8},{16,20},{20,16},{24,28},{28,24},{32,36},... | collective-permute-start | bytes 1572872 | tf_op jit(solution)/shard_map/ppermute | solution.py:30
  91.3 1.1 reduce_sum.38
  92.9 0.6 fusion.24
  93.5 3.6 %cholesky.44 = f32[32,32]{1,0:T(8,128)S(1)} custom-call(f32[32,32]{1,0:T(8,128)} %fusion.24), custom_call_target="Cholesky" | custom-call | tf_op jit(solution)/shard_map/jit(cholesky)/cholesky | solution.py:42
  97.1 0.6 compare_reduce_fusion.1
  97.8 0.7 fusion.17
  98.4 3.1 %custom-call.6 = f32[1,32,32]{1,2,0:T(8,128)} custom-call(f32[1,32,32]{2,1,0:T(8,128)S(1)} %fusion.17), custom_call_target="InvertDiagBlocksLowerTriangular" | custom-call | tf_op jit(solution)/shard_map/jit(_solve_triangular)/triangular_solve | solution.py:44
  101.5 0.9 fusion.15
  102.4 0.3 fusion.10
  102.7 0.4 fusion.38
  103.1 0.6 fusion.39
  103.9 0.9 broadcast_in_dim.19
  104.7 4.5 %all-to-all-start.4 = ((f32[4,32,1152]{2,1,0:T(8,128)}), f32[4,32,1152]{2,1,0:T(8,128)}, u32[]{:S(2)}, u32[]{:S(2)}) async-start(f32[4,32,1152]{2,1,0:T(8,128)} %broadcast_in_dim.19), calls=%async_computation.4 | async-start | bytes 1179648 | tf_op jit(solution)/shard_map/all_to_all | solution.py:130
  109.4 7.3 %all-to-all-done.4 = f32[4,32,1152]{2,1,0:T(8,128)} async-done(((f32[4,32,1152]{2,1,0:T(8,128)}), f32[4,32,1152]{2,1,0:T(8,128)}, u32[]{:S(2)}, u32[]{:S(2)}) %all-to-all-start.4) | async-done | bytes 589856 | tf_op jit(solution)/shard_map/all_to_all | solution.py:130
  116.6 1.1 reduce_sum.39
  118.2 2.9 %cholesky.55 = f32[32,32]{1,0:T(8,128)S(1)} custom-call(f32[32,32]{1,0:T(8,128)S(1)} %fusion.22), custom_call_target="Cholesky" | custom-call | tf_op jit(solution)/shard_map/jit(cholesky)/cholesky | solution.py:42
  121.1 0.6 compare_reduce_fusion
  121.8 0.7 fusion.18
  122.4 2.4 %custom-call.7 = f32[1,32,32]{1,2,0:T(8,128)S(1)} custom-call(f32[1,32,32]{2,1,0:T(8,128)S(1)} %fusion.18), custom_call_target="InvertDiagBlocksLowerTriangular" | custom-call | tf_op jit(solution)/shard_map/jit(_solve_triangular)/triangular_solve | solution.py:44
  125.1 0.3 fusion.7
  125.4 0.4 fusion.41
  125.9 7.9 %collective-permute-start.1 = (f32[32,1152]{1,0:T(8,128)S(1)}, f32[32,1152]{1,0:T(8,128)S(1)}, u32[]{:S(2)}, u32[]{:S(2)}) collective-permute-start(f32[32,1152]{1,0:T(8,128)S(1)} %pad_maximum_fusion.2), channel_id=1, source_target_pairs={{0,4},{4,0},{8,12},{12,8},{16,20},{20,16},{24,28},{28,24},{32,36},... | collective-permute-start | bytes 442376 | tf_op jit(solution)/shard_map/ppermute | solution.py:30
  133.9 0.6 dynamic-slice_add_fusion.2
  134.6 0.6 sub.31
  135.3 1.0 bitcast_subtract_fusion
  136.3 1.0 copy.201
  137.3 1.0 copy.202
  138.3 0.6 dynamic-slice_add_fusion
  138.9 3.0 %multiply_subtract_fusion = (f32[1024,128]{1,0:T(8,128)}, f32[1,1024,128]{2,1,0:T(8,128)}, f32[1024,128]{1,0:T(8,128)S(1)}) fusion(f32[1024,128]{1,0:T(8,128)} %collective-permute-done.2, pred[]{:T(512)S(6)} %eq.11, f32[8,8,16,128]{3,2,1,0:T(8,128)S(1)} %bitcast_select_fusion, f32[1,1024,128]{2,1,0:T(8,128)S(1)} %convert_add_fusion.1, ...), kind=kOutput, calls=%fused_computation.18 | convolution fusion | flops 50987008 | bytes 3293185 | tf_op jit(solution)/shard_map/dot_general | solution.py:14
  142.0 0.6 dynamic-slice_add_fusion.1
  (96 shorter events, 4.1 us)
Async XLA Ops:
  0.6 76.7 %copy-start = (f32[1024,32]{0,1:T(8,128)S(1)}, f32[1024,32]{0,1:T(8,128)}, u32[]{:S(2)}) copy-start(f32[1024,32]{0,1:T(8,128)} %param.21) | copy-start | bytes 393220
  0.6 1.3 copy-start.3
  2.1 0.7 copy-start.9
  2.2 0.9 copy-start.12
  2.2 0.9 copy-start.14
  2.2 1.1 copy-start.1
  2.2 1.1 copy-start.2
  3.4 0.7 copy-start.5
  3.4 0.7 copy-start.7
  3.4 0.7 copy-start.10
  3.4 0.7 copy-start.11
  4.1 10.4 %collective-permute-start = (f32[1104,128]{1,0:T(8,128)S(1)}, f32[1104,128]{1,0:T(8,128)S(1)}, u32[]{:S(2)}, u32[]{:S(2)}) collective-permute-start(f32[1104,128]{1,0:T(8,128)S(1)} %select_maximum_fusion), channel_id=1, source_target_pairs={{0,4},{4,0},{8,12},{12,8},{16,20},{20,16},{24,28},{28,24},{32,36},... | collective-permute-start | bytes 1695752 | tf_op jit(solution)/shard_map/ppermute | solution.py:30
  15.4 17.2 %all-to-all-start = ((f32[8,136,128]{2,1,0:T(8,128)}), f32[8,136,128]{2,1,0:T(8,128)S(1)}, u32[]{:S(2)}, u32[]{:S(2)}) async-start(f32[8,136,128]{2,1,0:T(8,128)} %fusion), calls=%async_computation | async-start | bytes 1114112 | tf_op jit(solution)/shard_map/all_to_all | solution.py:34
  54.4 22.0 %all-to-all-start.2 = ((f32[8,272,128]{2,1,0:T(8,128)}), f32[8,272,128]{2,1,0:T(8,128)S(1)}, u32[]{:S(2)}, u32[]{:S(2)}) async-start(f32[8,272,128]{2,1,0:T(8,128)} %broadcast_in_dim.17), calls=%async_computation.2 | async-start | bytes 2228224 | tf_op jit(solution)/shard_map/all_to_all | solution.py:34
  58.0 19.3 %copy-start.4 = (f32[128,32]{0,1:T(8,128)S(1)}, f32[128,32]{0,1:T(8,128)}, u32[]{:S(2)}) copy-start(f32[128,32]{0,1:T(8,128)} %param.20) | copy-start | bytes 49156
  79.4 11.9 %all-to-all-start.3 = ((f32[4,32,1152]{2,1,0:T(8,128)}), f32[4,32,1152]{2,1,0:T(8,128)}, u32[]{:S(2)}, u32[]{:S(2)}) async-start(f32[4,32,1152]{2,1,0:T(8,128)} %broadcast_in_dim.18), calls=%async_computation.3 | async-start | bytes 1179648 | tf_op jit(solution)/shard_map/all_to_all | solution.py:130
  84.9 50.4 %collective-permute-start.2 = (f32[1024,128]{1,0:T(8,128)S(1)}, f32[1024,128]{1,0:T(8,128)}, u32[]{:S(2)}, u32[]{:S(2)}) collective-permute-start(f32[1024,128]{1,0:T(8,128)S(1)} %bitcast.95), channel_id=1, source_target_pairs={{0,4},{4,0},{8,12},{12,8},{16,20},{20,16},{24,28},{28,24},{32,36},... | collective-permute-start | bytes 1572872 | tf_op jit(solution)/shard_map/ppermute | solution.py:30
  104.7 11.9 %all-to-all-start.4 = ((f32[4,32,1152]{2,1,0:T(8,128)}), f32[4,32,1152]{2,1,0:T(8,128)}, u32[]{:S(2)}, u32[]{:S(2)}) async-start(f32[4,32,1152]{2,1,0:T(8,128)} %broadcast_in_dim.19), calls=%async_computation.4 | async-start | bytes 1179648 | tf_op jit(solution)/shard_map/all_to_all | solution.py:130
  109.4 24.5 %copy-start.13 = (f32[28]{0:T(128)S(1)}, f32[28]{0:T(128)}, u32[]{:S(2)}) copy-start(f32[28]{0:T(128)} %param.27) | copy-start | bytes 340
  125.9 9.3 %collective-permute-start.1 = (f32[32,1152]{1,0:T(8,128)S(1)}, f32[32,1152]{1,0:T(8,128)S(1)}, u32[]{:S(2)}, u32[]{:S(2)}) collective-permute-start(f32[32,1152]{1,0:T(8,128)S(1)} %pad_maximum_fusion.2), channel_id=1, source_target_pairs={{0,4},{4,0},{8,12},{12,8},{16,20},{20,16},{24,28},{28,24},{32,36},... | collective-permute-start | bytes 442376 | tf_op jit(solution)/shard_map/ppermute | solution.py:30
  136.3 2.0 %copy-start.6 = (f32[128,8]{0,1:T(8,128)S(1)}, f32[128,8]{0,1:T(8,128)}, u32[]{:S(2)}) copy-start(f32[128,8]{0,1:T(8,128)} %param.25) | copy-start | bytes 12292
  138.9 3.0 %copy-start.8 = (f32[8,128]{1,0:T(8,128)S(1)}, f32[8,128]{1,0:T(8,128)}, u32[]{:S(2)}) copy-start(f32[8,128]{1,0:T(8,128)} %param.24) | copy-start | bytes 12292

commit v2 on v1

--- a/solution.py
+++ b/solution.py
@@ -1,7 +1,10 @@
+import functools
+
 import jax
 import jax.numpy as jnp
-import numpy as np
 from jax import lax
+from jax.experimental import pallas as pl
+from jax.experimental.pallas import tpu as pltpu
 from jax.sharding import PartitionSpec as P
 
 ROUNDS = 2
@@ -38,10 +41,163 @@
     return exchange(jnp.broadcast_to(value[None], (size, *value.shape)), group)
 
 
-def inverse_lower(gram):
-    lower = jnp.linalg.cholesky(gram)
-    eye = jnp.eye(gram.shape[0], dtype=gram.dtype)
-    return jax.scipy.linalg.solve_triangular(lower, eye, lower=True)
+def invert_lower(gram):
+    rank = gram.shape[0]
+    tiles = rank // 8
+    half = LANES // 2
+    lane = lax.broadcasted_iota(jnp.int32, (8, LANES), 1)
+    sub = lax.broadcasted_iota(jnp.int32, (8, LANES), 0)
+    rows = [
+        jnp.where(lane < rank, gram[8 * t:8 * t + 8], jnp.where(lane == sub + (8 * t + half), 1.0, 0.0))
+        for t in range(tiles)
+    ]
+    done = [jnp.zeros((8, LANES), jnp.float32) for _ in range(tiles)]
+    for k in range(rank):
+        at, place = k // 8, k % 8
+        row = jnp.broadcast_to(rows[at][place:place + 1], (8, LANES))
+        columns = [jnp.broadcast_to(rows[t][:, k:k + 1], (8, LANES)) for t in range(at, tiles)]
+        pivot = jnp.broadcast_to(columns[0][place:place + 1], (8, LANES))
+        scaled = row / pivot
+        done[at] = jnp.where(sub == place, row * lax.rsqrt(pivot), done[at])
+        for t in range(at, tiles):
+            take = columns[t - at] * scaled
+            rows[t] = rows[t] - (jnp.where(sub > place, take, 0.0) if t == at else take)
+    return pltpu.roll(jnp.concatenate(done), half, 1)
+
+
+def send_partials(narrow, recv, gram, sent, block):
+    ring = recv.shape[0]
+    rank = narrow.shape[0]
+    gram[...] = jnp.zeros_like(gram)
+    gram[:, :rank] = dot(narrow, narrow, ((1,), (1,)))
+    own = gram[...]
+    for copy in range(sent.shape[0]):
+        sent[copy, :, ring * block:] = own
+    for j in range(ring):
+        part = dot(narrow, recv[j, :block], ((1,), (1,)))
+        for copy in range(sent.shape[0]):
+            sent[copy, :, j * block:(j + 1) * block] = part
+
+
+def normalized(spot, got, gram, block, ring):
+    rank = got.shape[1]
+    total = got[0]
+    for copy in range(1, got.shape[0]):
+        total = total + got[copy]
+    wide = total[:, :ring * block]
+    gram[...] = total[:, ring * block:]
+
+    @pl.when(spot[1] == 0)
+    def _():
+        gram[:, :rank] = dot(wide, wide, ((1,), (1,)))
+
+    inverse = invert_lower(gram[...])[:, :rank]
+    return inverse, dot(inverse, wide, ((1,), (0,)))
+
+
+def times_matrix(wide, recv, block):
+    return sum(dot(wide[:, j * block:(j + 1) * block], recv[j, :block], ((1,), (0,))) for j in range(recv.shape[0]))
+
+
+def first_kernel(block, spot, recv, start_query, start_output, sent, narrow, gram):
+    @pl.when(spot[1] == 0)
+    def _():
+        narrow[...] = start_query[...]
+
+    @pl.when(spot[1] == 1)
+    def _():
+        narrow[...] = times_matrix(start_output[...], recv, block)
+
+    send_partials(narrow[...], recv, gram, sent, block)
+
+
+def middle_kernel(block, spot, recv, got, sent, narrow, gram):
+    _, wide = normalized(spot, got, gram, block, recv.shape[0])
+    value = times_matrix(wide, recv, block)
+    narrow[...] = value
+    send_partials(value, recv, gram, sent, block)
+
+
+def last_kernel(block, spot, recv, got, narrow, factors, gram):
+    ring = recv.shape[0]
+    inverse, wide = normalized(spot, got, gram, block, ring)
+    factors[:, :ring * block] = wide
+
+    @pl.when(spot[1] == 0)
+    def _():
+        factors[:, ring * block:] = times_matrix(wide, recv, block)
+
+    @pl.when(spot[1] == 1)
+    def _():
+        factors[:, ring * block:] = dot(inverse, narrow[...], ((1,), (0,)))
+
+
+def final_kernel(
+    block, shards, spot, mine, other, kept_mine, kept_other, grad_query, error_query, grad_output, error_output,
+    moment_query, moment_output, new_error_query, new_error_output, new_moment_query, new_moment_output,
+    new_weight_query, new_weight_output, error_q, error_o, weight_q, weight_o, sems,
+):
+    height, width = error_query.shape
+    rows = moment_query.shape[0]
+    scale = 1.0 / shards
+    ring = height // block
+    index = spot[0]
+
+    def copies(j):
+        down = pl.ds(j * block, block)
+        return (
+            pltpu.make_async_copy(error_q.at[down], new_error_query.at[down], sems.at[0, j]),
+            pltpu.make_async_copy(weight_q.at[down], new_weight_query.at[down], sems.at[1, j]),
+            pltpu.make_async_copy(error_o.at[:, down], new_error_output.at[:, down], sems.at[2, j]),
+            pltpu.make_async_copy(weight_o.at[:, down], new_weight_output.at[:, down], sems.at[3, j]),
+        )
+
+    def body(query, output, kept_query, kept_output):
+        right = query[:, height:] * scale
+        left = output[:, height:] * scale
+        for j in range(ring):
+            down = slice(j * block, (j + 1) * block)
+            approx = dot(query[:, down], right, ((0,), (0,)))
+            error_q[down] = grad_query[down].astype(jnp.float32) + error_query[down] - approx
+            weight_q[down] = kept_query[down] - 0.01 * approx
+            approx = dot(left, output[:, down], ((0,), (0,)))
+            error_o[:, down] = grad_output[:, down].astype(jnp.float32) + error_output[:, down] - approx
+            weight_o[:, down] = kept_output[down] - 0.01 * approx
+            for copy in copies(j):
+                copy.start()
+        along = index * rows
+        base = pl.multiple_of(along // LANES * LANES, LANES)
+        picked = pltpu.roll(query[:, pl.ds(base, LANES)], (LANES - along % LANES) % LANES, 1)
+        new_moment_query[...] = 0.9 * moment_query[...] + dot(picked, right, ((0,), (0,)))[:rows]
+        picked = pltpu.roll(output[:, pl.ds(base, LANES)], (LANES - along % LANES) % LANES, 1)
+        new_moment_output[...] = 0.9 * moment_output[...] + dot(picked, left, ((0,), (0,)))[:rows]
+
+    @pl.when(spot[1] == 0)
+    def _():
+        body(mine, other, kept_mine, kept_other)
+
+    @pl.when(spot[1] == 1)
+    def _():
+        body(other, mine, kept_other, kept_mine)
+
+    for j in range(ring):
+        for copy in copies(j):
+            copy.wait()
+
+
+def shape(*dims):
+    return jax.ShapeDtypeStruct(dims, jnp.float32)
+
+
+def run(kernel, given, out_shape, scratch, out_specs=None, **options):
+    whole = pl.BlockSpec(memory_space=pltpu.VMEM)
+    specs = [pl.BlockSpec(memory_space=pltpu.SMEM)] + [whole] * (len(given) - 1)
+    if out_specs is None:
+        out_specs = jax.tree.map(lambda _: whole, out_shape)
+    return pl.pallas_call(
+        kernel, out_shape=out_shape, in_specs=specs, out_specs=out_specs, scratch_shapes=scratch,
+        compiler_params=pltpu.CompilerParams(vmem_limit_bytes=40 * 2**20), **options,
+    )(*given)
 
 
 def local(
@@ -114,43 +270,50 @@
     kept_rows = every[:, block + vec_rows:block + vec_rows + 2 * rows].reshape(block, LANES)
     kept_vectors = every[:, block + vec_rows + 2 * rows]
     every = share(jnp.concatenate([square, whole[block:], kept_rows, kept_vectors]), first, ring)
-    matrix = every[:, :block].reshape(height, width)
     vector_sum = every[:, block:block + vec_rows].reshape(ring, -1)[:, :piece].reshape(vec)
     kept_all = every[:, block + vec_rows:2 * block + vec_rows].reshape(ring, ring, 2 * rows, LANES)
-    kept_all = jnp.where(even, kept_all, kept_all.transpose(1, 0, 2, 3)).reshape(height, LANES)
+    kept_turned = kept_all.transpose(1, 0, 2, 3).reshape(ring, block, LANES).transpose(0, 2, 1)
+    kept_all = jnp.where(even, kept_all.reshape(ring, block, LANES), kept_turned).reshape(height, LANES)
     kept_vectors = every[:, 2 * block + vec_rows:][:, :, :2 * small]
     kept_vectors = jnp.where(even, kept_vectors, kept_vectors.transpose(1, 0, 2)).reshape(vec)
     kept_other = swap_cores(kept_all, shards)
 
-    narrow = jnp.where(even, start_query.T, dot(start_output, matrix, ((0,), (0,))))
-    for turn in range(ROUNDS):
-        wide = dot(narrow, matrix, ((1,), (1,)))
-        gram = jnp.pad(dot(narrow, narrow, ((1,), (1,))), ((0, 0), (0, LANES - rank)))
-        sent = jnp.concatenate([wide, gram], axis=1)
-        got = lax.all_to_all(jnp.broadcast_to(sent[None], (tensors, *sent.shape)), "tensor", 0, 0, tiled=True).sum(0)
-        wide = got[:, :height]
-        gram = jnp.where(even, dot(wide, wide, ((1,), (1,))), got[:, height:height + rank])
-        inverse = inverse_lower(gram)
-        wide = dot(inverse, wide, ((1,), (0,)))
-        scaled = dot(inverse, narrow, ((1,), (0,)))
-        narrow = dot(wide, matrix, ((1,), (0,)))
-    mine = jnp.concatenate([wide, jnp.where(even, narrow, scaled)], axis=1)
+    spot = jnp.stack([index, index % 2]).astype(jnp.int32)
+    gram = pltpu.VMEM((rank, LANES), jnp.float32)
+    partials = shape(tensors, rank, height + LANES)
+
+    def gathered(value):
+        return lax.all_to_all(value, "tensor", 0, 0, tiled=True)
+
+    sent, narrow = run(
+        functools.partial(first_kernel, block), (spot, every, start_query.T, start_output.T),
+        (partials, shape(rank, width)), [gram],
+    )
+    for turn in range(ROUNDS - 1):
+        sent, narrow = run(
+            functools.partial(middle_kernel, block), (spot, every, gathered(sent)), (partials, shape(rank, width)), [gram]
+        )
+    mine = run(
+        functools.partial(last_kernel, block), (spot, every, gathered(sent), narrow), shape(rank, height + width), [gram]
+    )
     other = swap_cores(mine, shards)
-    of_query = jnp.where(even, mine, other)
-    of_output = jnp.where(even, other, mine)
-    approx_query = dot(of_query[:, :height], of_query[:, height:], ((0,), (0,))) / shards
-    approx_output = dot(of_output[:, height:], of_output[:, :height], ((0,), (0,))) / shards
-    kept_query = jnp.where(even, kept_all, kept_other)
-    kept_output = jnp.where(even, kept_other, kept_all).T
-
-    new_error_query = (total_query - approx_query)[None]
-    new_error_output = (total_output - approx_output)[None]
-    block_query = lax.dynamic_slice_in_dim(approx_query, index * rows, rows, 0)
-    block_output = lax.dynamic_slice_in_dim(approx_output, index * rows, rows, 1)
-    new_moment_query = 0.9 * moment_query + block_query
-    new_moment_output = 0.9 * moment_output + block_output
-    new_weight_query = kept_query - 0.01 * approx_query
-    new_weight_output = kept_output - 0.01 * approx_output
+    big = [pltpu.VMEM((height, width), jnp.float32), pltpu.VMEM((width, height), jnp.float32)]
+    outside, within = pl.BlockSpec(memory_space=pl.ANY), pl.BlockSpec(memory_space=pltpu.VMEM)
+    (
+        new_error_query, new_error_output, new_moment_query, new_moment_output, new_weight_query, new_weight_output,
+    ) = run(
+        functools.partial(final_kernel, block, shards),
+        (
+            spot, mine, other, kept_all, kept_other, grad_query[0], error_query[0], grad_output[0], error_output[0],
+            moment_query, moment_output.T,
+        ),
+        (shape(height, width), shape(width, height), shape(rows, width), shape(rows, width), shape(height, width), shape(width, height)),
+        [big[0], big[1], big[0], big[1], pltpu.SemaphoreType.DMA((4, ring))],
+        (outside, outside, within, within, outside, outside),
+    )
+    new_error_query = new_error_query[None]
+    new_error_output = new_error_output[None]
+    new_moment_output = new_moment_output.T
     vector_mean = vector_sum / shards
     new_moment_vector = 0.9 * moment_vector + lax.dynamic_slice_in_dim(vector_mean, index * small, small, 0)
     new_weight_vector = kept_vectors - 0.01 * vector_mean

time: 143 us -> 133 us (0.930)
  Pallas kernels: 0 us -> 17.7 us
  other arithmetic: 22.8 us -> 6.78 us
  matrix products: 9.04 us -> 0 us
  waiting for transfers between devices: 39.2 us -> 32.8 us
  local copies, waits for them, and re-layouts: 10 us -> 14.3 us
    pallas_call x0 -> x4, Pallas kernels: none -> 17.7 us  [run(): pl.pallas_call(kernel, out_shape=out_shape, in_specs=specs, out_specs=out...]
    another operation x10 -> x1, other arithmetic: 14.7 us -> 0.08 us  [local(): spot = jnp.stack([index, index % 2]).astype(jnp.int32)]
    dot_general x14 -> x0, matrix products: 7.88 us -> none  [dot(): lax.dot_general(left, right, (dims, ((), ())), precision=highest, preferr...]
    all_to_all x2, waiting for transfers between devices: 7.28 us -> 0.53 us  [gathered(): return lax.all_to_all(value, 'tensor', 0, 0, tiled=True)]
    unnamed x40 -> x39, local copies, waits for them, and re-layouts: 4.96 us -> 8.23 us
    reduce_sum x2 -> x0, other arithmetic: 2.22 us -> none  [local(): lax.all_to_all(jnp.broadcast_to(sent[None], (tensors, *sent.shape)), 'ten...]
    broadcast_in_dim x2 -> x0, local copies, waits for them, and re-layouts: 1.72 us -> none  [local(): jnp.broadcast_to(sent[None], (tensors, *sent.shape))]
  transfers between devices with their start and end apart: 7 -> 7, of which waited for: 4 -> 4; matrix products, arithmetic and copies ran while one was open for 18% -> 7% of each run, Pallas kernels for 0% -> 9%
where the time goes in v2:
time: 133 us; the launch traced here: 132 us
  starting transfers between devices  39.4 us (30%)
  waiting for transfers between devices  32.8 us (25%)
  blocking collectives  20.2 us (15%)
  Pallas kernels  17.7 us (13%)
  local copies, waits for them, and re-layouts  14.3 us (11%)
  other arithmetic  6.78 us (5%)
    all_to_all x2, waiting for transfers between devices, exchange(): lax.all_to_all(value, 'shard', 0, 0, axis_index_groups=group, tiled=True)  30.7 us
    ppermute x3, starting transfers between devices, swap_cores(): return lax.ppermute(value, 'shard', [(s, s ^ 1) for s in range(shards)])  23.2 us
    all_to_all x1, blocking collectives, exchange(): lax.all_to_all(value, 'shard', 0, 0, axis_index_groups=group, tiled=True)  20.2 us
    pallas_call x4, Pallas kernels, run(): pl.pallas_call(kernel, out_shape=out_shape, in_specs=specs, out_specs=out...  17.7 us
    unnamed x39, local copies, waits for them, and re-layouts  8.23 us
    all_to_all x2, starting transfers between devices, exchange(): lax.all_to_all(value, 'shard', 0, 0, axis_index_groups=group, tiled=True)  8.22 us
    all_to_all x2, starting transfers between devices, gathered(): return lax.all_to_all(value, 'tensor', 0, 0, tiled=True)  8.01 us
  transfers between devices with their start and end apart: 7, of which 4 were waited for; matrix products, arithmetic and copies ran while one was open for 7% of the time, Pallas kernels for 9%

profile of v2, /device:TPU:1, one launch (start us, length us, event | category | flops | bytes accessed | tf_op | source)
XLA Modules:
  0.0 132.2 jit_solution(6174290759985935254)
XLA Ops:
  0.6 0.7 multiply_subtract_fusion.2
  1.3 0.8 reduce
  2.1 0.1 convert_element_type.25
  2.2 1.1 copy.32
  3.3 1.2 copy.33
  4.6 0.2 copy.34
  4.9 0.8 copy-done
  5.6 0.1 copy-done.2
  5.8 0.1 bitcast_select_fusion.2
  5.9 0.5 copy-done.8
  6.4 0.0 copy-done.10
  6.4 0.0 copy-done.14
  6.5 8.8 %collective-permute-start = (f32[1104,128]{1,0:T(8,128)S(1)}, f32[1104,128]{1,0:T(8,128)S(1)}, u32[]{:S(2)}, u32[]{:S(2)}) collective-permute-start(f32[1104,128]{1,0:T(8,128)S(1)} %select_maximum_fusion), channel_id=1, source_target_pairs={{0,4},{4,0},{8,12},{12,8},{16,20},{20,16},{24,28},{28,24},{32,36},... | collective-permute-start | bytes 1695752 | tf_op jit(solution)/shard_map/ppermute | solution.py:33
  15.3 1.6 %collective-permute-done = f32[1104,128]{1,0:T(8,128)S(1)} collective-permute-done((f32[1104,128]{1,0:T(8,128)S(1)}, f32[1104,128]{1,0:T(8,128)S(1)}, u32[]{:S(2)}, u32[]{:S(2)}) %collective-permute-start) | collective-permute-done | bytes 565280 | tf_op jit(solution)/shard_map/ppermute | solution.py:33
  16.9 0.9 fusion
  17.8 4.7 %all-to-all-start = ((f32[8,136,128]{2,1,0:T(8,128)}), f32[8,136,128]{2,1,0:T(8,128)S(1)}, u32[]{:S(2)}, u32[]{:S(2)}) async-start(f32[8,136,128]{2,1,0:T(8,128)} %fusion), calls=%async_computation | async-start | bytes 1114112 | tf_op jit(solution)/shard_map/all_to_all | solution.py:37
  22.5 0.1 broadcast_select_fusion
  22.6 12.4 %all-to-all-done = f32[8,136,128]{2,1,0:T(8,128)S(1)} async-done(((f32[8,136,128]{2,1,0:T(8,128)}), f32[8,136,128]{2,1,0:T(8,128)S(1)}, u32[]{:S(2)}, u32[]{:S(2)}) %all-to-all-start) | async-done | bytes 557088 | tf_op jit(solution)/shard_map/all_to_all | solution.py:37
  35.1 20.2 %all_to_all.25 = f32[8,160,128]{2,1,0:T(8,128)S(1)} all-to-all(f32[8,160,128]{2,1,0:T(8,128)S(1)} %broadcast_in_dim.11), channel_id=1, replica_groups={{0,8,16,24,32,40,48,56},{64,72,80,88,96,104,112,120},{128,136,144,152,1..., dimensions={0} | all-to-all | bytes 1310720 | tf_op jit(solution)/shard_map/all_to_all | solution.py:37
  55.3 0.1 copy.35
  55.5 1.1 broadcast_in_dim.24
  56.5 3.6 %all-to-all-start.2 = ((f32[8,272,128]{2,1,0:T(8,128)}), f32[8,272,128]{2,1,0:T(8,128)S(1)}, u32[]{:S(2)}, u32[]{:S(2)}) async-start(f32[8,272,128]{2,1,0:T(8,128)} %broadcast_in_dim.24), calls=%async_computation.2 | async-start | bytes 2228224 | tf_op jit(solution)/shard_map/all_to_all | solution.py:37
  60.1 0.1 pad_add_fusion.spot
  60.2 18.3 %all-to-all-done.2.recv = f32[8,272,128]{2,1,0:T(8,128)S(1)} async-done(((f32[8,272,128]{2,1,0:T(8,128)}), f32[8,272,128]{2,1,0:T(8,128)S(1)}, u32[]{:S(2)}, u32[]{:S(2)}) %all-to-all-start.2) | async-done | bytes 1114144 | tf_op jit(solution)/shard_map/all_to_all | solution.py:37
  78.6 0.2 copy.38
  78.9 0.6 copy-done.6
  79.5 2.0 %shard_map.188 = (f32[4,32,1152]{2,1,0:T(8,128)S(1)}, f32[32,128]{1,0:T(8,128)}) custom-call(s32[2]{0:T(128)S(1)} %pad_add_fusion.spot, f32[8,272,128]{2,1,0:T(8,128)S(1)} %all-to-all-done.2.recv, f32[32,128]{1,0:T(8,128)S(1)} %bitcast.57, f32[32,1024]{1,0:T(8,128)S(1)} %bitcast.56), custom_call_target="tpu_custom_call" | custom-call | tf_op jit(solution)/shard_map/pallas_call | solution.py:197
  81.5 0.8 copy-done.5
  82.4 4.0 %all-to-all-start.3 = ((f32[4,32,1152]{2,1,0:T(8,128)}), f32[4,32,1152]{2,1,0:T(8,128)S(1)}, u32[]{:S(2)}, u32[]{:S(2)}) async-start(f32[4,32,1152]{2,1,0:T(8,128)} %copy-done.5), calls=%async_computation.3 | async-start | bytes 1179648 | tf_op jit(solution)/shard_map/all_to_all | solution.py:286
  86.4 0.1 bitcast_select_fusion
  86.5 6.0 %collective-permute-start.2 = (f32[1024,128]{1,0:T(8,128)S(1)}, f32[1024,128]{1,0:T(8,128)}, u32[]{:S(2)}, u32[]{:S(2)}) collective-permute-start(f32[1024,128]{1,0:T(8,128)S(1)} %bitcast.52), channel_id=1, source_target_pairs={{0,4},{4,0},{8,12},{12,8},{16,20},{20,16},{24,28},{28,24},{32,36},... | collective-permute-start | bytes 1572872 | tf_op jit(solution)/shard_map/ppermute | solution.py:33
  92.5 0.6 bitcast_select_fusion.4
  93.2 0.5 all-to-all-done.3.got
  93.7 7.0 %shard_map.189 = (f32[4,32,1152]{2,1,0:T(8,128)S(1)}, f32[32,128]{1,0:T(8,128)S(1)}) custom-call(s32[2]{0:T(128)S(1)} %pad_add_fusion.spot, f32[8,272,128]{2,1,0:T(8,128)S(1)} %all-to-all-done.2.recv, f32[4,32,1152]{2,1,0:T(8,128)S(1)} %all-to-all-done.3.got), custom_call_target="tpu_custom_call" | custom-call | tf_op jit(solution)/shard_map/pallas_call | solution.py:197
  100.7 0.9 copy-done.4
  101.5 4.0 %all-to-all-start.4 = ((f32[4,32,1152]{2,1,0:T(8,128)}), f32[4,32,1152]{2,1,0:T(8,128)S(1)}, u32[]{:S(2)}, u32[]{:S(2)}) async-start(f32[4,32,1152]{2,1,0:T(8,128)} %copy-done.4), calls=%async_computation.4 | async-start | bytes 1179648 | tf_op jit(solution)/shard_map/all_to_all | solution.py:286
  105.5 0.6 slice_bitcast_fusion
  106.1 1.4 %reshape.127 = f32[3584]{0:T(1024)} reshape(f32[8,8,56]{2,1,0:T(8,128)} %bitcast_select_fusion.4) | data formatting | bytes 28672 | tf_op jit(solution)/shard_map/reshape | solution.py:278
  107.6 0.8 copy.46
  108.4 0.6 slice_multiply_fusion
  109.0 1.4 %mul.39 = f32[3584]{0:T(1024)} reshape(f32[8,448]{1,0:T(8,128)} %get-tuple-element.28) | data formatting | bytes 28672 | tf_op jit(solution)/shard_map/mul | solution.py:319
  110.4 1.4 %div.10 = f32[3584]{0:T(1024)} reshape(f32[8,448]{1,0:T(8,128)} %get-tuple-element.29) | data formatting | bytes 28672 | tf_op jit(solution)/shard_map/div | solution.py:317
  111.8 1.3 %sub.15 = f32[3584]{0:T(1024)} subtract(f32[3584]{0:T(1024)} %reshape.127, f32[3584]{0:T(1024)} %mul.39) | non-fusion elementwise | flops 3584 | bytes 43008 | tf_op jit(solution)/shard_map/sub | solution.py:319
  113.1 0.7 copy-done.13
  113.8 4.9 %shard_map.190.mine = f32[32,1152]{1,0:T(8,128)S(1)} custom-call(s32[2]{0:T(128)S(1)} %copy-done.13, f32[8,272,128]{2,1,0:T(8,128)S(1)} %all-to-all-done.2.recv, f32[4,32,1152]{2,1,0:T(8,128)S(1)} %all-to-all-done.4.got, f32[32,128]{1,0:T(8,128)S(1)} %get-tuple-element.19.narrow), custom_call_target="tpu_custom_call" | custom-call | tf_op jit(solution)/shard_map/pallas_call | solution.py:197
  118.8 8.4 %collective-permute-start.1 = (f32[32,1152]{1,0:T(8,128)S(1)}, f32[32,1152]{1,0:T(8,128)S(1)}, u32[]{:S(2)}, u32[]{:S(2)}) collective-permute-start(f32[32,1152]{1,0:T(8,128)S(1)} %shard_map.190.mine), channel_id=1, source_target_pairs={{0,4},{4,0},{8,12},{12,8},{16,20},{20,16},{24,28},{28,24},{32,36},... | collective-permute-start | bytes 442376 | tf_op jit(solution)/shard_map/ppermute | solution.py:33
  127.1 1.3 dynamic-slice_add_fusion
  128.5 3.7 %shard_map.191 = (f32[1024,128]{1,0:T(8,128)}, f32[128,1024]{1,0:T(8,128)}, f32[8,128]{1,0:T(8,128)}, f32[8,128]{1,0:T(8,128)}, f32[1024,128]{1,0:T(8,128)}, /*index=5*/f32[128,1024]{1,0:T(8,128)}) custom-call(s32[2]{0:T(128)S(1)} %copy-done.13, f32[32,1152]{1,0:T(8,128)S(1)} %shard_map.190.mine, f32[32,1152]{1,0:T(8,128)S(1)} %collective-permute-done.1.other, ...), custom_call_target="tpu_custom_call" | custom-call | tf_op jit(solution)/shard_map/pallas_call | solution.py:197
  (53 shorter events, 0.6 us)
Async XLA Ops:
  4.6 1.0 copy-start
  4.6 1.1 copy-start.2
  5.7 0.7 copy-start.8
  5.7 0.7 copy-start.10
  5.8 0.7 copy-start.14
  5.8 0.7 copy-start.15
  6.5 10.4 %collective-permute-start = (f32[1104,128]{1,0:T(8,128)S(1)}, f32[1104,128]{1,0:T(8,128)S(1)}, u32[]{:S(2)}, u32[]{:S(2)}) collective-permute-start(f32[1104,128]{1,0:T(8,128)S(1)} %select_maximum_fusion), channel_id=1, source_target_pairs={{0,4},{4,0},{8,12},{12,8},{16,20},{20,16},{24,28},{28,24},{32,36},... | collective-permute-start | bytes 1695752 | tf_op jit(solution)/shard_map/ppermute | solution.py:33
  17.8 17.2 %all-to-all-start = ((f32[8,136,128]{2,1,0:T(8,128)}), f32[8,136,128]{2,1,0:T(8,128)S(1)}, u32[]{:S(2)}, u32[]{:S(2)}) async-start(f32[8,136,128]{2,1,0:T(8,128)} %fusion), calls=%async_computation | async-start | bytes 1114112 | tf_op jit(solution)/shard_map/all_to_all | solution.py:37
  56.5 22.0 %all-to-all-start.2 = ((f32[8,272,128]{2,1,0:T(8,128)}), f32[8,272,128]{2,1,0:T(8,128)S(1)}, u32[]{:S(2)}, u32[]{:S(2)}) async-start(f32[8,272,128]{2,1,0:T(8,128)} %broadcast_in_dim.24), calls=%async_computation.2 | async-start | bytes 2228224 | tf_op jit(solution)/shard_map/all_to_all | solution.py:37
  60.2 33.5 %copy-start.12 = (s32[2]{0:T(128)}, s32[2]{0:T(128)S(1)}, u32[]{:S(2)}) copy-start(s32[2]{0:T(128)S(1)} %pad_add_fusion.spot) | copy-start | bytes 28
  78.6 0.9 copy-start.6
  78.6 0.9 copy-start.7
  81.5 0.8 copy-start.5
  82.4 11.3 %all-to-all-start.3 = ((f32[4,32,1152]{2,1,0:T(8,128)}), f32[4,32,1152]{2,1,0:T(8,128)S(1)}, u32[]{:S(2)}, u32[]{:S(2)}) async-start(f32[4,32,1152]{2,1,0:T(8,128)} %copy-done.5), calls=%async_computation.3 | async-start | bytes 1179648 | tf_op jit(solution)/shard_map/all_to_all | solution.py:286
  86.5 42.0 %collective-permute-start.2 = (f32[1024,128]{1,0:T(8,128)S(1)}, f32[1024,128]{1,0:T(8,128)}, u32[]{:S(2)}, u32[]{:S(2)}) collective-permute-start(f32[1024,128]{1,0:T(8,128)S(1)} %bitcast.52), channel_id=1, source_target_pairs={{0,4},{4,0},{8,12},{12,8},{16,20},{20,16},{24,28},{28,24},{32,36},... | collective-permute-start | bytes 1572872 | tf_op jit(solution)/shard_map/ppermute | solution.py:33
  100.7 0.9 copy-start.4
  101.5 11.6 %all-to-all-start.4 = ((f32[4,32,1152]{2,1,0:T(8,128)}), f32[4,32,1152]{2,1,0:T(8,128)S(1)}, u32[]{:S(2)}, u32[]{:S(2)}) async-start(f32[4,32,1152]{2,1,0:T(8,128)} %copy-done.4), calls=%async_computation.4 | async-start | bytes 1179648 | tf_op jit(solution)/shard_map/all_to_all | solution.py:286
  105.5 22.9 %copy-start.1 = (f32[1,128,1024]{2,1,0:T(8,128)S(1)}, f32[1,128,1024]{2,1,0:T(8,128)}, u32[]{:S(2)}) copy-start(f32[1,128,1024]{2,1,0:T(8,128)} %param.16) | copy-start | bytes 1572868
  113.1 15.3 %copy-start.3 = (bf16[1,128,1024]{2,1,0:T(8,128)(2,1)S(1)}, bf16[1,128,1024]{2,1,0:T(8,128)(2,1)}, u32[]{:S(2)}) copy-start(bf16[1,128,1024]{2,1,0:T(8,128)(2,1)} %param.15) | copy-start | bytes 786436
  113.1 15.3 %copy-start.9 = (f32[128,8]{0,1:T(8,128)S(1)}, f32[128,8]{0,1:T(8,128)}, u32[]{:S(2)}) copy-start(f32[128,8]{0,1:T(8,128)} %param.22) | copy-start | bytes 12292
  113.1 15.3 %copy-start.11 = (f32[8,128]{1,0:T(8,128)S(1)}, f32[8,128]{1,0:T(8,128)}, u32[]{:S(2)}) copy-start(f32[8,128]{1,0:T(8,128)} %moment_query.1) | copy-start | bytes 12292
  113.1 0.7 copy-start.13
  113.8 13.3 %copy-start.16 = (f32[28]{0:T(128)S(1)}, f32[28]{0:T(128)}, u32[]{:S(2)}) copy-start(f32[28]{0:T(128)} %param.24) | copy-start | bytes 340
  118.8 9.7 %collective-permute-start.1 = (f32[32,1152]{1,0:T(8,128)S(1)}, f32[32,1152]{1,0:T(8,128)S(1)}, u32[]{:S(2)}, u32[]{:S(2)}) collective-permute-start(f32[32,1152]{1,0:T(8,128)S(1)} %shard_map.190.mine), channel_id=1, source_target_pairs={{0,4},{4,0},{8,12},{12,8},{16,20},{20,16},{24,28},{28,24},{32,36},... | collective-permute-start | bytes 442376 | tf_op jit(solution)/shard_map/ppermute | solution.py:33

commit v3 on v2

--- a/solution.py
+++ b/solution.py
@@ -52,31 +52,43 @@
         for t in range(tiles)
     ]
     done = [jnp.zeros((8, LANES), jnp.float32) for _ in range(tiles)]
-    for k in range(rank):
+    wide = (8, LANES)
+    for k in range(0, rank, 2):
         at, place = k // 8, k % 8
-        row = jnp.broadcast_to(rows[at][place:place + 1], (8, LANES))
-        columns = [jnp.broadcast_to(rows[t][:, k:k + 1], (8, LANES)) for t in range(at, tiles)]
-        pivot = jnp.broadcast_to(columns[0][place:place + 1], (8, LANES))
-        scaled = row / pivot
-        done[at] = jnp.where(sub == place, row * lax.rsqrt(pivot), done[at])
+        near = [jnp.broadcast_to(rows[t][:, k:k + 1], wide) for t in range(at, tiles)]
+        far = [jnp.broadcast_to(rows[t][:, k + 1:k + 2], wide) for t in range(at, tiles)]
+        upper = jnp.broadcast_to(rows[at][place:place + 1], wide)
+        lower = jnp.broadcast_to(rows[at][place + 1:place + 2], wide)
+        pivot = jnp.broadcast_to(near[0][place:place + 1], wide)
+        below = jnp.broadcast_to(near[0][place + 1:place + 2], wide)
+        corner = jnp.broadcast_to(far[0][place + 1:place + 2], wide)
+        inverse = 1.0 / pivot
+        ratio = below * inverse
+        second = corner - below * ratio
+        lower = lower - ratio * upper
+        done[at] = jnp.where(sub == place, upper * lax.rsqrt(pivot), done[at])
+        done[at] = jnp.where(sub == place + 1, lower * lax.rsqrt(second), done[at])
+        upper = upper * inverse
+        lower = lower * (1.0 / second)
         for t in range(at, tiles):
-            take = columns[t - at] * scaled
-            rows[t] = rows[t] - (jnp.where(sub > place, take, 0.0) if t == at else take)
+            one, two = near[t - at], far[t - at]
+            take = one * upper + (two - one * ratio) * lower
+            rows[t] = rows[t] - (jnp.where(sub > place + 1, take, 0.0) if t == at else take)
     return pltpu.roll(jnp.concatenate(done), half, 1)
 
 
-def send_partials(narrow, recv, gram, sent, block):
+def send_partials(narrow, recv, stage, sent, sems, block):
     ring = recv.shape[0]
     rank = narrow.shape[0]
-    gram[...] = jnp.zeros_like(gram)
-    gram[:, :rank] = dot(narrow, narrow, ((1,), (1,)))
-    own = gram[...]
-    for copy in range(sent.shape[0]):
-        sent[copy, :, ring * block:] = own
+    stage[:, ring * block:] = jnp.zeros((rank, LANES), jnp.float32)
+    stage[:, ring * block:ring * block + rank] = dot(narrow, narrow, ((1,), (1,)))
     for j in range(ring):
-        part = dot(narrow, recv[j, :block], ((1,), (1,)))
-        for copy in range(sent.shape[0]):
-            sent[copy, :, j * block:(j + 1) * block] = part
+        stage[:, j * block:(j + 1) * block] = dot(narrow, recv[j, :block], ((1,), (1,)))
+    copies = [pltpu.make_async_copy(stage, sent.at[peer], sems.at[peer]) for peer in range(sent.shape[0])]
+    for copy in copies:
+        copy.start()
+    for copy in copies:
+        copy.wait()
 
 
 def normalized(spot, got, gram, block, ring):
@@ -99,7 +111,7 @@
     return sum(dot(wide[:, j * block:(j + 1) * block], recv[j, :block], ((1,), (0,))) for j in range(recv.shape[0]))
 
 
-def first_kernel(block, spot, recv, start_query, start_output, sent, narrow, gram):
+def first_kernel(block, spot, recv, start_query, start_output, sent, narrow, stage, sems):
     @pl.when(spot[1] == 0)
     def _():
         narrow[...] = start_query[...]
@@ -108,14 +120,14 @@
     def _():
         narrow[...] = times_matrix(start_output[...], recv, block)
 
-    send_partials(narrow[...], recv, gram, sent, block)
-
-
-def middle_kernel(block, spot, recv, got, sent, narrow, gram):
+    send_partials(narrow[...], recv, stage, sent, sems, block)
+
+
+def middle_kernel(block, spot, recv, got, sent, narrow, gram, stage, sems):
     _, wide = normalized(spot, got, gram, block, recv.shape[0])
     value = times_matrix(wide, recv, block)
     narrow[...] = value
-    send_partials(value, recv, gram, sent, block)
+    send_partials(value, recv, stage, sent, sems, block)
 
 
 def last_kernel(block, spot, recv, got, narrow, factors, gram):
@@ -185,13 +197,97 @@
             copy.wait()
 
 
+def prelude_kernel(
+    ring, per, slot, vec, spot, grad_query, error_query, grad_output, error_output, grad_vector, weight_query,
+    moment_query, weight_output, moment_output, weight_vector, moment_vector, mine, sent, kept,
+    grad_q, error_q, grad_o, error_o, line, sems,
+):
+    height, width = grad_query.shape
+    block = height // ring
+    tall = block + slot
+    rows = weight_query.shape[0]
+    small = weight_vector.shape[1]
+    index, odd = spot[0], spot[1]
+    moves = [
+        pltpu.make_async_copy(*pair, sems.at[n])
+        for n, pair in enumerate(
+            ((grad_query, grad_q), (error_query, error_q), (grad_output, grad_o), (error_output, error_o))
+        )
+    ]
+    for move in moves:
+        move.start()
+
+    line[...] = jnp.zeros_like(line)
+    line[0:1, :small] = weight_vector[...] - 0.009 * moment_vector[...]
+    first = index * small
+    spread = pltpu.roll(jnp.broadcast_to(line[0:1], (slot, LANES)), first % LANES, 1)
+    sub = lax.broadcasted_iota(jnp.int32, (slot, LANES), 0)
+    lane = lax.broadcasted_iota(jnp.int32, (slot, LANES), 1)
+    for j in range(ring):
+        after = LANES * (per * j + sub - per) + lane - first
+        inside = (sub >= per) & (sub < 2 * per) & (after >= 0) & (after < small)
+        value = jnp.where(inside, spread, 0.0)
+        for ref in (mine, sent):
+            ref[j * tall + block:(j + 1) * tall] = value
+        for n in range(per):
+            r = per * j + n
+            if r * LANES < vec:
+                row = grad_vector[:, r * LANES:(r + 1) * LANES].astype(jnp.float32)
+                for ref in (mine, sent):
+                    ref[j * tall + block + n:j * tall + block + n + 1] = row
+    kept_query = weight_query[...] - 0.009 * moment_query[...]
+    kept_output = weight_output[...] - 0.009 * moment_output[...]
+    kept[...] = jnp.where(odd == 0, kept_query, kept_output)
+    sent[ring * tall:ring * tall + rows] = jnp.where(odd == 0, kept_output, kept_query)
+
+    def totals(query, output):
+        moves[0].wait()
+        moves[1].wait()
+        for j in range(ring):
+            down = slice(j * block, (j + 1) * block)
+            query[j * tall:j * tall + block] = grad_q[down].astype(jnp.float32) + error_q[down]
+        moves[2].wait()
+        moves[3].wait()
+        for j in range(ring):
+            down = slice(j * block, (j + 1) * block)
+            output[j * tall:j * tall + block] = grad_o[:, down].astype(jnp.float32) + error_o[:, down]
+
+    @pl.when(odd == 0)
+    def _():
+        totals(mine, sent)
+
+    @pl.when(odd == 1)
+    def _():
+        totals(sent, mine)
+
+
+def vector_kernel(block, per, shards, spot, recv, moment_vector, new_moment, new_weight, mean, kept):
+    ring = recv.shape[0]
+    small = moment_vector.shape[1]
+    for j in range(ring):
+        mean[per * j:per * (j + 1)] = recv[j, block:block + per] * (1.0 / shards)
+        kept[per * j:per * (j + 1)] = recv[j, block + per:block + 2 * per]
+    mean[per * ring:] = jnp.zeros((mean.shape[0] - per * ring, LANES), jnp.float32)
+    lines = new_weight.shape[0]
+    new_weight[...] = kept[:lines] - 0.01 * mean[:lines]
+    first = spot[0] * small
+    row, off = first // LANES, first % LANES
+    shift = (LANES - off) % LANES
+    one = pltpu.roll(jnp.broadcast_to(mean[pl.ds(row, 1)], (8, LANES)), shift, 1)
+    two = pltpu.roll(jnp.broadcast_to(mean[pl.ds(row + 1, 1)], (8, LANES)), shift, 1)
+    lane = lax.broadcasted_iota(jnp.int32, (8, LANES), 1)
+    own = jnp.where(lane < LANES - off, one, two)
+    new_moment[...] = 0.9 * moment_vector[...] + own[0:1, :small]
+
+
 def shape(*dims):
     return jax.ShapeDtypeStruct(dims, jnp.float32)
 
 
-def run(kernel, given, out_shape, scratch, out_specs=None, **options):
+def run(kernel, given, out_shape, scratch, out_specs=None, outside=0, **options):
     whole = pl.BlockSpec(memory_space=pltpu.VMEM)
-    specs = [pl.BlockSpec(memory_space=pltpu.SMEM)] + [whole] * (len(given) - 1)
+    left = [pl.BlockSpec(memory_space=pl.ANY)] * outside
+    specs = [pl.BlockSpec(memory_space=pltpu.SMEM)] + left + [whole] * (len(given) - 1 - outside)
     if out_specs is None:
         out_specs = jax.tree.map(lambda _: whole, out_shape)
     return pl.pallas_call(
@@ -227,78 +323,71 @@
     block = height // ring
     rows = height // shards
     vec = grad_vector.shape[1]
-    piece = vec // ring
     small = vec // shards
-    assert width == LANES and rows % 8 == 0 or rows * shards == height
-    vec_rows = -(-piece // (8 * LANES)) * 8
-
-    total_query = grad_query[0].astype(jnp.float32) + error_query[0]
-    total_output = grad_output[0].astype(jnp.float32) + error_output[0]
-    query_blocks = total_query.reshape(ring, block, width)
-    output_blocks = total_output.reshape(width, ring, block).transpose(1, 0, 2)
-    vector_blocks = jnp.pad(
-        grad_vector[0].astype(jnp.float32).reshape(ring, piece), ((0, 0), (0, vec_rows * LANES - piece))
-    ).reshape(ring, vec_rows, LANES)
-
-    kept_query = weight_query - 0.009 * moment_query
-    kept_output = (weight_output - 0.009 * moment_output).T
-    kept_vector = jnp.pad(weight_vector - 0.009 * moment_vector, (0, LANES - small))
-
-    mine = jnp.where(even, query_blocks, output_blocks)
-    theirs = jnp.where(even, output_blocks, query_blocks)
-    own_kept = jnp.where(even, kept_query, kept_output)
-    other_kept = jnp.where(even, kept_output, kept_query)
-    sent = jnp.concatenate([
-        jnp.concatenate([theirs, vector_blocks], axis=1).reshape(-1, LANES),
-        other_kept,
-        jnp.pad(kept_vector[None], ((0, 7), (0, 0))),
-    ])
+    lines = vec // LANES
+    per = -(-lines // ring)
+    slot = -(-2 * per // 8) * 8
+    tall = block + slot
+    assert width == LANES and rows * shards == height and small * shards == vec and lines * LANES == vec
+
+    spot = jnp.stack([index, index % 2]).astype(jnp.int32)
+    mine, sent, own_kept = run(
+        functools.partial(prelude_kernel, ring, per, slot, vec),
+        (
+            spot, grad_query[0], error_query[0], grad_output[0], error_output[0], grad_vector, weight_query,
+            moment_query, weight_output.T, moment_output.T, weight_vector[None], moment_vector[None],
+        ),
+        (shape(ring * tall, LANES), shape(ring * tall + rows, LANES), shape(rows, LANES)),
+        [
+            pltpu.VMEM((height, width), grad_query.dtype), pltpu.VMEM((height, width), jnp.float32),
+            pltpu.VMEM((width, height), grad_output.dtype), pltpu.VMEM((width, height), jnp.float32),
+            pltpu.VMEM((8, LANES), jnp.float32), pltpu.SemaphoreType.DMA((4,)),
+        ],
+        outside=4,
+    )
     got = swap_cores(sent, shards)
-    tall = ring * (block + vec_rows)
-    summed = jnp.concatenate([mine, vector_blocks], axis=1) + got[:tall].reshape(ring, block + vec_rows, LANES)
-    got_kept = got[tall:tall + rows]
-    got_vector = got[tall + rows, :small]
-    own_vector = kept_vector[:small]
+    summed = (mine + got[:ring * tall]).reshape(ring, tall, LANES)
+    got_kept = got[ring * tall:]
     pair_kept = jnp.where(even, jnp.concatenate([own_kept, got_kept]), jnp.concatenate([got_kept, own_kept]))
-    pair_vector = jnp.where(even, jnp.concatenate([own_vector, got_vector]), jnp.concatenate([got_vector, own_vector]))
-    pair_vector = jnp.pad(pair_vector[None], ((0, 7), (0, LANES - 2 * small)))
 
     part = exchange(summed, first).sum(0)
-    every = share(jnp.concatenate([part, pair_kept, pair_vector]), second, ring)
-    whole = every[:, :block + vec_rows].sum(0)
+    every = share(jnp.concatenate([part, pair_kept]), second, ring)
+    whole = every[:, :tall].sum(0)
     square = jnp.where(even, whole[:block], whole[:block].T)
-    kept_rows = every[:, block + vec_rows:block + vec_rows + 2 * rows].reshape(block, LANES)
-    kept_vectors = every[:, block + vec_rows + 2 * rows]
-    every = share(jnp.concatenate([square, whole[block:], kept_rows, kept_vectors]), first, ring)
-    vector_sum = every[:, block:block + vec_rows].reshape(ring, -1)[:, :piece].reshape(vec)
-    kept_all = every[:, block + vec_rows:2 * block + vec_rows].reshape(ring, ring, 2 * rows, LANES)
+    kept_rows = every[:, tall:].reshape(block, LANES)
+    every = share(jnp.concatenate([square, whole[block:], kept_rows]), first, ring)
+    kept_all = every[:, tall:].reshape(ring, ring, 2 * rows, LANES)
     kept_turned = kept_all.transpose(1, 0, 2, 3).reshape(ring, block, LANES).transpose(0, 2, 1)
     kept_all = jnp.where(even, kept_all.reshape(ring, block, LANES), kept_turned).reshape(height, LANES)
-    kept_vectors = every[:, 2 * block + vec_rows:][:, :, :2 * small]
-    kept_vectors = jnp.where(even, kept_vectors, kept_vectors.transpose(1, 0, 2)).reshape(vec)
     kept_other = swap_cores(kept_all, shards)
-
-    spot = jnp.stack([index, index % 2]).astype(jnp.int32)
+    new_moment_vector, new_weight_vector = run(
+        functools.partial(vector_kernel, block, per, shards), (spot, every, moment_vector[None]),
+        (shape(1, small), shape(lines, LANES)),
+        [pltpu.VMEM((per * ring + 8, LANES), jnp.float32), pltpu.VMEM((per * ring, LANES), jnp.float32)],
+    )
+
     gram = pltpu.VMEM((rank, LANES), jnp.float32)
     partials = shape(tensors, rank, height + LANES)
 
     def gathered(value):
         return lax.all_to_all(value, "tensor", 0, 0, tiled=True)
 
+    stage = [pltpu.VMEM((rank, height + LANES), jnp.float32), pltpu.SemaphoreType.DMA((tensors,))]
+    outside, within = pl.BlockSpec(memory_space=pl.ANY), pl.BlockSpec(memory_space=pltpu.VMEM)
     sent, narrow = run(
         functools.partial(first_kernel, block), (spot, every, start_query.T, start_output.T),
-        (partials, shape(rank, width)), [gram],
+        (partials, shape(rank, width)), stage, (outside, within),
     )
     for turn in range(ROUNDS - 1):
         sent, narrow = run(
-            functools.partial(middle_kernel, block), (spot, every, gathered(sent)), (partials, shape(rank, width)), [gram]
+            functools.partial(middle_kernel, block), (spot, every, gathered(sent)), (partials, shape(rank, width)),
+            [gram, *stage], (outside, within),
         )
     mine = run(
         functools.partial(last_kernel, block), (spot, every, gathered(sent), narrow), shape(rank, height + width), [gram]
     )
     other = swap_cores(mine, shards)
     big = [pltpu.VMEM((height, width), jnp.float32), pltpu.VMEM((width, height), jnp.float32)]
-    outside, within = pl.BlockSpec(memory_space=pl.ANY), pl.BlockSpec(memory_space=pltpu.VMEM)
     (
         new_error_query, new_error_output, new_moment_query, new_moment_output, new_weight_query, new_weight_output,
     ) = run(
@@ -314,9 +403,6 @@
     new_error_query = new_error_query[None]
     new_error_output = new_error_output[None]
     new_moment_output = new_moment_output.T
-    vector_mean = vector_sum / shards
-    new_moment_vector = 0.9 * moment_vector + lax.dynamic_slice_in_dim(vector_mean, index * small, small, 0)
-    new_weight_vector = kept_vectors - 0.01 * vector_mean
     return (
         new_error_query,
         new_error_output,
@@ -324,8 +410,8 @@
         new_moment_output,
         new_weight_query,
         new_weight_output,
-        new_moment_vector,
-        new_weight_vector,
+        new_moment_vector[0],
+        new_weight_vector.reshape(vec),
     )
 
 

time: 133 us -> 129 us (0.970)
  blocking collectives: 20.2 us -> 40.7 us
  waiting for transfers between devices: 32.8 us -> 21.1 us
  other arithmetic: 6.78 us -> 1.16 us
  local copies, waits for them, and re-layouts: 14.3 us -> 9.29 us
  starting transfers between devices: 39.4 us -> 37 us
    all_to_all x1 -> x2, blocking collectives: 20.2 us -> 40.7 us  [exchange(): lax.all_to_all(value, 'shard', 0, 0, axis_index_groups=group, tiled=True)]
    all_to_all x2 -> x1, waiting for transfers between devices: 30.7 us -> 12.5 us  [exchange(): lax.all_to_all(value, 'shard', 0, 0, axis_index_groups=group, tiled=True)]
    all_to_all x2, waiting for transfers between devices: 0.53 us -> 7.03 us  [gathered(): return lax.all_to_all(value, 'tensor', 0, 0, tiled=True)]
    all_to_all x2 -> x1, starting transfers between devices: 8.22 us -> 4.66 us  [exchange(): lax.all_to_all(value, 'shard', 0, 0, axis_index_groups=group, tiled=True)]
    sub x2 -> x0, other arithmetic: 2.02 us -> none  [the longest x1 1.34 us: local(): new_weight_vector = kept_vectors - 0.01 * vector_mean]
    ppermute x3, starting transfers between devices: 23.2 us -> 24.8 us  [swap_cores(): return lax.ppermute(value, 'shard', [(s, s ^ 1) for s in range(shards)])]
    reshape x2 -> x1, local copies, waits for them, and re-layouts: 1.49 us -> 0.04 us  [local(): kept_all = every[:, tall:].reshape(ring, ring, 2 * rows, LANES)]
    div x1 -> x0, local copies, waits for them, and re-layouts: 1.4 us -> none  [local(): vector_mean = vector_sum / shards]
  transfers between devices with their start and end apart: 7 -> 6, of which waited for: 4 -> 3; matrix products, arithmetic and copies ran while one was open for 7% -> 0% of each run, Pallas kernels for 9% -> 3%
where the time goes in v3:
time: 129 us
  blocking collectives  40.7 us (32%)
  starting transfers between devices  37 us (29%)
  waiting for transfers between devices  21.1 us (16%)
  Pallas kernels  18.4 us (14%)
  local copies, waits for them, and re-layouts  9.29 us (7%)
    all_to_all x2, blocking collectives, exchange(): lax.all_to_all(value, 'shard', 0, 0, axis_index_groups=group, tiled=True)  40.7 us
    ppermute x3, starting transfers between devices, swap_cores(): return lax.ppermute(value, 'shard', [(s, s ^ 1) for s in range(shards)])  24.8 us
    pallas_call x6, Pallas kernels, run(): pl.pallas_call(kernel, out_shape=out_shape, in_specs=specs, out_specs=out...  18.4 us
    all_to_all x1, waiting for transfers between devices, exchange(): lax.all_to_all(value, 'shard', 0, 0, axis_index_groups=group, tiled=True)  12.5 us
    unnamed x40, local copies, waits for them, and re-layouts  8.8 us
    all_to_all x2, starting transfers between devices, gathered(): return lax.all_to_all(value, 'tensor', 0, 0, tiled=True)  7.51 us
    all_to_all x2, waiting for transfers between devices, gathered(): return lax.all_to_all(value, 'tensor', 0, 0, tiled=True)  7.03 us
    all_to_all x1, starting transfers between devices, exchange(): lax.all_to_all(value, 'shard', 0, 0, axis_index_groups=group, tiled=True)  4.66 us
  transfers between devices with their start and end apart: 6, of which 3 were waited for; matrix products, arithmetic and copies ran while one was open for 0% of the time, Pallas kernels for 3%

profile of v3, /device:TPU:1, one launch (start us, length us, event | category | flops | bytes accessed | tf_op | source)
XLA Modules:
  0.0 128.6 jit_solution(16798457219656832409)
XLA Ops:
  0.6 0.1 pad_add_fusion.spot
  0.7 1.0 copy-done
  1.8 1.0 copy-done.2
  2.8 0.9 copy-done.4
  3.8 0.9 copy-done.6
  4.7 0.7 copy-done.10
  5.4 0.7 copy-done.12
  6.1 0.7 copy-done.14
  6.8 0.7 copy-done.15
  7.5 0.7 copy-done.16
  8.2 0.7 copy-done.17
  8.8 0.7 copy-done.19
  9.5 0.9 shard_map.188
  10.4 8.8 %collective-permute-start = (f32[1096,128]{1,0:T(8,128)S(1)}, f32[1096,128]{1,0:T(8,128)S(1)}, u32[]{:S(2)}, u32[]{:S(2)}) collective-permute-start(f32[1096,128]{1,0:T(8,128)S(1)} %get-tuple-element.23), channel_id=1, source_target_pairs={{0,4},{4,0},{8,12},{12,8},{16,20},{20,16},{24,28},{28,24},{32,36},... | collective-permute-start | bytes 1683464 | tf_op jit(solution)/shard_map/ppermute | solution.py:33
  19.2 1.6 %collective-permute-done = f32[1096,128]{1,0:T(8,128)S(1)} collective-permute-done((f32[1096,128]{1,0:T(8,128)S(1)}, f32[1096,128]{1,0:T(8,128)S(1)}, u32[]{:S(2)}, u32[]{:S(2)}) %collective-permute-start) | collective-permute-done | bytes 561184 | tf_op jit(solution)/shard_map/ppermute | solution.py:33
  20.7 0.9 slice_add_fusion
  21.7 4.7 %all-to-all-start = ((f32[8,136,128]{2,1,0:T(8,128)}), f32[8,136,128]{2,1,0:T(8,128)S(1)}, u32[]{:S(2)}, u32[]{:S(2)}) async-start(f32[8,136,128]{2,1,0:T(8,128)} %bitcast.10), calls=%async_computation | async-start | bytes 1114112 | tf_op jit(solution)/shard_map/all_to_all | solution.py:37
  26.3 12.5 %all-to-all-done = f32[8,136,128]{2,1,0:T(8,128)S(1)} async-done(((f32[8,136,128]{2,1,0:T(8,128)}), f32[8,136,128]{2,1,0:T(8,128)S(1)}, u32[]{:S(2)}, u32[]{:S(2)}) %all-to-all-start) | async-done | bytes 557088 | tf_op jit(solution)/shard_map/all_to_all | solution.py:37
  38.9 19.8 %all_to_all.25 = f32[8,152,128]{2,1,0:T(8,128)S(1)} all-to-all(f32[8,152,128]{2,1,0:T(8,128)S(1)} %broadcast_in_dim.27), channel_id=1, replica_groups={{0,8,16,24,32,40,48,56},{64,72,80,88,96,104,112,120},{128,136,144,152,1..., dimensions={0} | all-to-all | bytes 1245184 | tf_op jit(solution)/shard_map/all_to_all | solution.py:37
  58.8 0.1 copy.23
  58.9 0.1 broadcast_in_dim.28
  59.0 0.0 copy-start.8
  59.0 0.0 copy-start.9
  59.0 20.9 %all_to_all.26.recv = f32[8,264,128]{2,1,0:T(8,128)S(1)} all-to-all(f32[8,264,128]{2,1,0:T(8,128)S(1)} %broadcast_in_dim.28), channel_id=1, replica_groups={{0,64,128,192,256,320,384,448},{8,72,136,200,264,328,392,456},{16,80,14..., dimensions={0} | all-to-all | bytes 2162688 | tf_op jit(solution)/shard_map/all_to_all | solution.py:37
  80.0 0.0 copy-done.9
  80.0 3.5 %shard_map.189 = (f32[4,32,1152]{2,1,0:T(8,128)}, f32[32,128]{1,0:T(8,128)}) custom-call(s32[2]{0:T(128)S(1)} %pad_add_fusion.spot, f32[8,264,128]{2,1,0:T(8,128)S(1)} %all_to_all.26.recv, f32[32,128]{1,0:T(8,128)S(1)} %bitcast.39, f32[32,1024]{1,0:T(8,128)S(1)} %bitcast.38), custom_call_target="tpu_custom_call" | custom-call | tf_op jit(solution)/shard_map/pallas_call | solution.py:293
  83.5 4.0 %all-to-all-start.3 = ((f32[4,32,1152]{2,1,0:T(8,128)}), f32[4,32,1152]{2,1,0:T(8,128)S(1)}, u32[]{:S(2)}, u32[]{:S(2)}) async-start(f32[4,32,1152]{2,1,0:T(8,128)} %get-tuple-element.25), calls=%async_computation.3 | async-start | bytes 1179648 | tf_op jit(solution)/shard_map/all_to_all | solution.py:373
  87.6 0.2 copy.25
  87.8 7.0 %all-to-all-done.3.got = f32[4,32,1152]{2,1,0:T(8,128)S(1)} async-done(((f32[4,32,1152]{2,1,0:T(8,128)}), f32[4,32,1152]{2,1,0:T(8,128)S(1)}, u32[]{:S(2)}, u32[]{:S(2)}) %all-to-all-start.3) | async-done | bytes 589856 | tf_op jit(solution)/shard_map/all_to_all | solution.py:373
  94.8 6.3 %shard_map.190 = (f32[4,32,1152]{2,1,0:T(8,128)}, f32[32,128]{1,0:T(8,128)S(1)}) custom-call(s32[2]{0:T(128)S(1)} %pad_add_fusion.spot, f32[8,264,128]{2,1,0:T(8,128)S(1)} %all_to_all.26.recv, f32[4,32,1152]{2,1,0:T(8,128)S(1)} %all-to-all-done.3.got), custom_call_target="tpu_custom_call" | custom-call | tf_op jit(solution)/shard_map/pallas_call | solution.py:293
  101.1 3.5 %all-to-all-start.4 = ((f32[4,32,1152]{2,1,0:T(8,128)}), f32[4,32,1152]{2,1,0:T(8,128)S(1)}, u32[]{:S(2)}, u32[]{:S(2)}) async-start(f32[4,32,1152]{2,1,0:T(8,128)} %get-tuple-element.26), calls=%async_computation.4 | async-start | bytes 1179648 | tf_op jit(solution)/shard_map/all_to_all | solution.py:373
  104.6 0.1 bitcast_select_fusion
  104.6 0.0 copy-start.18
  104.7 7.1 %collective-permute-start.2 = (f32[1024,128]{1,0:T(8,128)S(1)}, f32[1024,128]{1,0:T(8,128)S(1)}, u32[]{:S(2)}, u32[]{:S(2)}) collective-permute-start(f32[1024,128]{1,0:T(8,128)S(1)} %bitcast.32), channel_id=1, source_target_pairs={{0,4},{4,0},{8,12},{12,8},{16,20},{20,16},{24,28},{28,24},{32,36},... | collective-permute-start | bytes 1572872 | tf_op jit(solution)/shard_map/ppermute | solution.py:33
  111.8 0.0 all-to-all-done.4.got
  111.8 0.0 copy-start.7
  111.9 0.0 copy-start.11
  111.9 0.0 copy-start.13
  111.9 3.3 %shard_map.191.mine = f32[32,1152]{1,0:T(8,128)S(1)} custom-call(s32[2]{0:T(128)S(1)} %pad_add_fusion.spot, f32[8,264,128]{2,1,0:T(8,128)S(1)} %all_to_all.26.recv, f32[4,32,1152]{2,1,0:T(8,128)S(1)} %all-to-all-done.4.got, f32[32,128]{1,0:T(8,128)S(1)} %get-tuple-element.27.narrow), custom_call_target="tpu_custom_call" | custom-call | tf_op jit(solution)/shard_map/pallas_call | solution.py:293
  115.2 8.9 %collective-permute-start.1 = (f32[32,1152]{1,0:T(8,128)S(1)}, f32[32,1152]{1,0:T(8,128)S(1)}, u32[]{:S(2)}, u32[]{:S(2)}) collective-permute-start(f32[32,1152]{1,0:T(8,128)S(1)} %shard_map.191.mine), channel_id=1, source_target_pairs={{0,4},{4,0},{8,12},{12,8},{16,20},{20,16},{24,28},{28,24},{32,36},... | collective-permute-start | bytes 442376 | tf_op jit(solution)/shard_map/ppermute | solution.py:33
  124.1 1.2 shard_map.193
  125.3 0.0 collective-permute-done.2.kept_other
  125.3 0.0 collective-permute-done.1.other
  125.3 0.0 copy-done.1
  125.3 0.0 copy-done.3
  125.3 0.0 copy-done.5
  125.3 0.0 copy-done.7
  125.3 3.3 %shard_map.192 = (f32[1024,128]{1,0:T(8,128)}, f32[128,1024]{1,0:T(8,128)}, f32[8,128]{1,0:T(8,128)}, f32[8,128]{1,0:T(8,128)}, f32[1024,128]{1,0:T(8,128)}, /*index=5*/f32[128,1024]{1,0:T(8,128)}) custom-call(s32[2]{0:T(128)S(1)} %pad_add_fusion.spot, f32[32,1152]{1,0:T(8,128)S(1)} %shard_map.191.mine, f32[32,1152]{1,0:T(8,128)S(1)} %collective-permute-done.1.other, ...), custom_call_target="tpu_custom_call" | custom-call | tf_op jit(solution)/shard_map/pallas_call | solution.py:293
  (31 shorter events, 0.3 us)
Async XLA Ops:
  0.7 1.0 copy-start
  1.8 1.0 copy-start.2
  2.8 0.9 copy-start.4
  3.8 0.9 copy-start.6
  4.7 0.7 copy-start.10
  5.4 0.7 copy-start.12
  6.1 0.7 copy-start.14
  6.8 0.7 copy-start.15
  7.5 0.7 copy-start.16
  8.2 0.7 copy-start.17
  8.8 0.7 copy-start.19
  10.4 10.4 %collective-permute-start = (f32[1096,128]{1,0:T(8,128)S(1)}, f32[1096,128]{1,0:T(8,128)S(1)}, u32[]{:S(2)}, u32[]{:S(2)}) collective-permute-start(f32[1096,128]{1,0:T(8,128)S(1)} %get-tuple-element.23), channel_id=1, source_target_pairs={{0,4},{4,0},{8,12},{12,8},{16,20},{20,16},{24,28},{28,24},{32,36},... | collective-permute-start | bytes 1683464 | tf_op jit(solution)/shard_map/ppermute | solution.py:33
  21.7 17.2 %all-to-all-start = ((f32[8,136,128]{2,1,0:T(8,128)}), f32[8,136,128]{2,1,0:T(8,128)S(1)}, u32[]{:S(2)}, u32[]{:S(2)}) async-start(f32[8,136,128]{2,1,0:T(8,128)} %bitcast.10), calls=%async_computation | async-start | bytes 1114112 | tf_op jit(solution)/shard_map/all_to_all | solution.py:37
  59.0 20.9 %copy-start.8 = (f32[1024,32]{0,1:T(8,128)S(1)}, f32[1024,32]{0,1:T(8,128)}, u32[]{:S(2)}) copy-start(f32[1024,32]{0,1:T(8,128)} %param.18) | copy-start | bytes 393220
  59.0 20.9 %copy-start.9 = (f32[128,32]{0,1:T(8,128)S(1)}, f32[128,32]{0,1:T(8,128)}, u32[]{:S(2)}) copy-start(f32[128,32]{0,1:T(8,128)} %param.17) | copy-start | bytes 49156
  83.5 11.3 %all-to-all-start.3 = ((f32[4,32,1152]{2,1,0:T(8,128)}), f32[4,32,1152]{2,1,0:T(8,128)S(1)}, u32[]{:S(2)}, u32[]{:S(2)}) async-start(f32[4,32,1152]{2,1,0:T(8,128)} %get-tuple-element.25), calls=%async_computation.3 | async-start | bytes 1179648 | tf_op jit(solution)/shard_map/all_to_all | solution.py:373
  101.1 10.7 %all-to-all-start.4 = ((f32[4,32,1152]{2,1,0:T(8,128)}), f32[4,32,1152]{2,1,0:T(8,128)S(1)}, u32[]{:S(2)}, u32[]{:S(2)}) async-start(f32[4,32,1152]{2,1,0:T(8,128)} %get-tuple-element.26), calls=%async_computation.4 | async-start | bytes 1179648 | tf_op jit(solution)/shard_map/all_to_all | solution.py:373
  104.6 19.4 %copy-start.18 = (f32[28]{0:T(128)S(1)}, f32[28]{0:T(128)}, u32[]{:S(2)}) copy-start(f32[28]{0:T(128)} %param.24) | copy-start | bytes 340
  104.7 20.6 %collective-permute-start.2 = (f32[1024,128]{1,0:T(8,128)S(1)}, f32[1024,128]{1,0:T(8,128)S(1)}, u32[]{:S(2)}, u32[]{:S(2)}) collective-permute-start(f32[1024,128]{1,0:T(8,128)S(1)} %bitcast.32), channel_id=1, source_target_pairs={{0,4},{4,0},{8,12},{12,8},{16,20},{20,16},{24,28},{28,24},{32,36},... | collective-permute-start | bytes 1572872 | tf_op jit(solution)/shard_map/ppermute | solution.py:33
  111.8 13.4 %copy-start.1 = (f32[1,1024,128]{2,1,0:T(8,128)S(1)}, f32[1,1024,128]{2,1,0:T(8,128)}, u32[]{:S(2)}) copy-start(f32[1,1024,128]{2,1,0:T(8,128)} %param.14) | copy-start | bytes 1572868
  111.8 13.4 %copy-start.3 = (f32[1,128,1024]{2,1,0:T(8,128)S(1)}, f32[1,128,1024]{2,1,0:T(8,128)}, u32[]{:S(2)}) copy-start(f32[1,128,1024]{2,1,0:T(8,128)} %param.16) | copy-start | bytes 1572868
  111.8 13.5 %copy-start.5 = (bf16[1,1024,128]{2,1,0:T(8,128)(2,1)S(1)}, bf16[1,1024,128]{2,1,0:T(8,128)(2,1)}, u32[]{:S(2)}) copy-start(bf16[1,1024,128]{2,1,0:T(8,128)(2,1)} %param.13) | copy-start | bytes 786436
  111.8 13.5 %copy-start.7 = (bf16[1,128,1024]{2,1,0:T(8,128)(2,1)S(1)}, bf16[1,128,1024]{2,1,0:T(8,128)(2,1)}, u32[]{:S(2)}) copy-start(bf16[1,128,1024]{2,1,0:T(8,128)(2,1)} %param.15) | copy-start | bytes 786436
  111.9 13.5 %copy-start.11 = (f32[8,128]{1,0:T(8,128)S(1)}, f32[8,128]{1,0:T(8,128)}, u32[]{:S(2)}) copy-start(f32[8,128]{1,0:T(8,128)} %moment_query.3) | copy-start | bytes 12292
  111.9 13.5 %copy-start.13 = (f32[128,8]{0,1:T(8,128)S(1)}, f32[128,8]{0,1:T(8,128)}, u32[]{:S(2)}) copy-start(f32[128,8]{0,1:T(8,128)} %param.22) | copy-start | bytes 12292
  115.2 10.1 %collective-permute-start.1 = (f32[32,1152]{1,0:T(8,128)S(1)}, f32[32,1152]{1,0:T(8,128)S(1)}, u32[]{:S(2)}, u32[]{:S(2)}) collective-permute-start(f32[32,1152]{1,0:T(8,128)S(1)} %shard_map.191.mine), channel_id=1, source_target_pairs={{0,4},{4,0},{8,12},{12,8},{16,20},{20,16},{24,28},{28,24},{32,36},... | collective-permute-start | bytes 442376 | tf_op jit(solution)/shard_map/ppermute | solution.py:33

commit v4 on v3

--- a/solution.py
+++ b/solution.py
@@ -26,7 +26,7 @@
 def groups(ring):
     along_y = [[[(2 * (ring * y + z)) + c for y in range(ring)] for z in range(ring)] for c in range(2)]
     along_z = [[[(2 * (ring * y + z)) + c for z in range(ring)] for y in range(ring)] for c in range(2)]
-    return along_y[0] + along_z[1], along_z[0] + along_y[1]
+    return along_z[0] + along_y[1], along_y[0] + along_z[1]
 
 
 def swap_cores(value, shards):
@@ -145,7 +145,7 @@
 
 
 def final_kernel(
-    block, shards, spot, mine, other, kept_mine, kept_other, grad_query, error_query, grad_output, error_output,
+    block, shards, spot, mine, other, kept, grad_query, error_query, grad_output, error_output,
     moment_query, moment_output, new_error_query, new_error_output, new_moment_query, new_moment_output,
     new_weight_query, new_weight_output, error_q, error_o, weight_q, weight_o, sems,
 ):
@@ -164,17 +164,18 @@
             pltpu.make_async_copy(weight_o.at[:, down], new_weight_output.at[:, down], sems.at[3, j]),
         )
 
-    def body(query, output, kept_query, kept_output):
+    def body(query, output):
         right = query[:, height:] * scale
         left = output[:, height:] * scale
         for j in range(ring):
             down = slice(j * block, (j + 1) * block)
+            old = kept[j * block // rows:(j + 1) * block // rows]
             approx = dot(query[:, down], right, ((0,), (0,)))
             error_q[down] = grad_query[down].astype(jnp.float32) + error_query[down] - approx
-            weight_q[down] = kept_query[down] - 0.01 * approx
+            weight_q[down] = old[:, :rows].reshape(block, width) - 0.01 * approx
             approx = dot(left, output[:, down], ((0,), (0,)))
             error_o[:, down] = grad_output[:, down].astype(jnp.float32) + error_output[:, down] - approx
-            weight_o[:, down] = kept_output[down] - 0.01 * approx
+            weight_o[:, down] = old[:, rows:].reshape(block, width).T - 0.01 * approx
             for copy in copies(j):
                 copy.start()
         along = index * rows
@@ -186,11 +187,11 @@
 
     @pl.when(spot[1] == 0)
     def _():
-        body(mine, other, kept_mine, kept_other)
+        body(mine, other)
 
     @pl.when(spot[1] == 1)
     def _():
-        body(other, mine, kept_other, kept_mine)
+        body(other, mine)
 
     for j in range(ring):
         for copy in copies(j):
@@ -198,24 +199,20 @@
 
 
 def prelude_kernel(
-    ring, per, slot, vec, spot, grad_query, error_query, grad_output, error_output, grad_vector, weight_query,
-    moment_query, weight_output, moment_output, weight_vector, moment_vector, mine, sent, kept,
-    grad_q, error_q, grad_o, error_o, line, sems,
+    ring, per, slot, vec, spot, *refs
 ):
-    height, width = grad_query.shape
+    far, (mine, sent), near, (line, sems) = refs[:7], refs[7:9], refs[9:16], refs[16:]
+    moves = [pltpu.make_async_copy(*pair, sems.at[n]) for n, pair in enumerate(zip(far, near))]
+    for move in moves:
+        move.start()
+    grad_q, error_q, grad_o, error_o, grad_vector, weight_vector, moment_vector = near
+    height, width = grad_q.shape
     block = height // ring
     tall = block + slot
-    rows = weight_query.shape[0]
     small = weight_vector.shape[1]
     index, odd = spot[0], spot[1]
-    moves = [
-        pltpu.make_async_copy(*pair, sems.at[n])
-        for n, pair in enumerate(
-            ((grad_query, grad_q), (error_query, error_q), (grad_output, grad_o), (error_output, error_o))
-        )
-    ]
-    for move in moves:
-        move.start()
+    for move in moves[4:]:
+        move.wait()
 
     line[...] = jnp.zeros_like(line)
     line[0:1, :small] = weight_vector[...] - 0.009 * moment_vector[...]
@@ -235,10 +232,6 @@
                 row = grad_vector[:, r * LANES:(r + 1) * LANES].astype(jnp.float32)
                 for ref in (mine, sent):
                     ref[j * tall + block + n:j * tall + block + n + 1] = row
-    kept_query = weight_query[...] - 0.009 * moment_query[...]
-    kept_output = weight_output[...] - 0.009 * moment_output[...]
-    kept[...] = jnp.where(odd == 0, kept_query, kept_output)
-    sent[ring * tall:ring * tall + rows] = jnp.where(odd == 0, kept_output, kept_query)
 
     def totals(query, output):
         moves[0].wait()
@@ -286,7 +279,7 @@
 
 def run(kernel, given, out_shape, scratch, out_specs=None, outside=0, **options):
     whole = pl.BlockSpec(memory_space=pltpu.VMEM)
-    left = [pl.BlockSpec(memory_space=pl.ANY)] * outside
+    left = [pl.BlockSpec(memory_space=pltpu.HBM)] * outside
     specs = [pl.BlockSpec(memory_space=pltpu.SMEM)] + left + [whole] * (len(given) - 1 - outside)
     if out_specs is None:
         out_specs = jax.tree.map(lambda _: whole, out_shape)
@@ -316,7 +309,7 @@
     index = lax.axis_index("shard")
     ring = ring_size(shards)
     first, second = groups(ring)
-    even = (index % 2) == 0
+    asks = (index % 2) == 1
     width = start_query.shape[0]
     height = start_output.shape[0]
     rank = start_query.shape[1]
@@ -330,36 +323,29 @@
     tall = block + slot
     assert width == LANES and rows * shards == height and small * shards == vec and lines * LANES == vec
 
-    spot = jnp.stack([index, index % 2]).astype(jnp.int32)
-    mine, sent, own_kept = run(
-        functools.partial(prelude_kernel, ring, per, slot, vec),
-        (
-            spot, grad_query[0], error_query[0], grad_output[0], error_output[0], grad_vector, weight_query,
-            moment_query, weight_output.T, moment_output.T, weight_vector[None], moment_vector[None],
-        ),
-        (shape(ring * tall, LANES), shape(ring * tall + rows, LANES), shape(rows, LANES)),
+    kept = jnp.concatenate([weight_query - 0.009 * moment_query, (weight_output - 0.009 * moment_output).T])
+    kept = lax.all_gather(kept, "shard", axis=0, tiled=False)
+
+    spot = jnp.stack([index, 1 - index % 2]).astype(jnp.int32)
+    given = (
+        grad_query[0], error_query[0], grad_output[0], error_output[0], grad_vector, weight_vector[None],
+        moment_vector[None],
+    )
+    given = [pltpu.with_memory_space_constraint(value, pltpu.HBM) for value in given]
+    mine, sent = run(
+        functools.partial(prelude_kernel, ring, per, slot, vec), (spot, *given),
+        (shape(ring * tall, LANES), shape(ring * tall, LANES)),
         [
-            pltpu.VMEM((height, width), grad_query.dtype), pltpu.VMEM((height, width), jnp.float32),
-            pltpu.VMEM((width, height), grad_output.dtype), pltpu.VMEM((width, height), jnp.float32),
-            pltpu.VMEM((8, LANES), jnp.float32), pltpu.SemaphoreType.DMA((4,)),
+            *(pltpu.VMEM(value.shape, value.dtype) for value in given),
+            pltpu.VMEM((8, LANES), jnp.float32), pltpu.SemaphoreType.DMA((len(given),)),
         ],
-        outside=4,
-    )
-    got = swap_cores(sent, shards)
-    summed = (mine + got[:ring * tall]).reshape(ring, tall, LANES)
-    got_kept = got[ring * tall:]
-    pair_kept = jnp.where(even, jnp.concatenate([own_kept, got_kept]), jnp.concatenate([got_kept, own_kept]))
-
+        outside=len(given),
+    )
+    summed = (mine + swap_cores(sent, shards)).reshape(ring, tall, LANES)
     part = exchange(summed, first).sum(0)
-    every = share(jnp.concatenate([part, pair_kept]), second, ring)
-    whole = every[:, :tall].sum(0)
-    square = jnp.where(even, whole[:block], whole[:block].T)
-    kept_rows = every[:, tall:].reshape(block, LANES)
-    every = share(jnp.concatenate([square, whole[block:], kept_rows]), first, ring)
-    kept_all = every[:, tall:].reshape(ring, ring, 2 * rows, LANES)
-    kept_turned = kept_all.transpose(1, 0, 2, 3).reshape(ring, block, LANES).transpose(0, 2, 1)
-    kept_all = jnp.where(even, kept_all.reshape(ring, block, LANES), kept_turned).reshape(height, LANES)
-    kept_other = swap_cores(kept_all, shards)
+    whole = share(part, second, ring).sum(0)
+    square = jnp.where(asks, whole[:block], whole[:block].T)
+    every = share(jnp.concatenate([square, whole[block:]]), first, ring)
     new_moment_vector, new_weight_vector = run(
         functools.partial(vector_kernel, block, per, shards), (spot, every, moment_vector[None]),
         (shape(1, small), shape(lines, LANES)),
@@ -383,9 +369,10 @@
             functools.partial(middle_kernel, block), (spot, every, gathered(sent)), (partials, shape(rank, width)),
             [gram, *stage], (outside, within),
         )
-    mine = run(
-        functools.partial(last_kernel, block), (spot, every, gathered(sent), narrow), shape(rank, height + width), [gram]
-    )
+    got, new_moment_vector, new_weight_vector = lax.optimization_barrier(
+        (gathered(sent), new_moment_vector, new_weight_vector)
+    )
+    mine = run(functools.partial(last_kernel, block), (spot, every, got, narrow), shape(rank, height + width), [gram])
     other = swap_cores(mine, shards)
     big = [pltpu.VMEM((height, width), jnp.float32), pltpu.VMEM((width, height), jnp.float32)]
     (
@@ -393,7 +380,7 @@
     ) = run(
         functools.partial(final_kernel, block, shards),
         (
-            spot, mine, other, kept_all, kept_other, grad_query[0], error_query[0], grad_output[0], error_output[0],
+            spot, mine, other, kept, grad_query[0], error_query[0], grad_output[0], error_output[0],
             moment_query, moment_output.T,
         ),
         (shape(height, width), shape(width, height), shape(rows, width), shape(rows, width), shape(height, width), shape(width, height)),

time: 129 us -> 139 us (1.078)
  between operations: 0.93 us -> 14.3 us
  waiting for transfers between devices: 21.1 us -> 29.5 us
  starting transfers between devices: 37 us -> 29.5 us
  local copies, waits for them, and re-layouts: 9.29 us -> 2.86 us
    all_to_all x0 -> x1, blocking collectives: none -> 11.1 us  [gathered(): return lax.all_to_all(value, 'tensor', 0, 0, tiled=True)]
    all_gather x0 -> x1, waiting for transfers between devices: none -> 10.7 us  [local(): kept = lax.all_gather(kept, 'shard', axis=0, tiled=False)]
    all_to_all x2, blocking collectives: 40.7 us -> 30.2 us  [exchange(): lax.all_to_all(value, 'shard', 0, 0, axis_index_groups=group, tiled=True)]
    ppermute x3 -> x2, starting transfers between devices: 24.8 us -> 17 us  [swap_cores(): return lax.ppermute(value, 'shard', [(s, s ^ 1) for s in range(shards)])]
    unnamed x40 -> x24, local copies, waits for them, and re-layouts: 8.8 us -> 1.87 us
    all_to_all x1, starting transfers between devices: 4.66 us -> 9.04 us  [exchange(): lax.all_to_all(value, 'shard', 0, 0, axis_index_groups=group, tiled=True)]
    all_to_all x2 -> x1, starting transfers between devices: 7.51 us -> 3.49 us  [gathered(): return lax.all_to_all(value, 'tensor', 0, 0, tiled=True)]
    all_to_all x2 -> x1, waiting for transfers between devices: 7.03 us -> 6.06 us  [gathered(): return lax.all_to_all(value, 'tensor', 0, 0, tiled=True)]
  transfers between devices with their start and end apart: 6 -> 5, of which waited for: 3 -> 4; matrix products, arithmetic and copies ran while one was open for 0% -> 1% of each run, Pallas kernels for 3% -> 10%
where the time goes in v4:
time: 139 us; the launch traced here: 138 us
  blocking collectives  41.3 us (30%)
  starting transfers between devices  29.5 us (21%)
  waiting for transfers between devices  29.5 us (21%)
  Pallas kernels  19.7 us (14%)
  between operations  14.3 us (10%)
  local copies, waits for them, and re-layouts  2.86 us (2%)
    all_to_all x2, blocking collectives, exchange(): lax.all_to_all(value, 'shard', 0, 0, axis_index_groups=group, tiled=True)  30.2 us
    pallas_call x6, Pallas kernels, run(): pl.pallas_call(kernel, out_shape=out_shape, in_specs=specs, out_specs=out...  19.7 us
    ppermute x2, starting transfers between devices, swap_cores(): return lax.ppermute(value, 'shard', [(s, s ^ 1) for s in range(shards)])  17 us
    all_to_all x1, waiting for transfers between devices, exchange(): lax.all_to_all(value, 'shard', 0, 0, axis_index_groups=group, tiled=True)  11.2 us
    all_to_all x1, blocking collectives, gathered(): return lax.all_to_all(value, 'tensor', 0, 0, tiled=True)  11.1 us
    all_gather x1, waiting for transfers between devices, local(): kept = lax.all_gather(kept, 'shard', axis=0, tiled=False)  10.7 us
    all_to_all x1, starting transfers between devices, exchange(): lax.all_to_all(value, 'shard', 0, 0, axis_index_groups=group, tiled=True)  9.04 us
    all_to_all x1, waiting for transfers between devices, gathered(): return lax.all_to_all(value, 'tensor', 0, 0, tiled=True)  6.06 us
  transfers between devices with their start and end apart: 5, of which 4 were waited for; matrix products, arithmetic and copies ran while one was open for 1% of the time, Pallas kernels for 10%

profile of v4, /device:TPU:1, one launch (start us, length us, event | category | flops | bytes accessed | tf_op | source)
XLA Modules:
  0.0 138.0 jit_solution(13958817138678468354)
XLA Ops:
  7.2 0.1 pad_add_fusion.spot
  7.3 2.0 %shard_map.188 = (f32[1088,128]{1,0:T(8,128)S(1)}, f32[1088,128]{1,0:T(8,128)S(1)}) custom-call(s32[2]{0:T(128)S(1)} %pad_add_fusion.spot, bf16[1024,128]{1,0:T(8,128)(2,1)} %bitcast.27, f32[1024,128]{1,0:T(8,128)} %bitcast.22, bf16[128,1024]{1,0:T(8,128)(2,1)} %bitcast.29, f32[128,1024]{1,0:T(8,128)} %bitcast.24, bf16[1,3584]{1,0:T(2,128)(2,1)} %refs_4_.1, ...), custom_call_target="tpu_custom_call" | custom-call | tf_op jit(solution)/shard_map/pallas_call | solution.py:286
  9.3 8.8 %collective-permute-start = (f32[1088,128]{1,0:T(8,128)S(1)}, f32[1088,128]{1,0:T(8,128)S(1)}, u32[]{:S(2)}, u32[]{:S(2)}) collective-permute-start(f32[1088,128]{1,0:T(8,128)S(1)} %get-tuple-element.25), channel_id=1, source_target_pairs={{0,4},{4,0},{8,12},{12,8},{16,20},{20,16},{24,28},{28,24},{32,36},... | collective-permute-start | bytes 1671176 | tf_op jit(solution)/shard_map/ppermute | solution.py:33
  18.1 1.6 %collective-permute-done = f32[1088,128]{1,0:T(8,128)S(1)} collective-permute-done((f32[1088,128]{1,0:T(8,128)S(1)}, f32[1088,128]{1,0:T(8,128)S(1)}, u32[]{:S(2)}, u32[]{:S(2)}) %collective-permute-start) | collective-permute-done | bytes 557088 | tf_op jit(solution)/shard_map/ppermute | solution.py:33
  19.6 0.1 add.9
  19.7 14.9 %all_to_all.25 = f32[8,136,128]{2,1,0:T(8,128)S(1)} all-to-all(f32[8,136,128]{2,1,0:T(8,128)S(1)} %bitcast.36), channel_id=1, replica_groups={{0,8,16,24,32,40,48,56},{64,72,80,88,96,104,112,120},{128,136,144,152,1..., dimensions={0} | all-to-all | bytes 1114112 | tf_op jit(solution)/shard_map/all_to_all | solution.py:37
  34.6 0.9 broadcast_in_dim.27
  35.4 0.0 copy-start.7
  35.4 0.0 copy-start.10
  35.5 9.0 %all-to-all-start.1 = ((f32[8,136,128]{2,1,0:T(8,128)}), f32[8,136,128]{2,1,0:T(8,128)S(1)}, u32[]{:S(2)}, u32[]{:S(2)}) async-start(f32[8,136,128]{2,1,0:T(8,128)} %broadcast_in_dim.27), calls=%async_computation.1 | async-start | bytes 1114112 | tf_op jit(solution)/shard_map/all_to_all | solution.py:37
  44.5 0.0 copy-start.6
  44.5 0.0 copy-start.11
  44.5 0.0 all-gather.3.cloned.1.call-start
  44.6 0.0 copy-done.7
  44.6 0.0 copy-done.10
  44.6 0.6 copy-done.6
  45.2 0.0 copy-done.11
  45.2 0.6 pad_maximum_fusion.1
  45.8 0.0 all-gather.3.cloned.1.call-update
  45.8 11.2 %all-to-all-done.1 = f32[8,136,128]{2,1,0:T(8,128)S(1)} async-done(((f32[8,136,128]{2,1,0:T(8,128)}), f32[8,136,128]{2,1,0:T(8,128)S(1)}, u32[]{:S(2)}, u32[]{:S(2)}) %all-to-all-start.1) | async-done | bytes 557088 | tf_op jit(solution)/shard_map/all_to_all | solution.py:37
  57.0 0.1 copy.22
  57.2 0.0 copy-start.5
  57.2 0.0 copy-start.8
  57.2 15.4 %all_to_all.26.recv = f32[8,136,128]{2,1,0:T(8,128)S(1)} all-to-all(f32[8,136,128]{2,1,0:T(8,128)S(1)} %broadcast_in_dim.28), channel_id=1, replica_groups={{0,8,16,24,32,40,48,56},{64,72,80,88,96,104,112,120},{128,136,144,152,1..., dimensions={0} | all-to-all | bytes 1114112 | tf_op jit(solution)/shard_map/all_to_all | solution.py:37
  72.6 0.0 copy-done.5
  72.6 0.0 copy-done.8
  72.6 2.9 %shard_map.189 = (f32[4,32,1152]{2,1,0:T(8,128)S(1)}, f32[32,128]{1,0:T(8,128)}) custom-call(s32[2]{0:T(128)S(1)} %pad_add_fusion.spot, f32[8,136,128]{2,1,0:T(8,128)S(1)} %all_to_all.26.recv, f32[32,128]{1,0:T(8,128)S(1)} %bitcast.33, f32[32,1024]{1,0:T(8,128)S(1)} %bitcast.31), custom_call_target="tpu_custom_call" | custom-call | tf_op jit(solution)/shard_map/pallas_call | solution.py:286
  75.5 11.1 %all_to_all.27.got = f32[4,32,1152]{2,1,0:T(8,128)S(1)} all-to-all(f32[4,32,1152]{2,1,0:T(8,128)S(1)} %get-tuple-element.26), channel_id=1, replica_groups=mesh['shard'=128,'tensor'=4] {'tensor'}, dimensions={0} | all-to-all | bytes 1179648 | tf_op jit(solution)/shard_map/all_to_all | solution.py:359
  86.6 6.5 %shard_map.190 = (f32[4,32,1152]{2,1,0:T(8,128)}, f32[32,128]{1,0:T(8,128)S(1)}) custom-call(s32[2]{0:T(128)S(1)} %pad_add_fusion.spot, f32[8,136,128]{2,1,0:T(8,128)S(1)} %all_to_all.26.recv, f32[4,32,1152]{2,1,0:T(8,128)S(1)} %all_to_all.27.got), custom_call_target="tpu_custom_call" | custom-call | tf_op jit(solution)/shard_map/pallas_call | solution.py:286
  93.1 0.0 copy-start.9
  93.1 3.5 %all-to-all-start.4 = ((f32[4,32,1152]{2,1,0:T(8,128)}), f32[4,32,1152]{2,1,0:T(8,128)S(1)}, u32[]{:S(2)}, u32[]{:S(2)}) async-start(f32[4,32,1152]{2,1,0:T(8,128)} %get-tuple-element.27), calls=%async_computation.4 | async-start | bytes 1179648 | tf_op jit(solution)/shard_map/all_to_all | solution.py:359
  96.6 0.0 copy-done.9
  96.6 0.0 copy-start.4
  96.6 1.2 shard_map.191
  97.8 6.1 %all-to-all-done.4.got = f32[4,32,1152]{2,1,0:T(8,128)S(1)} async-done(((f32[4,32,1152]{2,1,0:T(8,128)}), f32[4,32,1152]{2,1,0:T(8,128)S(1)}, u32[]{:S(2)}, u32[]{:S(2)}) %all-to-all-start.4) | async-done | bytes 589856 | tf_op jit(solution)/shard_map/all_to_all | solution.py:359
  103.9 0.0 copy-start
  103.9 0.0 copy-start.1
  103.9 3.9 %shard_map.192.mine = f32[32,1152]{1,0:T(8,128)S(1)} custom-call(s32[2]{0:T(128)S(1)} %pad_add_fusion.spot, f32[8,136,128]{2,1,0:T(8,128)S(1)} %all_to_all.26.recv, f32[4,32,1152]{2,1,0:T(8,128)S(1)} %all-to-all-done.4.got, f32[32,128]{1,0:T(8,128)S(1)} %get-tuple-element.31.narrow), custom_call_target="tpu_custom_call" | custom-call | tf_op jit(solution)/shard_map/pallas_call | solution.py:286
  107.8 8.2 %collective-permute-start.1 = (f32[32,1152]{1,0:T(8,128)S(1)}, f32[32,1152]{1,0:T(8,128)S(1)}, u32[]{:S(2)}, u32[]{:S(2)}) collective-permute-start(f32[32,1152]{1,0:T(8,128)S(1)} %shard_map.192.mine), channel_id=1, source_target_pairs={{0,4},{4,0},{8,12},{12,8},{16,20},{20,16},{24,28},{28,24},{32,36},... | collective-permute-start | bytes 442376 | tf_op jit(solution)/shard_map/ppermute | solution.py:33
  116.0 10.7 %all-gather.3.cloned.1.call-done = f32[2048,128]{1,0:T(8,128)} async-done(((f32[16,128]{1,0:T(8,128)}), f32[2048,128]{1,0:T(8,128)}) %all-gather.3.cloned.1.call-update) | async-done | bytes 1048592 | tf_op jit(solution)/shard_map/all_gather | solution.py:327
  126.7 0.0 collective-permute-done.1.other
  126.7 0.0 copy-done.4
  126.7 0.0 copy-done
  126.7 0.0 copy-done.1
  126.7 0.0 copy-done.3
  126.7 0.0 copy-start.2
  126.7 1.2 copy-done.2
  127.9 3.2 %shard_map.193 = (f32[1024,128]{1,0:T(8,128)}, f32[128,1024]{1,0:T(8,128)}, f32[8,128]{1,0:T(8,128)}, f32[8,128]{1,0:T(8,128)}, f32[1024,128]{1,0:T(8,128)}, /*index=5*/f32[128,1024]{1,0:T(8,128)}) custom-call(s32[2]{0:T(128)S(1)} %pad_add_fusion.spot, f32[32,1152]{1,0:T(8,128)S(1)} %shard_map.192.mine, f32[32,1152]{1,0:T(8,128)S(1)} %collective-permute-done.1.other, ...), custom_call_target="tpu_custom_call" | custom-call | tf_op jit(solution)/shard_map/pallas_call | solution.py:286
  (10 shorter events, 0.1 us)
Async XLA Ops:
  9.3 10.4 %collective-permute-start = (f32[1088,128]{1,0:T(8,128)S(1)}, f32[1088,128]{1,0:T(8,128)S(1)}, u32[]{:S(2)}, u32[]{:S(2)}) collective-permute-start(f32[1088,128]{1,0:T(8,128)S(1)} %get-tuple-element.25), channel_id=1, source_target_pairs={{0,4},{4,0},{8,12},{12,8},{16,20},{20,16},{24,28},{28,24},{32,36},... | collective-permute-start | bytes 1671176 | tf_op jit(solution)/shard_map/ppermute | solution.py:33
  35.4 9.1 %copy-start.7 = (f32[8,128]{1,0:T(8,128)S(1)}, f32[8,128]{1,0:T(8,128)}, u32[]{:S(2)}) copy-start(f32[8,128]{1,0:T(8,128)} %moment_query.1) | copy-start | bytes 12292
  35.4 9.1 %copy-start.10 = (f32[8,128]{1,0:T(8,128)S(1)}, f32[8,128]{1,0:T(8,128)}, u32[]{:S(2)}) copy-start(f32[8,128]{1,0:T(8,128)} %param.19) | copy-start | bytes 12292
  35.5 21.5 %all-to-all-start.1 = ((f32[8,136,128]{2,1,0:T(8,128)}), f32[8,136,128]{2,1,0:T(8,128)S(1)}, u32[]{:S(2)}, u32[]{:S(2)}) async-start(f32[8,136,128]{2,1,0:T(8,128)} %broadcast_in_dim.27), calls=%async_computation.1 | async-start | bytes 1114112 | tf_op jit(solution)/shard_map/all_to_all | solution.py:37
  44.5 0.7 copy-start.6
  44.5 0.7 copy-start.11
  44.5 82.2 %all-gather.3.cloned.1.call-start = ((), (), s32[]{:S(2)}) async-start(), calls=%async_computation.5 | async-start | bytes 1056768 | tf_op jit(solution)/shard_map/all_gather | solution.py:327
  57.2 15.4 %copy-start.5 = (f32[1024,32]{0,1:T(8,128)S(1)}, f32[1024,32]{0,1:T(8,128)}, u32[]{:S(2)}) copy-start(f32[1024,32]{0,1:T(8,128)} %param.18) | copy-start | bytes 393220
  57.2 15.4 %copy-start.8 = (f32[128,32]{0,1:T(8,128)S(1)}, f32[128,32]{0,1:T(8,128)}, u32[]{:S(2)}) copy-start(f32[128,32]{0,1:T(8,128)} %param.17) | copy-start | bytes 49156
  93.1 3.5 %copy-start.9 = (f32[28]{0:T(128)S(1)}, f32[28]{0:T(128)}, u32[]{:S(2)}) copy-start(f32[28]{0:T(128)} %param.24) | copy-start | bytes 340
  93.1 10.7 %all-to-all-start.4 = ((f32[4,32,1152]{2,1,0:T(8,128)}), f32[4,32,1152]{2,1,0:T(8,128)S(1)}, u32[]{:S(2)}, u32[]{:S(2)}) async-start(f32[4,32,1152]{2,1,0:T(8,128)} %get-tuple-element.27), calls=%async_computation.4 | async-start | bytes 1179648 | tf_op jit(solution)/shard_map/all_to_all | solution.py:359
  96.6 30.1 %copy-start.4 = (bf16[1,128,1024]{2,1,0:T(8,128)(2,1)S(1)}, bf16[1,128,1024]{2,1,0:T(8,128)(2,1)}, u32[]{:S(2)}) copy-start(bf16[1,128,1024]{2,1,0:T(8,128)(2,1)} %param.15) | copy-start | bytes 786436
  103.9 22.8 %copy-start = (f32[1,1024,128]{2,1,0:T(8,128)S(1)}, f32[1,1024,128]{2,1,0:T(8,128)}, u32[]{:S(2)}) copy-start(f32[1,1024,128]{2,1,0:T(8,128)} %param.14) | copy-start | bytes 1572868
  103.9 22.8 %copy-start.1 = (f32[1,128,1024]{2,1,0:T(8,128)S(1)}, f32[1,128,1024]{2,1,0:T(8,128)}, u32[]{:S(2)}) copy-start(f32[1,128,1024]{2,1,0:T(8,128)} %param.16) | copy-start | bytes 1572868
  103.9 22.8 %copy-start.3 = (bf16[1,1024,128]{2,1,0:T(8,128)(2,1)S(1)}, bf16[1,1024,128]{2,1,0:T(8,128)(2,1)}, u32[]{:S(2)}) copy-start(bf16[1,1024,128]{2,1,0:T(8,128)(2,1)} %param.13) | copy-start | bytes 786436
  107.8 18.9 %collective-permute-start.1 = (f32[32,1152]{1,0:T(8,128)S(1)}, f32[32,1152]{1,0:T(8,128)S(1)}, u32[]{:S(2)}, u32[]{:S(2)}) collective-permute-start(f32[32,1152]{1,0:T(8,128)S(1)} %shard_map.192.mine), channel_id=1, source_target_pairs={{0,4},{4,0},{8,12},{12,8},{16,20},{20,16},{24,28},{28,24},{32,36},... | collective-permute-start | bytes 442376 | tf_op jit(solution)/shard_map/ppermute | solution.py:33
  126.7 1.2 copy-start.2
Sparse Core Ops, SparseCore 0:
  48.9 77.6 all-gather.2

commit v5 on v4

--- a/solution.py
+++ b/solution.py
@@ -77,13 +77,21 @@
     return pltpu.roll(jnp.concatenate(done), half, 1)
 
 
-def send_partials(narrow, recv, stage, sent, sems, block):
+def partials_of(narrow, recv, block, refs):
     ring = recv.shape[0]
     rank = narrow.shape[0]
-    stage[:, ring * block:] = jnp.zeros((rank, LANES), jnp.float32)
-    stage[:, ring * block:ring * block + rank] = dot(narrow, narrow, ((1,), (1,)))
+    square = dot(narrow, narrow, ((1,), (1,)))
+    for ref in refs:
+        ref[:, ring * block:] = jnp.zeros((rank, LANES), jnp.float32)
+        ref[:, ring * block:ring * block + rank] = square
     for j in range(ring):
-        stage[:, j * block:(j + 1) * block] = dot(narrow, recv[j, :block], ((1,), (1,)))
+        part = dot(narrow, recv[j, :block], ((1,), (1,)))
+        for ref in refs:
+            ref[:, j * block:(j + 1) * block] = part
+
+
+def send_partials(narrow, recv, stage, sent, sems, block):
+    partials_of(narrow, recv, block, [stage])
     copies = [pltpu.make_async_copy(stage, sent.at[peer], sems.at[peer]) for peer in range(sent.shape[0])]
     for copy in copies:
         copy.start()
@@ -111,7 +119,7 @@
     return sum(dot(wide[:, j * block:(j + 1) * block], recv[j, :block], ((1,), (0,))) for j in range(recv.shape[0]))
 
 
-def first_kernel(block, spot, recv, start_query, start_output, sent, narrow, stage, sems):
+def first_kernel(block, spot, recv, start_query, start_output, sent, narrow, gram):
     @pl.when(spot[1] == 0)
     def _():
         narrow[...] = start_query[...]
@@ -120,7 +128,7 @@
     def _():
         narrow[...] = times_matrix(start_output[...], recv, block)
 
-    send_partials(narrow[...], recv, stage, sent, sems, block)
+    partials_of(narrow[...], recv, block, [sent.at[peer] for peer in range(sent.shape[0])])
 
 
 def middle_kernel(block, spot, recv, got, sent, narrow, gram, stage, sems):
@@ -145,7 +153,7 @@
 
 
 def final_kernel(
-    block, shards, spot, mine, other, kept, grad_query, error_query, grad_output, error_output,
+    block, shards, spot, mine, other, kept_mine, kept_other, grad_query, error_query, grad_output, error_output,
     moment_query, moment_output, new_error_query, new_error_output, new_moment_query, new_moment_output,
     new_weight_query, new_weight_output, error_q, error_o, weight_q, weight_o, sems,
 ):
@@ -164,18 +172,17 @@
             pltpu.make_async_copy(weight_o.at[:, down], new_weight_output.at[:, down], sems.at[3, j]),
         )
 
-    def body(query, output):
+    def body(query, output, kept_query, kept_output):
         right = query[:, height:] * scale
         left = output[:, height:] * scale
         for j in range(ring):
             down = slice(j * block, (j + 1) * block)
-            old = kept[j * block // rows:(j + 1) * block // rows]
             approx = dot(query[:, down], right, ((0,), (0,)))
             error_q[down] = grad_query[down].astype(jnp.float32) + error_query[down] - approx
-            weight_q[down] = old[:, :rows].reshape(block, width) - 0.01 * approx
+            weight_q[down] = kept_query[down] - 0.01 * approx
             approx = dot(left, output[:, down], ((0,), (0,)))
             error_o[:, down] = grad_output[:, down].astype(jnp.float32) + error_output[:, down] - approx
-            weight_o[:, down] = old[:, rows:].reshape(block, width).T - 0.01 * approx
+            weight_o[:, down] = kept_output[down] - 0.01 * approx
             for copy in copies(j):
                 copy.start()
         along = index * rows
@@ -187,33 +194,43 @@
 
     @pl.when(spot[1] == 0)
     def _():
-        body(mine, other)
+        body(mine, other, kept_mine, kept_other)
 
     @pl.when(spot[1] == 1)
     def _():
-        body(other, mine)
+        body(other, mine, kept_other, kept_mine)
 
     for j in range(ring):
         for copy in copies(j):
             copy.wait()
 
 
-def prelude_kernel(
-    ring, per, slot, vec, spot, *refs
-):
-    far, (mine, sent), near, (line, sems) = refs[:7], refs[7:9], refs[9:16], refs[16:]
+def prelude_kernel(ring, per, slot, vec, spot, *refs):
+    far, total, near, (line, sems) = refs[:11], refs[11], refs[12:23], refs[23:]
     moves = [pltpu.make_async_copy(*pair, sems.at[n]) for n, pair in enumerate(zip(far, near))]
-    for move in moves:
-        move.start()
-    grad_q, error_q, grad_o, error_o, grad_vector, weight_vector, moment_vector = near
+    grad_q, error_q, grad_o, error_o, grad_vector, weight_query, moment_query, weight_output, moment_output = near[:9]
+    weight_vector, moment_vector = near[9:]
     height, width = grad_q.shape
     block = height // ring
     tall = block + slot
+    rows = weight_query.shape[0]
     small = weight_vector.shape[1]
-    index, odd = spot[0], spot[1]
+    index, which = spot[0], spot[1]
+
+    @pl.when(which == 0)
+    def _():
+        moves[0].start()
+        moves[1].start()
+
+    @pl.when(which == 1)
+    def _():
+        moves[2].start()
+        moves[3].start()
+
+    for move in moves[4:]:
+        move.start()
     for move in moves[4:]:
         move.wait()
-
     line[...] = jnp.zeros_like(line)
     line[0:1, :small] = weight_vector[...] - 0.009 * moment_vector[...]
     first = index * small
@@ -223,35 +240,30 @@
     for j in range(ring):
         after = LANES * (per * j + sub - per) + lane - first
         inside = (sub >= per) & (sub < 2 * per) & (after >= 0) & (after < small)
-        value = jnp.where(inside, spread, 0.0)
-        for ref in (mine, sent):
-            ref[j * tall + block:(j + 1) * tall] = value
+        total[j * tall + block:(j + 1) * tall] = jnp.where(inside, spread, 0.0)
         for n in range(per):
             r = per * j + n
             if r * LANES < vec:
                 row = grad_vector[:, r * LANES:(r + 1) * LANES].astype(jnp.float32)
-                for ref in (mine, sent):
-                    ref[j * tall + block + n:j * tall + block + n + 1] = row
-
-    def totals(query, output):
+                total[j * tall + block + n:j * tall + block + n + 1] = row
+
+    @pl.when(which == 0)
+    def _():
+        total[ring * tall:] = weight_query[...] - 0.009 * moment_query[...]
         moves[0].wait()
         moves[1].wait()
         for j in range(ring):
             down = slice(j * block, (j + 1) * block)
-            query[j * tall:j * tall + block] = grad_q[down].astype(jnp.float32) + error_q[down]
+            total[j * tall:j * tall + block] = grad_q[down].astype(jnp.float32) + error_q[down]
+
+    @pl.when(which == 1)
+    def _():
+        total[ring * tall:] = weight_output[...] - 0.009 * moment_output[...]
         moves[2].wait()
         moves[3].wait()
         for j in range(ring):
             down = slice(j * block, (j + 1) * block)
-            output[j * tall:j * tall + block] = grad_o[:, down].astype(jnp.float32) + error_o[:, down]
-
-    @pl.when(odd == 0)
-    def _():
-        totals(mine, sent)
-
-    @pl.when(odd == 1)
-    def _():
-        totals(sent, mine)
+            total[j * tall:j * tall + block] = grad_o[:, down].astype(jnp.float32) + error_o[:, down]
 
 
 def vector_kernel(block, per, shards, spot, recv, moment_vector, new_moment, new_weight, mean, kept):
@@ -323,34 +335,35 @@
     tall = block + slot
     assert width == LANES and rows * shards == height and small * shards == vec and lines * LANES == vec
 
-    kept = jnp.concatenate([weight_query - 0.009 * moment_query, (weight_output - 0.009 * moment_output).T])
-    kept = lax.all_gather(kept, "shard", axis=0, tiled=False)
-
     spot = jnp.stack([index, 1 - index % 2]).astype(jnp.int32)
     given = (
-        grad_query[0], error_query[0], grad_output[0], error_output[0], grad_vector, weight_vector[None],
-        moment_vector[None],
+        grad_query[0], error_query[0], grad_output[0], error_output[0], grad_vector, weight_query, moment_query,
+        weight_output.T, moment_output.T, weight_vector[None], moment_vector[None],
     )
     given = [pltpu.with_memory_space_constraint(value, pltpu.HBM) for value in given]
-    mine, sent = run(
-        functools.partial(prelude_kernel, ring, per, slot, vec), (spot, *given),
-        (shape(ring * tall, LANES), shape(ring * tall, LANES)),
-        [
-            *(pltpu.VMEM(value.shape, value.dtype) for value in given),
-            pltpu.VMEM((8, LANES), jnp.float32), pltpu.SemaphoreType.DMA((len(given),)),
-        ],
-        outside=len(given),
-    )
-    summed = (mine + swap_cores(sent, shards)).reshape(ring, tall, LANES)
+
+    def prelude(spot):
+        return run(
+            functools.partial(prelude_kernel, ring, per, slot, vec), (spot, *given), shape(ring * tall + rows, LANES),
+            [
+                *(pltpu.VMEM(value.shape, value.dtype) for value in given),
+                pltpu.VMEM((8, LANES), jnp.float32), pltpu.SemaphoreType.DMA((len(given),)),
+            ],
+            outside=len(given),
+        )
+
+    got = swap_cores(prelude(jnp.stack([index, index % 2]).astype(jnp.int32)), shards)
+    mine = prelude(spot)
+    summed = (mine[:ring * tall] + got[:ring * tall]).reshape(ring, tall, LANES)
+    own_kept, got_kept = mine[ring * tall:], got[ring * tall:]
+    pair_kept = jnp.where(asks, jnp.concatenate([got_kept, own_kept]), jnp.concatenate([own_kept, got_kept]))
+
     part = exchange(summed, first).sum(0)
-    whole = share(part, second, ring).sum(0)
+    every = share(jnp.concatenate([part, pair_kept]), second, ring)
+    whole = every[:, :tall].sum(0)
     square = jnp.where(asks, whole[:block], whole[:block].T)
-    every = share(jnp.concatenate([square, whole[block:]]), first, ring)
-    new_moment_vector, new_weight_vector = run(
-        functools.partial(vector_kernel, block, per, shards), (spot, every, moment_vector[None]),
-        (shape(1, small), shape(lines, LANES)),
-        [pltpu.VMEM((per * ring + 8, LANES), jnp.float32), pltpu.VMEM((per * ring, LANES), jnp.float32)],
-    )
+    kept_rows = every[:, tall:].reshape(block, LANES)
+    every = share(jnp.concatenate([square, whole[block:], kept_rows]), first, ring)
 
     gram = pltpu.VMEM((rank, LANES), jnp.float32)
     partials = shape(tensors, rank, height + LANES)
@@ -362,13 +375,24 @@
     outside, within = pl.BlockSpec(memory_space=pl.ANY), pl.BlockSpec(memory_space=pltpu.VMEM)
     sent, narrow = run(
         functools.partial(first_kernel, block), (spot, every, start_query.T, start_output.T),
-        (partials, shape(rank, width)), stage, (outside, within),
+        (partials, shape(rank, width)), [gram],
     )
     for turn in range(ROUNDS - 1):
         sent, narrow = run(
             functools.partial(middle_kernel, block), (spot, every, gathered(sent)), (partials, shape(rank, width)),
             [gram, *stage], (outside, within),
         )
+
+    sent, every = lax.optimization_barrier((sent, every))
+    kept_all = every[:, tall:].reshape(ring, ring, 2 * rows, LANES)
+    kept_turned = kept_all.transpose(1, 0, 2, 3).reshape(ring, block, LANES).transpose(0, 2, 1)
+    kept_all = jnp.where(asks, kept_all.reshape(ring, block, LANES), kept_turned).reshape(height, LANES)
+    kept_other = swap_cores(kept_all, shards)
+    new_moment_vector, new_weight_vector = run(
+        functools.partial(vector_kernel, block, per, shards), (spot, every, moment_vector[None]),
+        (shape(1, small), shape(lines, LANES)),
+        [pltpu.VMEM((per * ring + 8, LANES), jnp.float32), pltpu.VMEM((per * ring, LANES), jnp.float32)],
+    )
     got, new_moment_vector, new_weight_vector = lax.optimization_barrier(
         (gathered(sent), new_moment_vector, new_weight_vector)
     )
@@ -380,7 +404,7 @@
     ) = run(
         functools.partial(final_kernel, block, shards),
         (
-            spot, mine, other, kept, grad_query[0], error_query[0], grad_output[0], error_output[0],
+            spot, mine, other, kept_all, kept_other, grad_query[0], error_query[0], grad_output[0], error_output[0],
             moment_query, moment_output.T,
         ),
         (shape(height, width), shape(width, height), shape(rows, width), shape(rows, width), shape(height, width), shape(width, height)),

time: 139 us -> 119 us (0.86)
  waiting for transfers between devices: 29.5 us -> 13.3 us
  between operations: 14.3 us -> 0.95 us
  blocking collectives: 41.3 us -> 52.9 us
  local copies, waits for them, and re-layouts: 2.86 us -> 0.54 us
    all_to_all x2, blocking collectives: 30.2 us -> 41.8 us  [exchange(): lax.all_to_all(value, 'shard', 0, 0, axis_index_groups=group, tiled=True)]
    all_gather x1 -> x0, waiting for transfers between devices: 10.7 us -> none  [local(): kept = lax.all_gather(kept, 'shard', axis=0, tiled=False)]
    all_to_all x1, waiting for transfers between devices: 6.06 us -> 0.01 us  [gathered(): return lax.all_to_all(value, 'tensor', 0, 0, tiled=True)]
    all_to_all x1, starting transfers between devices: 9.04 us -> 3.54 us  [exchange(): lax.all_to_all(value, 'shard', 0, 0, axis_index_groups=group, tiled=True)]
    ppermute x2 -> x3, starting transfers between devices: 17 us -> 21.7 us  [swap_cores(): return lax.ppermute(value, 'shard', [(s, s ^ 1) for s in range(shards)])]
    unnamed x24 -> x18, local copies, waits for them, and re-layouts: 1.87 us -> 0.05 us
    pallas_call x6 -> x7, Pallas kernels: 19.7 us -> 20.6 us  [run(): pl.pallas_call(kernel, out_shape=out_shape, in_specs=specs, out_specs=out...]
  transfers between devices with their start and end apart: 5 -> 5, of which waited for: 4 -> 2; matrix products, arithmetic and copies ran while one was open for 1% -> 1% of each run, Pallas kernels for 10% -> 6%
where the time goes in v5:
time: 119 us
  blocking collectives  52.9 us (44%)
  starting transfers between devices  28.7 us (24%)
  Pallas kernels  20.6 us (17%)
  waiting for transfers between devices  13.3 us (11%)
  other arithmetic  1.99 us (2%)
    all_to_all x2, blocking collectives, exchange(): lax.all_to_all(value, 'shard', 0, 0, axis_index_groups=group, tiled=True)  41.8 us
    ppermute x3, starting transfers between devices, swap_cores(): return lax.ppermute(value, 'shard', [(s, s ^ 1) for s in range(shards)])  21.7 us
    pallas_call x7, Pallas kernels, run(): pl.pallas_call(kernel, out_shape=out_shape, in_specs=specs, out_specs=out...  20.6 us
    all_to_all x1, waiting for transfers between devices, exchange(): lax.all_to_all(value, 'shard', 0, 0, axis_index_groups=group, tiled=True)  12.4 us
    all_to_all x1, blocking collectives, gathered(): return lax.all_to_all(value, 'tensor', 0, 0, tiled=True)  11.1 us
    all_to_all x1, starting transfers between devices, exchange(): lax.all_to_all(value, 'shard', 0, 0, axis_index_groups=group, tiled=True)  3.54 us
    all_to_all x1, starting transfers between devices, gathered(): return lax.all_to_all(value, 'tensor', 0, 0, tiled=True)  3.49 us
  transfers between devices with their start and end apart: 5, of which 2 were waited for; matrix products, arithmetic and copies ran while one was open for 1% of the time, Pallas kernels for 6%

profile of v5, /device:TPU:1, one launch (start us, length us, event | category | flops | bytes accessed | tf_op | source)
XLA Modules:
  0.0 119.0 jit_solution(9887099768871193999)
XLA Ops:
  0.6 0.1 pad_add_fusion.1.spot
  0.7 1.8 %shard_map.189 = f32[1096,128]{1,0:T(8,128)S(1)} custom-call(s32[2]{0:T(128)S(1)} %pad_add_fusion.1.spot, bf16[1024,128]{1,0:T(8,128)(2,1)} %bitcast.35, f32[1024,128]{1,0:T(8,128)} %bitcast.29, bf16[128,1024]{1,0:T(8,128)(2,1)} %bitcast.38, f32[128,1024]{1,0:T(8,128)} %bitcast.32, bf16[1,3584]{1,0:T(2,128)(2,1)} %refs_4_.3, f32[8,128]{1,0:T(8,128)} %refs_5_.3, ...), custom_call_target="tpu_custom_call" | custom-call | tf_op jit(solution)/shard_map/pallas_call | solution.py:298
  2.5 8.8 %collective-permute-start = (f32[1096,128]{1,0:T(8,128)S(1)}, f32[1096,128]{1,0:T(8,128)S(1)}, u32[]{:S(2)}, u32[]{:S(2)}) collective-permute-start(f32[1096,128]{1,0:T(8,128)S(1)} %shard_map.189), channel_id=1, source_target_pairs={{0,4},{4,0},{8,12},{12,8},{16,20},{20,16},{24,28},{28,24},{32,36},... | collective-permute-start | bytes 1683464 | tf_op jit(solution)/shard_map/ppermute | solution.py:33
  11.3 0.1 pad_add_fusion.spot
  11.4 1.8 %shard_map.188 = f32[1096,128]{1,0:T(8,128)S(1)} custom-call(s32[2]{0:T(128)S(1)} %pad_add_fusion.spot, bf16[1024,128]{1,0:T(8,128)(2,1)} %bitcast.36, f32[1024,128]{1,0:T(8,128)} %bitcast.30, bf16[128,1024]{1,0:T(8,128)(2,1)} %bitcast.39, f32[128,1024]{1,0:T(8,128)} %bitcast.33, bf16[1,3584]{1,0:T(2,128)(2,1)} %refs_4_.3, f32[8,128]{1,0:T(8,128)} %refs_5_.3, ...), custom_call_target="tpu_custom_call" | custom-call | tf_op jit(solution)/shard_map/pallas_call | solution.py:298
  13.2 0.0 collective-permute-done
  13.2 0.9 slice_add_fusion
  14.1 3.5 %all-to-all-start = ((f32[8,136,128]{2,1,0:T(8,128)}), f32[8,136,128]{2,1,0:T(8,128)S(1)}, u32[]{:S(2)}, u32[]{:S(2)}) async-start(f32[8,136,128]{2,1,0:T(8,128)} %bitcast.11), calls=%async_computation | async-start | bytes 1114112 | tf_op jit(solution)/shard_map/all_to_all | solution.py:37
  17.7 12.4 %all-to-all-done = f32[8,136,128]{2,1,0:T(8,128)S(1)} async-done(((f32[8,136,128]{2,1,0:T(8,128)}), f32[8,136,128]{2,1,0:T(8,128)S(1)}, u32[]{:S(2)}, u32[]{:S(2)}) %all-to-all-start) | async-done | bytes 557088 | tf_op jit(solution)/shard_map/all_to_all | solution.py:37
  30.2 21.0 %all_to_all.25 = f32[8,152,128]{2,1,0:T(8,128)S(1)} all-to-all(f32[8,152,128]{2,1,0:T(8,128)S(1)} %broadcast_in_dim.27), channel_id=1, replica_groups={{0,64,128,192,256,320,384,448},{8,72,136,200,264,328,392,456},{16,80,14..., dimensions={0} | all-to-all | bytes 1245184 | tf_op jit(solution)/shard_map/all_to_all | solution.py:37
  51.2 0.1 copy.23
  51.4 0.1 broadcast_in_dim.28
  51.5 0.0 copy-start.4
  51.5 0.0 copy-start.7
  51.5 20.8 %all_to_all.26.recv = f32[8,264,128]{2,1,0:T(8,128)S(1)} all-to-all(f32[8,264,128]{2,1,0:T(8,128)S(1)} %broadcast_in_dim.28), channel_id=1, replica_groups={{0,8,16,24,32,40,48,56},{64,72,80,88,96,104,112,120},{128,136,144,152,1..., dimensions={0} | all-to-all | bytes 2162688 | tf_op jit(solution)/shard_map/all_to_all | solution.py:37
  72.3 0.0 copy-done.4
  72.3 0.0 copy-done.7
  72.3 1.5 %shard_map.190 = (f32[4,32,1152]{2,1,0:T(8,128)S(1)}, f32[32,128]{1,0:T(8,128)}) custom-call(s32[2]{0:T(128)S(1)} %pad_add_fusion.spot, f32[8,264,128]{2,1,0:T(8,128)S(1)} %all_to_all.26.recv, f32[32,128]{1,0:T(8,128)S(1)} %bitcast.45, f32[32,1024]{1,0:T(8,128)S(1)} %bitcast.41), custom_call_target="tpu_custom_call" | custom-call | tf_op jit(solution)/shard_map/pallas_call | solution.py:298
  73.8 11.1 %all_to_all.27.got = f32[4,32,1152]{2,1,0:T(8,128)S(1)} all-to-all(f32[4,32,1152]{2,1,0:T(8,128)S(1)} %get-tuple-element.24), channel_id=1, replica_groups=mesh['shard'=128,'tensor'=4] {'tensor'}, dimensions={0} | all-to-all | bytes 1179648 | tf_op jit(solution)/shard_map/all_to_all | solution.py:372
  84.9 6.5 %shard_map.191 = (f32[4,32,1152]{2,1,0:T(8,128)}, f32[32,128]{1,0:T(8,128)S(1)}) custom-call(s32[2]{0:T(128)S(1)} %pad_add_fusion.spot, f32[8,264,128]{2,1,0:T(8,128)S(1)} %all_to_all.26.recv, f32[4,32,1152]{2,1,0:T(8,128)S(1)} %all_to_all.27.got), custom_call_target="tpu_custom_call" | custom-call | tf_op jit(solution)/shard_map/pallas_call | solution.py:298
  91.3 3.5 %all-to-all-start.4 = ((f32[4,32,1152]{2,1,0:T(8,128)}), f32[4,32,1152]{2,1,0:T(8,128)S(1)}, u32[]{:S(2)}, u32[]{:S(2)}) async-start(f32[4,32,1152]{2,1,0:T(8,128)} %get-tuple-element.27), calls=%async_computation.4 | async-start | bytes 1179648 | tf_op jit(solution)/shard_map/all_to_all | solution.py:372
  94.9 0.0 copy-start.8
  94.9 0.2 copy.25
  95.2 0.9 bitcast_select_fusion
  96.0 7.5 %collective-permute-start.2 = (f32[1024,128]{1,0:T(8,128)}, f32[1024,128]{1,0:T(8,128)}, u32[]{:S(2)}, u32[]{:S(2)}) collective-permute-start(f32[1024,128]{1,0:T(8,128)} %bitcast.20.kept_mine), channel_id=1, source_target_pairs={{0,4},{4,0},{8,12},{12,8},{16,20},{20,16},{24,28},{28,24},{32,36},... | collective-permute-start | bytes 1572872 | tf_op jit(solution)/shard_map/ppermute | solution.py:33
  103.6 0.0 copy-done.8
  103.6 1.2 shard_map.192
  104.7 0.0 copy-start
  104.7 0.0 copy-start.1
  104.7 0.0 copy-start.2
  104.7 0.0 copy-start.3
  104.7 0.0 copy-start.5
  104.8 0.0 copy-start.6
  104.8 0.0 all-to-all-done.4.got
  104.8 4.0 %shard_map.193.mine = f32[32,1152]{1,0:T(8,128)S(1)} custom-call(s32[2]{0:T(128)S(1)} %pad_add_fusion.spot, f32[8,264,128]{2,1,0:T(8,128)S(1)} %all_to_all.26.recv, f32[4,32,1152]{2,1,0:T(8,128)S(1)} %all-to-all-done.4.got, f32[32,128]{1,0:T(8,128)S(1)} %get-tuple-element.31.narrow), custom_call_target="tpu_custom_call" | custom-call | tf_op jit(solution)/shard_map/pallas_call | solution.py:298
  108.7 5.4 %collective-permute-start.1 = (f32[32,1152]{1,0:T(8,128)S(1)}, f32[32,1152]{1,0:T(8,128)S(1)}, u32[]{:S(2)}, u32[]{:S(2)}) collective-permute-start(f32[32,1152]{1,0:T(8,128)S(1)} %shard_map.193.mine), channel_id=1, source_target_pairs={{0,4},{4,0},{8,12},{12,8},{16,20},{20,16},{24,28},{28,24},{32,36},... | collective-permute-start | bytes 442376 | tf_op jit(solution)/shard_map/ppermute | solution.py:33
  114.1 0.0 collective-permute-done.2.kept_other
  114.1 1.0 collective-permute-done.1.other
  115.1 0.0 copy-done
  115.1 0.0 copy-done.1
  115.1 0.0 copy-done.2
  115.1 0.0 copy-done.3
  115.1 0.0 copy-done.5
  115.1 0.0 copy-done.6
  115.1 3.9 %shard_map.194 = (f32[1024,128]{1,0:T(8,128)}, f32[128,1024]{1,0:T(8,128)}, f32[8,128]{1,0:T(8,128)}, f32[8,128]{1,0:T(8,128)}, f32[1024,128]{1,0:T(8,128)}, /*index=5*/f32[128,1024]{1,0:T(8,128)}) custom-call(s32[2]{0:T(128)S(1)} %pad_add_fusion.spot, f32[32,1152]{1,0:T(8,128)S(1)} %shard_map.193.mine, f32[32,1152]{1,0:T(8,128)S(1)} %collective-permute-done.1.other, ...), custom_call_target="tpu_custom_call" | custom-call | tf_op jit(solution)/shard_map/pallas_call | solution.py:298
  (14 shorter events, 0.2 us)
Async XLA Ops:
  2.5 10.7 %collective-permute-start = (f32[1096,128]{1,0:T(8,128)S(1)}, f32[1096,128]{1,0:T(8,128)S(1)}, u32[]{:S(2)}, u32[]{:S(2)}) collective-permute-start(f32[1096,128]{1,0:T(8,128)S(1)} %shard_map.189), channel_id=1, source_target_pairs={{0,4},{4,0},{8,12},{12,8},{16,20},{20,16},{24,28},{28,24},{32,36},... | collective-permute-start | bytes 1683464 | tf_op jit(solution)/shard_map/ppermute | solution.py:33
  14.1 15.9 %all-to-all-start = ((f32[8,136,128]{2,1,0:T(8,128)}), f32[8,136,128]{2,1,0:T(8,128)S(1)}, u32[]{:S(2)}, u32[]{:S(2)}) async-start(f32[8,136,128]{2,1,0:T(8,128)} %bitcast.11), calls=%async_computation | async-start | bytes 1114112 | tf_op jit(solution)/shard_map/all_to_all | solution.py:37
  51.5 20.8 %copy-start.4 = (f32[1024,32]{0,1:T(8,128)S(1)}, f32[1024,32]{0,1:T(8,128)}, u32[]{:S(2)}) copy-start(f32[1024,32]{0,1:T(8,128)} %param.18) | copy-start | bytes 393220
  51.5 20.8 %copy-start.7 = (f32[128,32]{0,1:T(8,128)S(1)}, f32[128,32]{0,1:T(8,128)}, u32[]{:S(2)}) copy-start(f32[128,32]{0,1:T(8,128)} %param.17) | copy-start | bytes 49156
  91.3 13.4 %all-to-all-start.4 = ((f32[4,32,1152]{2,1,0:T(8,128)}), f32[4,32,1152]{2,1,0:T(8,128)S(1)}, u32[]{:S(2)}, u32[]{:S(2)}) async-start(f32[4,32,1152]{2,1,0:T(8,128)} %get-tuple-element.27), calls=%async_computation.4 | async-start | bytes 1179648 | tf_op jit(solution)/shard_map/all_to_all | solution.py:372
  94.9 8.6 %copy-start.8 = (f32[28]{0:T(128)S(1)}, f32[28]{0:T(128)}, u32[]{:S(2)}) copy-start(f32[28]{0:T(128)} %param.24) | copy-start | bytes 340
  96.0 18.1 %collective-permute-start.2 = (f32[1024,128]{1,0:T(8,128)}, f32[1024,128]{1,0:T(8,128)}, u32[]{:S(2)}, u32[]{:S(2)}) collective-permute-start(f32[1024,128]{1,0:T(8,128)} %bitcast.20.kept_mine), channel_id=1, source_target_pairs={{0,4},{4,0},{8,12},{12,8},{16,20},{20,16},{24,28},{28,24},{32,36},... | collective-permute-start | bytes 1572872 | tf_op jit(solution)/shard_map/ppermute | solution.py:33
  104.7 10.4 %copy-start = (f32[1,1024,128]{2,1,0:T(8,128)S(1)}, f32[1,1024,128]{2,1,0:T(8,128)}, u32[]{:S(2)}) copy-start(f32[1,1024,128]{2,1,0:T(8,128)} %param.14) | copy-start | bytes 1572868
  104.7 10.4 %copy-start.1 = (f32[1,128,1024]{2,1,0:T(8,128)S(1)}, f32[1,128,1024]{2,1,0:T(8,128)}, u32[]{:S(2)}) copy-start(f32[1,128,1024]{2,1,0:T(8,128)} %param.16) | copy-start | bytes 1572868
  104.7 10.4 %copy-start.2 = (bf16[1,1024,128]{2,1,0:T(8,128)(2,1)S(1)}, bf16[1,1024,128]{2,1,0:T(8,128)(2,1)}, u32[]{:S(2)}) copy-start(bf16[1,1024,128]{2,1,0:T(8,128)(2,1)} %param.13) | copy-start | bytes 786436
  104.7 10.4 %copy-start.3 = (bf16[1,128,1024]{2,1,0:T(8,128)(2,1)S(1)}, bf16[1,128,1024]{2,1,0:T(8,128)(2,1)}, u32[]{:S(2)}) copy-start(bf16[1,128,1024]{2,1,0:T(8,128)(2,1)} %param.15) | copy-start | bytes 786436
  104.7 10.4 %copy-start.5 = (f32[8,128]{1,0:T(8,128)S(1)}, f32[8,128]{1,0:T(8,128)}, u32[]{:S(2)}) copy-start(f32[8,128]{1,0:T(8,128)} %moment_query.1) | copy-start | bytes 12292
  104.8 10.4 %copy-start.6 = (f32[128,8]{0,1:T(8,128)S(1)}, f32[128,8]{0,1:T(8,128)}, u32[]{:S(2)}) copy-start(f32[128,8]{0,1:T(8,128)} %param.22) | copy-start | bytes 12292
  108.7 6.4 %collective-permute-start.1 = (f32[32,1152]{1,0:T(8,128)S(1)}, f32[32,1152]{1,0:T(8,128)S(1)}, u32[]{:S(2)}, u32[]{:S(2)}) collective-permute-start(f32[32,1152]{1,0:T(8,128)S(1)} %shard_map.193.mine), channel_id=1, source_target_pairs={{0,4},{4,0},{8,12},{12,8},{16,20},{20,16},{24,28},{28,24},{32,36},... | collective-permute-start | bytes 442376 | tf_op jit(solution)/shard_map/ppermute | solution.py:33

commit v6 on v5

--- a/solution.py
+++ b/solution.py
@@ -90,16 +90,7 @@
             ref[:, j * block:(j + 1) * block] = part
 
 
-def send_partials(narrow, recv, stage, sent, sems, block):
-    partials_of(narrow, recv, block, [stage])
-    copies = [pltpu.make_async_copy(stage, sent.at[peer], sems.at[peer]) for peer in range(sent.shape[0])]
-    for copy in copies:
-        copy.start()
-    for copy in copies:
-        copy.wait()
-
-
-def normalized(spot, got, gram, block, ring):
+def totals_of(spot, got, gram, block, ring):
     rank = got.shape[1]
     total = got[0]
     for copy in range(1, got.shape[0]):
@@ -111,8 +102,7 @@
     def _():
         gram[:, :rank] = dot(wide, wide, ((1,), (1,)))
 
-    inverse = invert_lower(gram[...])[:, :rank]
-    return inverse, dot(inverse, wide, ((1,), (0,)))
+    return wide
 
 
 def times_matrix(wide, recv, block):
@@ -132,30 +122,47 @@
 
 
 def middle_kernel(block, spot, recv, got, sent, narrow, gram, stage, sems):
-    _, wide = normalized(spot, got, gram, block, recv.shape[0])
-    value = times_matrix(wide, recv, block)
+    ring = recv.shape[0]
+    rank = got.shape[1]
+    wide = totals_of(spot, got, gram, block, ring)
+    plain = times_matrix(wide, recv, block)
+    onward = [dot(plain, recv[j, :block], ((1,), (1,))) for j in range(ring)]
+    inverse = invert_lower(gram[...])[:, :rank]
+    value = dot(inverse, plain, ((1,), (0,)))
     narrow[...] = value
-    send_partials(value, recv, stage, sent, sems, block)
+    half = ring // 2 * block
+    parts = slice(0, half), slice(half, stage.shape[1])
+    copies = [
+        pltpu.make_async_copy(stage.at[:, part], sent.at[peer, :, part], sems.at[n, peer])
+        for n, part in enumerate(parts) for peer in range(sent.shape[0])
+    ]
+    peers = sent.shape[0]
+    stage[:, parts[0]] = dot(inverse, jnp.concatenate(onward[:ring // 2], axis=1), ((1,), (0,)))
+    for copy in copies[:peers]:
+        copy.start()
+    stage[:, half:ring * block] = dot(inverse, jnp.concatenate(onward[ring // 2:], axis=1), ((1,), (0,)))
+    stage[:, ring * block:] = jnp.zeros((rank, LANES), jnp.float32)
+    stage[:, ring * block:ring * block + rank] = dot(value, value, ((1,), (1,)))
+    for copy in copies[peers:]:
+        copy.start()
+    for copy in copies:
+        copy.wait()
 
 
 def last_kernel(block, spot, recv, got, narrow, factors, gram):
     ring = recv.shape[0]
-    inverse, wide = normalized(spot, got, gram, block, ring)
-    factors[:, :ring * block] = wide
-
-    @pl.when(spot[1] == 0)
-    def _():
-        factors[:, ring * block:] = times_matrix(wide, recv, block)
-
-    @pl.when(spot[1] == 1)
-    def _():
-        factors[:, ring * block:] = dot(inverse, narrow[...], ((1,), (0,)))
+    rank = got.shape[1]
+    wide = totals_of(spot, got, gram, block, ring)
+    plain = jnp.where(spot[1] == 0, times_matrix(wide, recv, block), narrow[...])
+    inverse = invert_lower(gram[...])[:, :rank]
+    factors[:, :ring * block] = dot(inverse, wide, ((1,), (0,)))
+    factors[:, ring * block:] = dot(inverse, plain, ((1,), (0,)))
 
 
 def final_kernel(
-    block, shards, spot, mine, other, kept_mine, kept_other, grad_query, error_query, grad_output, error_output,
+    block, shards, spot, kept_mine, kept_other, mine, other, grad_query, error_query, grad_output, error_output,
     moment_query, moment_output, new_error_query, new_error_output, new_moment_query, new_moment_output,
-    new_weight_query, new_weight_output, error_q, error_o, weight_q, weight_o, sems,
+    new_weight_query, new_weight_output, error_q, error_o, weight_q, weight_o, kept, sems,
 ):
     height, width = error_query.shape
     rows = moment_query.shape[0]
@@ -167,10 +174,16 @@
         down = pl.ds(j * block, block)
         return (
             pltpu.make_async_copy(error_q.at[down], new_error_query.at[down], sems.at[0, j]),
-            pltpu.make_async_copy(weight_q.at[down], new_weight_query.at[down], sems.at[1, j]),
-            pltpu.make_async_copy(error_o.at[:, down], new_error_output.at[:, down], sems.at[2, j]),
+            pltpu.make_async_copy(error_o.at[:, down], new_error_output.at[:, down], sems.at[1, j]),
+            pltpu.make_async_copy(weight_q.at[down], new_weight_query.at[down], sems.at[2, j]),
             pltpu.make_async_copy(weight_o.at[:, down], new_weight_output.at[:, down], sems.at[3, j]),
         )
+
+    loads = [
+        pltpu.make_async_copy(source, kept.at[n], sems.at[4, n]) for n, source in enumerate((kept_mine, kept_other))
+    ]
+    for load in loads:
+        load.start()
 
     def body(query, output, kept_query, kept_output):
         right = query[:, height:] * scale
@@ -179,11 +192,19 @@
             down = slice(j * block, (j + 1) * block)
             approx = dot(query[:, down], right, ((0,), (0,)))
             error_q[down] = grad_query[down].astype(jnp.float32) + error_query[down] - approx
-            weight_q[down] = kept_query[down] - 0.01 * approx
+            weight_q[down] = -0.01 * approx
             approx = dot(left, output[:, down], ((0,), (0,)))
             error_o[:, down] = grad_output[:, down].astype(jnp.float32) + error_output[:, down] - approx
-            weight_o[:, down] = kept_output[down] - 0.01 * approx
-            for copy in copies(j):
+            weight_o[:, down] = -0.01 * approx
+            for copy in copies(j)[:2]:
+                copy.start()
+        for load in loads:
+            load.wait()
+        for j in range(ring):
+            down = slice(j * block, (j + 1) * block)
+            weight_q[down] = kept[kept_query, down] + weight_q[down]
+            weight_o[:, down] = kept[kept_output, down] + weight_o[:, down]
+            for copy in copies(j)[2:]:
                 copy.start()
         along = index * rows
         base = pl.multiple_of(along // LANES * LANES, LANES)
@@ -194,11 +215,11 @@
 
     @pl.when(spot[1] == 0)
     def _():
-        body(mine, other, kept_mine, kept_other)
+        body(mine, other, 0, 1)
 
     @pl.when(spot[1] == 1)
     def _():
-        body(other, mine, kept_other, kept_mine)
+        body(other, mine, 1, 0)
 
     for j in range(ring):
         for copy in copies(j):
@@ -371,7 +392,7 @@
     def gathered(value):
         return lax.all_to_all(value, "tensor", 0, 0, tiled=True)
 
-    stage = [pltpu.VMEM((rank, height + LANES), jnp.float32), pltpu.SemaphoreType.DMA((tensors,))]
+    stage = [pltpu.VMEM((rank, height + LANES), jnp.float32), pltpu.SemaphoreType.DMA((2, tensors))]
     outside, within = pl.BlockSpec(memory_space=pl.ANY), pl.BlockSpec(memory_space=pltpu.VMEM)
     sent, narrow = run(
         functools.partial(first_kernel, block), (spot, every, start_query.T, start_output.T),
@@ -404,12 +425,12 @@
     ) = run(
         functools.partial(final_kernel, block, shards),
         (
-            spot, mine, other, kept_all, kept_other, grad_query[0], error_query[0], grad_output[0], error_output[0],
+            spot, kept_all, kept_other, mine, other, grad_query[0], error_query[0], grad_output[0], error_output[0],
             moment_query, moment_output.T,
         ),
         (shape(height, width), shape(width, height), shape(rows, width), shape(rows, width), shape(height, width), shape(width, height)),
-        [big[0], big[1], big[0], big[1], pltpu.SemaphoreType.DMA((4, ring))],
-        (outside, outside, within, within, outside, outside),
+        [big[0], big[1], big[0], big[1], pltpu.VMEM((2, height, width), jnp.float32), pltpu.SemaphoreType.DMA((5, ring))],
+        (outside, outside, within, within, outside, outside), 2,
     )
     new_error_query = new_error_query[None]
     new_error_output = new_error_output[None]

time: 119 us -> 117 us (0.983)
  Pallas kernels: 20.6 us -> 18.1 us
    pallas_call x7, Pallas kernels: 20.6 us -> 18.1 us  [run(): pl.pallas_call(kernel, out_shape=out_shape, in_specs=specs, out_specs=out...]
where the time goes in v6:
time: 117 us
  blocking collectives  52.9 us (45%)
  starting transfers between devices  29.1 us (25%)
  Pallas kernels  18.1 us (15%)
  waiting for transfers between devices  13.3 us (11%)
  other arithmetic  1.99 us (2%)
    all_to_all x2, blocking collectives, exchange(): lax.all_to_all(value, 'shard', 0, 0, axis_index_groups=group, tiled=True)  41.8 us
    ppermute x3, starting transfers between devices, swap_cores(): return lax.ppermute(value, 'shard', [(s, s ^ 1) for s in range(shards)])  22.1 us
    pallas_call x7, Pallas kernels, run(): pl.pallas_call(kernel, out_shape=out_shape, in_specs=specs, out_specs=out...  18.1 us
    all_to_all x1, waiting for transfers between devices, exchange(): lax.all_to_all(value, 'shard', 0, 0, axis_index_groups=group, tiled=True)  12.4 us
    all_to_all x1, blocking collectives, gathered(): return lax.all_to_all(value, 'tensor', 0, 0, tiled=True)  11.1 us
    all_to_all x1, starting transfers between devices, exchange(): lax.all_to_all(value, 'shard', 0, 0, axis_index_groups=group, tiled=True)  3.54 us
    all_to_all x1, starting transfers between devices, gathered(): return lax.all_to_all(value, 'tensor', 0, 0, tiled=True)  3.49 us
  transfers between devices with their start and end apart: 5, of which 2 were waited for; matrix products, arithmetic and copies ran while one was open for 1% of the time, Pallas kernels for 6%

profile of v6, /device:TPU:1, one launch (start us, length us, event | category | flops | bytes accessed | tf_op | source)
XLA Modules:
  0.0 117.0 jit_solution(13381445069488186291)
XLA Ops:
  0.6 0.1 pad_add_fusion.1.spot
  0.7 1.8 %shard_map.189 = f32[1096,128]{1,0:T(8,128)S(1)} custom-call(s32[2]{0:T(128)S(1)} %pad_add_fusion.1.spot, bf16[1024,128]{1,0:T(8,128)(2,1)} %bitcast.35, f32[1024,128]{1,0:T(8,128)} %bitcast.29, bf16[128,1024]{1,0:T(8,128)(2,1)} %bitcast.38, f32[128,1024]{1,0:T(8,128)} %bitcast.32, bf16[1,3584]{1,0:T(2,128)(2,1)} %refs_4_.3, f32[8,128]{1,0:T(8,128)} %refs_5_.3, ...), custom_call_target="tpu_custom_call" | custom-call | tf_op jit(solution)/shard_map/pallas_call | solution.py:319
  2.5 8.8 %collective-permute-start = (f32[1096,128]{1,0:T(8,128)S(1)}, f32[1096,128]{1,0:T(8,128)S(1)}, u32[]{:S(2)}, u32[]{:S(2)}) collective-permute-start(f32[1096,128]{1,0:T(8,128)S(1)} %shard_map.189), channel_id=1, source_target_pairs={{0,4},{4,0},{8,12},{12,8},{16,20},{20,16},{24,28},{28,24},{32,36},... | collective-permute-start | bytes 1683464 | tf_op jit(solution)/shard_map/ppermute | solution.py:33
  11.3 0.1 pad_add_fusion.spot
  11.4 1.8 %shard_map.188 = f32[1096,128]{1,0:T(8,128)S(1)} custom-call(s32[2]{0:T(128)S(1)} %pad_add_fusion.spot, bf16[1024,128]{1,0:T(8,128)(2,1)} %bitcast.36, f32[1024,128]{1,0:T(8,128)} %bitcast.30, bf16[128,1024]{1,0:T(8,128)(2,1)} %bitcast.39, f32[128,1024]{1,0:T(8,128)} %bitcast.33, bf16[1,3584]{1,0:T(2,128)(2,1)} %refs_4_.3, f32[8,128]{1,0:T(8,128)} %refs_5_.3, ...), custom_call_target="tpu_custom_call" | custom-call | tf_op jit(solution)/shard_map/pallas_call | solution.py:319
  13.2 0.0 collective-permute-done
  13.2 0.9 slice_add_fusion
  14.1 3.5 %all-to-all-start = ((f32[8,136,128]{2,1,0:T(8,128)}), f32[8,136,128]{2,1,0:T(8,128)S(1)}, u32[]{:S(2)}, u32[]{:S(2)}) async-start(f32[8,136,128]{2,1,0:T(8,128)} %bitcast.11), calls=%async_computation | async-start | bytes 1114112 | tf_op jit(solution)/shard_map/all_to_all | solution.py:37
  17.7 12.4 %all-to-all-done = f32[8,136,128]{2,1,0:T(8,128)S(1)} async-done(((f32[8,136,128]{2,1,0:T(8,128)}), f32[8,136,128]{2,1,0:T(8,128)S(1)}, u32[]{:S(2)}, u32[]{:S(2)}) %all-to-all-start) | async-done | bytes 557088 | tf_op jit(solution)/shard_map/all_to_all | solution.py:37
  30.2 21.0 %all_to_all.25 = f32[8,152,128]{2,1,0:T(8,128)S(1)} all-to-all(f32[8,152,128]{2,1,0:T(8,128)S(1)} %broadcast_in_dim.27), channel_id=1, replica_groups={{0,64,128,192,256,320,384,448},{8,72,136,200,264,328,392,456},{16,80,14..., dimensions={0} | all-to-all | bytes 1245184 | tf_op jit(solution)/shard_map/all_to_all | solution.py:37
  51.2 0.1 copy.23
  51.4 0.1 broadcast_in_dim.28
  51.5 0.0 copy-start.4
  51.5 0.0 copy-start.7
  51.5 20.8 %all_to_all.26.recv = f32[8,264,128]{2,1,0:T(8,128)S(1)} all-to-all(f32[8,264,128]{2,1,0:T(8,128)S(1)} %broadcast_in_dim.28), channel_id=1, replica_groups={{0,8,16,24,32,40,48,56},{64,72,80,88,96,104,112,120},{128,136,144,152,1..., dimensions={0} | all-to-all | bytes 2162688 | tf_op jit(solution)/shard_map/all_to_all | solution.py:37
  72.3 0.0 copy-done.4
  72.3 0.0 copy-done.7
  72.3 1.5 %shard_map.190 = (f32[4,32,1152]{2,1,0:T(8,128)S(1)}, f32[32,128]{1,0:T(8,128)}) custom-call(s32[2]{0:T(128)S(1)} %pad_add_fusion.spot, f32[8,264,128]{2,1,0:T(8,128)S(1)} %all_to_all.26.recv, f32[32,128]{1,0:T(8,128)S(1)} %bitcast.45, f32[32,1024]{1,0:T(8,128)S(1)} %bitcast.41), custom_call_target="tpu_custom_call" | custom-call | tf_op jit(solution)/shard_map/pallas_call | solution.py:319
  73.8 11.1 %all_to_all.27.got = f32[4,32,1152]{2,1,0:T(8,128)S(1)} all-to-all(f32[4,32,1152]{2,1,0:T(8,128)S(1)} %get-tuple-element.24), channel_id=1, replica_groups=mesh['shard'=128,'tensor'=4] {'tensor'}, dimensions={0} | all-to-all | bytes 1179648 | tf_op jit(solution)/shard_map/all_to_all | solution.py:393
  84.9 4.4 %shard_map.191 = (f32[4,32,1152]{2,1,0:T(8,128)}, f32[32,128]{1,0:T(8,128)S(1)}) custom-call(s32[2]{0:T(128)S(1)} %pad_add_fusion.spot, f32[8,264,128]{2,1,0:T(8,128)S(1)} %all_to_all.26.recv, f32[4,32,1152]{2,1,0:T(8,128)S(1)} %all_to_all.27.got), custom_call_target="tpu_custom_call" | custom-call | tf_op jit(solution)/shard_map/pallas_call | solution.py:319
  89.3 3.5 %all-to-all-start.4 = ((f32[4,32,1152]{2,1,0:T(8,128)}), f32[4,32,1152]{2,1,0:T(8,128)S(1)}, u32[]{:S(2)}, u32[]{:S(2)}) async-start(f32[4,32,1152]{2,1,0:T(8,128)} %get-tuple-element.27), calls=%async_computation.4 | async-start | bytes 1179648 | tf_op jit(solution)/shard_map/all_to_all | solution.py:393
  92.8 0.0 copy-start.8
  92.9 0.2 copy.25
  93.1 0.9 bitcast_select_fusion
  93.9 7.5 %collective-permute-start.1 = (f32[1024,128]{1,0:T(8,128)}, f32[1024,128]{1,0:T(8,128)}, u32[]{:S(2)}, u32[]{:S(2)}) collective-permute-start(f32[1024,128]{1,0:T(8,128)} %bitcast.20.kept_mine), channel_id=1, source_target_pairs={{0,4},{4,0},{8,12},{12,8},{16,20},{20,16},{24,28},{28,24},{32,36},... | collective-permute-start | bytes 1572872 | tf_op jit(solution)/shard_map/ppermute | solution.py:33
  101.5 0.0 copy-done.8
  101.5 1.2 shard_map.192
  102.6 0.0 copy-start
  102.6 0.0 copy-start.1
  102.6 0.0 copy-start.2
  102.6 0.0 copy-start.3
  102.7 0.0 copy-start.5
  102.7 0.0 copy-start.6
  102.7 0.0 all-to-all-done.4.got
  102.7 3.5 %shard_map.193.mine = f32[32,1152]{1,0:T(8,128)S(1)} custom-call(s32[2]{0:T(128)S(1)} %pad_add_fusion.spot, f32[8,264,128]{2,1,0:T(8,128)S(1)} %all_to_all.26.recv, f32[4,32,1152]{2,1,0:T(8,128)S(1)} %all-to-all-done.4.got, f32[32,128]{1,0:T(8,128)S(1)} %get-tuple-element.31.narrow), custom_call_target="tpu_custom_call" | custom-call | tf_op jit(solution)/shard_map/pallas_call | solution.py:319
  106.2 5.8 %collective-permute-start.2 = (f32[32,1152]{1,0:T(8,128)S(1)}, f32[32,1152]{1,0:T(8,128)S(1)}, u32[]{:S(2)}, u32[]{:S(2)}) collective-permute-start(f32[32,1152]{1,0:T(8,128)S(1)} %shard_map.193.mine), channel_id=1, source_target_pairs={{0,4},{4,0},{8,12},{12,8},{16,20},{20,16},{24,28},{28,24},{32,36},... | collective-permute-start | bytes 442376 | tf_op jit(solution)/shard_map/ppermute | solution.py:33
  112.0 0.0 collective-permute-done.1.kept_other
  112.0 1.0 collective-permute-done.2.other
  113.0 0.0 copy-done
  113.0 0.0 copy-done.1
  113.0 0.0 copy-done.2
  113.0 0.0 copy-done.3
  113.0 0.0 copy-done.5
  113.0 0.0 copy-done.6
  113.0 3.9 %shard_map.194 = (f32[1024,128]{1,0:T(8,128)}, f32[128,1024]{1,0:T(8,128)}, f32[8,128]{1,0:T(8,128)}, f32[8,128]{1,0:T(8,128)}, f32[1024,128]{1,0:T(8,128)}, /*index=5*/f32[128,1024]{1,0:T(8,128)}) custom-call(s32[2]{0:T(128)S(1)} %pad_add_fusion.spot, f32[1024,128]{1,0:T(8,128)} %bitcast.20.kept_mine, f32[1024,128]{1,0:T(8,128)} %collective-permute-done.1.kept_other, ...), custom_call_target="tpu_custom_call" | custom-call | tf_op jit(solution)/shard_map/pallas_call | solution.py:319
  (14 shorter events, 0.2 us)
Async XLA Ops:
  2.5 10.7 %collective-permute-start = (f32[1096,128]{1,0:T(8,128)S(1)}, f32[1096,128]{1,0:T(8,128)S(1)}, u32[]{:S(2)}, u32[]{:S(2)}) collective-permute-start(f32[1096,128]{1,0:T(8,128)S(1)} %shard_map.189), channel_id=1, source_target_pairs={{0,4},{4,0},{8,12},{12,8},{16,20},{20,16},{24,28},{28,24},{32,36},... | collective-permute-start | bytes 1683464 | tf_op jit(solution)/shard_map/ppermute | solution.py:33
  14.1 15.9 %all-to-all-start = ((f32[8,136,128]{2,1,0:T(8,128)}), f32[8,136,128]{2,1,0:T(8,128)S(1)}, u32[]{:S(2)}, u32[]{:S(2)}) async-start(f32[8,136,128]{2,1,0:T(8,128)} %bitcast.11), calls=%async_computation | async-start | bytes 1114112 | tf_op jit(solution)/shard_map/all_to_all | solution.py:37
  51.5 20.8 %copy-start.4 = (f32[1024,32]{0,1:T(8,128)S(1)}, f32[1024,32]{0,1:T(8,128)}, u32[]{:S(2)}) copy-start(f32[1024,32]{0,1:T(8,128)} %param.18) | copy-start | bytes 393220
  51.5 20.8 %copy-start.7 = (f32[128,32]{0,1:T(8,128)S(1)}, f32[128,32]{0,1:T(8,128)}, u32[]{:S(2)}) copy-start(f32[128,32]{0,1:T(8,128)} %param.17) | copy-start | bytes 49156
  89.3 13.4 %all-to-all-start.4 = ((f32[4,32,1152]{2,1,0:T(8,128)}), f32[4,32,1152]{2,1,0:T(8,128)S(1)}, u32[]{:S(2)}, u32[]{:S(2)}) async-start(f32[4,32,1152]{2,1,0:T(8,128)} %get-tuple-element.27), calls=%async_computation.4 | async-start | bytes 1179648 | tf_op jit(solution)/shard_map/all_to_all | solution.py:393
  92.8 8.6 %copy-start.8 = (f32[28]{0:T(128)S(1)}, f32[28]{0:T(128)}, u32[]{:S(2)}) copy-start(f32[28]{0:T(128)} %param.24) | copy-start | bytes 340
  93.9 18.1 %collective-permute-start.1 = (f32[1024,128]{1,0:T(8,128)}, f32[1024,128]{1,0:T(8,128)}, u32[]{:S(2)}, u32[]{:S(2)}) collective-permute-start(f32[1024,128]{1,0:T(8,128)} %bitcast.20.kept_mine), channel_id=1, source_target_pairs={{0,4},{4,0},{8,12},{12,8},{16,20},{20,16},{24,28},{28,24},{32,36},... | collective-permute-start | bytes 1572872 | tf_op jit(solution)/shard_map/ppermute | solution.py:33
  102.6 10.3 %copy-start = (f32[1,1024,128]{2,1,0:T(8,128)S(1)}, f32[1,1024,128]{2,1,0:T(8,128)}, u32[]{:S(2)}) copy-start(f32[1,1024,128]{2,1,0:T(8,128)} %param.14) | copy-start | bytes 1572868
  102.6 10.3 %copy-start.1 = (f32[1,128,1024]{2,1,0:T(8,128)S(1)}, f32[1,128,1024]{2,1,0:T(8,128)}, u32[]{:S(2)}) copy-start(f32[1,128,1024]{2,1,0:T(8,128)} %param.16) | copy-start | bytes 1572868
  102.6 10.3 %copy-start.2 = (bf16[1,1024,128]{2,1,0:T(8,128)(2,1)S(1)}, bf16[1,1024,128]{2,1,0:T(8,128)(2,1)}, u32[]{:S(2)}) copy-start(bf16[1,1024,128]{2,1,0:T(8,128)(2,1)} %param.13) | copy-start | bytes 786436
  102.6 10.3 %copy-start.3 = (bf16[1,128,1024]{2,1,0:T(8,128)(2,1)S(1)}, bf16[1,128,1024]{2,1,0:T(8,128)(2,1)}, u32[]{:S(2)}) copy-start(bf16[1,128,1024]{2,1,0:T(8,128)(2,1)} %param.15) | copy-start | bytes 786436
  102.7 10.3 %copy-start.5 = (f32[8,128]{1,0:T(8,128)S(1)}, f32[8,128]{1,0:T(8,128)}, u32[]{:S(2)}) copy-start(f32[8,128]{1,0:T(8,128)} %moment_query.1) | copy-start | bytes 12292
  102.7 10.3 %copy-start.6 = (f32[128,8]{0,1:T(8,128)S(1)}, f32[128,8]{0,1:T(8,128)}, u32[]{:S(2)}) copy-start(f32[128,8]{0,1:T(8,128)} %param.22) | copy-start | bytes 12292
  106.2 6.8 %collective-permute-start.2 = (f32[32,1152]{1,0:T(8,128)S(1)}, f32[32,1152]{1,0:T(8,128)S(1)}, u32[]{:S(2)}, u32[]{:S(2)}) collective-permute-start(f32[32,1152]{1,0:T(8,128)S(1)} %shard_map.193.mine), channel_id=1, source_target_pairs={{0,4},{4,0},{8,12},{12,8},{16,20},{20,16},{24,28},{28,24},{32,36},... | collective-permute-start | bytes 442376 | tf_op jit(solution)/shard_map/ppermute | solution.py:33

commit v7 on v6

--- a/solution.py
+++ b/solution.py
@@ -85,7 +85,7 @@
         ref[:, ring * block:] = jnp.zeros((rank, LANES), jnp.float32)
         ref[:, ring * block:ring * block + rank] = square
     for j in range(ring):
-        part = dot(narrow, recv[j, :block], ((1,), (1,)))
+        part = dot(recv[j, :block], narrow, ((1,), (1,))).T
         for ref in refs:
             ref[:, j * block:(j + 1) * block] = part
 
@@ -106,7 +106,7 @@
 
 
 def times_matrix(wide, recv, block):
-    return sum(dot(wide[:, j * block:(j + 1) * block], recv[j, :block], ((1,), (0,))) for j in range(recv.shape[0]))
+    return dot(wide, recv[:, :block].reshape(-1, block), ((1,), (0,)))
 
 
 def first_kernel(block, spot, recv, start_query, start_output, sent, narrow, gram):
@@ -159,70 +159,67 @@
     factors[:, ring * block:] = dot(inverse, plain, ((1,), (0,)))
 
 
-def final_kernel(
-    block, shards, spot, kept_mine, kept_other, mine, other, grad_query, error_query, grad_output, error_output,
-    moment_query, moment_output, new_error_query, new_error_output, new_moment_query, new_moment_output,
-    new_weight_query, new_weight_output, error_q, error_o, weight_q, weight_o, kept, sems,
-):
+def final_kernel(block, shards, earlier, spot, *refs):
+    refs = refs[earlier:]
+    old, factors, grad_query, error_query, grad_output, error_output, moment_query, moment_output = refs[:8]
+    (new_error_query, new_error_output, new_moment_query, new_moment_output, new_weight_query, new_weight_output) = refs[8:14]
+    error_q, error_o, weight_q, weight_o, moment, kept, sems = refs[14:]
     height, width = error_query.shape
     rows = moment_query.shape[0]
+    ring = height // block
     scale = 1.0 / shards
-    ring = height // block
-    index = spot[0]
-
-    def copies(j):
+    load = pltpu.make_async_copy(old, kept, sems.at[2, 0])
+    load.start()
+    along = spot[0] * rows
+    base = pl.multiple_of(along // LANES * LANES, LANES)
+    picked = pltpu.roll(factors[:, pl.ds(base, LANES)], (LANES - along % LANES) % LANES, 1)
+    narrow = factors[:, height:] * scale
+    change = dot(picked, narrow, ((0,), (0,)))[:rows]
+
+    def parts(j):
         down = pl.ds(j * block, block)
-        return (
-            pltpu.make_async_copy(error_q.at[down], new_error_query.at[down], sems.at[0, j]),
-            pltpu.make_async_copy(error_o.at[:, down], new_error_output.at[:, down], sems.at[1, j]),
-            pltpu.make_async_copy(weight_q.at[down], new_weight_query.at[down], sems.at[2, j]),
-            pltpu.make_async_copy(weight_o.at[:, down], new_weight_output.at[:, down], sems.at[3, j]),
-        )
-
-    loads = [
-        pltpu.make_async_copy(source, kept.at[n], sems.at[4, n]) for n, source in enumerate((kept_mine, kept_other))
-    ]
-    for load in loads:
-        load.start()
-
-    def body(query, output, kept_query, kept_output):
-        right = query[:, height:] * scale
-        left = output[:, height:] * scale
-        for j in range(ring):
-            down = slice(j * block, (j + 1) * block)
-            approx = dot(query[:, down], right, ((0,), (0,)))
+        return down, slice(j * block, (j + 1) * block)
+
+    @pl.when(spot[1] == 0)
+    def _():
+        moment[...] = 0.9 * moment_query[...] + change
+        copies = [pltpu.make_async_copy(moment, new_moment_query, sems.at[2, 1])]
+        copies[0].start()
+        for j in range(ring):
+            at, down = parts(j)
+            approx = dot(factors[:, down], narrow, ((0,), (0,)))
             error_q[down] = grad_query[down].astype(jnp.float32) + error_query[down] - approx
             weight_q[down] = -0.01 * approx
-            approx = dot(left, output[:, down], ((0,), (0,)))
+            copies.append(pltpu.make_async_copy(error_q.at[at], new_error_query.at[at], sems.at[0, j]))
+            copies[-1].start()
+        load.wait()
+        for j in range(ring):
+            at, down = parts(j)
+            weight_q[down] = kept[down] + weight_q[down]
+            copies.append(pltpu.make_async_copy(weight_q.at[at], new_weight_query.at[at], sems.at[1, j]))
+            copies[-1].start()
+        for copy in copies:
+            copy.wait()
+
+    @pl.when(spot[1] == 1)
+    def _():
+        moment[...] = 0.9 * moment_output[...] + change
+        copies = [pltpu.make_async_copy(moment, new_moment_output, sems.at[2, 1])]
+        copies[0].start()
+        for j in range(ring):
+            at, down = parts(j)
+            approx = dot(narrow, factors[:, down], ((0,), (0,)))
             error_o[:, down] = grad_output[:, down].astype(jnp.float32) + error_output[:, down] - approx
             weight_o[:, down] = -0.01 * approx
-            for copy in copies(j)[:2]:
-                copy.start()
-        for load in loads:
-            load.wait()
-        for j in range(ring):
-            down = slice(j * block, (j + 1) * block)
-            weight_q[down] = kept[kept_query, down] + weight_q[down]
-            weight_o[:, down] = kept[kept_output, down] + weight_o[:, down]
-            for copy in copies(j)[2:]:
-                copy.start()
-        along = index * rows
-        base = pl.multiple_of(along // LANES * LANES, LANES)
-        picked = pltpu.roll(query[:, pl.ds(base, LANES)], (LANES - along % LANES) % LANES, 1)
-        new_moment_query[...] = 0.9 * moment_query[...] + dot(picked, right, ((0,), (0,)))[:rows]
-        picked = pltpu.roll(output[:, pl.ds(base, LANES)], (LANES - along % LANES) % LANES, 1)
-        new_moment_output[...] = 0.9 * moment_output[...] + dot(picked, left, ((0,), (0,)))[:rows]
-
-    @pl.when(spot[1] == 0)
-    def _():
-        body(mine, other, 0, 1)
-
-    @pl.when(spot[1] == 1)
-    def _():
-        body(other, mine, 1, 0)
-
-    for j in range(ring):
-        for copy in copies(j):
+            copies.append(pltpu.make_async_copy(error_o.at[:, at], new_error_output.at[:, at], sems.at[0, j]))
+            copies[-1].start()
+        load.wait()
+        for j in range(ring):
+            at, down = parts(j)
+            weight_o[:, down] = kept[down] + weight_o[:, down]
+            copies.append(pltpu.make_async_copy(weight_o.at[:, at], new_weight_output.at[:, at], sems.at[1, j]))
+            copies[-1].start()
+        for copy in copies:
             copy.wait()
 
 
@@ -373,7 +370,8 @@
             outside=len(given),
         )
 
-    got = swap_cores(prelude(jnp.stack([index, index % 2]).astype(jnp.int32)), shards)
+    swapped = jnp.stack([index, index % 2]).astype(jnp.int32)
+    got = swap_cores(prelude(swapped), shards)
     mine = prelude(spot)
     summed = (mine[:ring * tall] + got[:ring * tall]).reshape(ring, tall, LANES)
     own_kept, got_kept = mine[ring * tall:], got[ring * tall:]
@@ -420,18 +418,20 @@
     mine = run(functools.partial(last_kernel, block), (spot, every, got, narrow), shape(rank, height + width), [gram])
     other = swap_cores(mine, shards)
     big = [pltpu.VMEM((height, width), jnp.float32), pltpu.VMEM((width, height), jnp.float32)]
+    ends = (shape(height, width), shape(width, height), shape(rows, width), shape(rows, width), shape(height, width), shape(width, height))
+    local_ones = (grad_query[0], error_query[0], grad_output[0], error_output[0], moment_query, moment_output.T)
+
+    def final(spot, before, kept, factors):
+        return run(
+            functools.partial(final_kernel, block, shards, len(before)), (spot, *before, kept, factors, *local_ones), ends,
+            [*big, *big, pltpu.VMEM((rows, width), jnp.float32), big[0], pltpu.SemaphoreType.DMA((3, ring))],
+            (outside,) * 6, len(before) + 1, input_output_aliases={n + 1: n for n in range(len(before))},
+        )
+
+    ends_of_mine = final(spot, (), kept_all, mine)
     (
         new_error_query, new_error_output, new_moment_query, new_moment_output, new_weight_query, new_weight_output,
-    ) = run(
-        functools.partial(final_kernel, block, shards),
-        (
-            spot, kept_all, kept_other, mine, other, grad_query[0], error_query[0], grad_output[0], error_output[0],
-            moment_query, moment_output.T,
-        ),
-        (shape(height, width), shape(width, height), shape(rows, width), shape(rows, width), shape(height, width), shape(width, height)),
-        [big[0], big[1], big[0], big[1], pltpu.VMEM((2, height, width), jnp.float32), pltpu.SemaphoreType.DMA((5, ring))],
-        (outside, outside, within, within, outside, outside), 2,
-    )
+    ) = final(swapped, ends_of_mine, kept_other, other)
     new_error_query = new_error_query[None]
     new_error_output = new_error_output[None]
     new_moment_output = new_moment_output.T

time: 117 us -> 117 us (level)
    pallas_call x7 -> x8, Pallas kernels: 18.1 us -> 19 us  [run(): pl.pallas_call(kernel, out_shape=out_shape, in_specs=specs, out_specs=out...]
  transfers between devices with their start and end apart: 5 -> 5, of which waited for: 2 -> 1; matrix products, arithmetic and copies ran while one was open for 1% -> 1% of each run, Pallas kernels for 6% -> 8%
where the time goes in v7:
time: 117 us
  blocking collectives  52.9 us (45%)
  starting transfers between devices  28.9 us (25%)
  Pallas kernels  19 us (16%)
  waiting for transfers between devices  12.4 us (11%)
  other arithmetic  1.98 us (2%)
    all_to_all x2, blocking collectives, exchange(): lax.all_to_all(value, 'shard', 0, 0, axis_index_groups=group, tiled=True)  41.8 us
    ppermute x3, starting transfers between devices, swap_cores(): return lax.ppermute(value, 'shard', [(s, s ^ 1) for s in range(shards)])  21.9 us
    pallas_call x8, Pallas kernels, run(): pl.pallas_call(kernel, out_shape=out_shape, in_specs=specs, out_specs=out...  19 us
    all_to_all x1, waiting for transfers between devices, exchange(): lax.all_to_all(value, 'shard', 0, 0, axis_index_groups=group, tiled=True)  12.4 us
    all_to_all x1, blocking collectives, gathered(): return lax.all_to_all(value, 'tensor', 0, 0, tiled=True)  11.1 us
    all_to_all x1, starting transfers between devices, exchange(): lax.all_to_all(value, 'shard', 0, 0, axis_index_groups=group, tiled=True)  3.54 us
    all_to_all x1, starting transfers between devices, gathered(): return lax.all_to_all(value, 'tensor', 0, 0, tiled=True)  3.49 us
  transfers between devices with their start and end apart: 5, of which 1 were waited for; matrix products, arithmetic and copies ran while one was open for 1% of the time, Pallas kernels for 8%

profile of v7, /device:TPU:1, one launch (start us, length us, event | category | flops | bytes accessed | tf_op | source)
XLA Modules:
  0.0 116.6 jit_solution(2223997026489611476)
XLA Ops:
  0.6 0.1 pad_add_fusion.spot
  0.7 1.8 %shard_map.189 = f32[1096,128]{1,0:T(8,128)S(1)} custom-call(s32[2]{0:T(128)S(1)} %pad_add_fusion.spot, bf16[1024,128]{1,0:T(8,128)(2,1)} %bitcast.37, f32[1024,128]{1,0:T(8,128)} %bitcast.29, bf16[128,1024]{1,0:T(8,128)(2,1)} %bitcast.41, f32[128,1024]{1,0:T(8,128)} %bitcast.33, bf16[1,3584]{1,0:T(2,128)(2,1)} %refs_4_.3, f32[8,128]{1,0:T(8,128)} %refs_5_.3, ...), custom_call_target="tpu_custom_call" | custom-call | tf_op jit(solution)/shard_map/pallas_call | solution.py:316
  2.5 8.8 %collective-permute-start = (f32[1096,128]{1,0:T(8,128)S(1)}, f32[1096,128]{1,0:T(8,128)S(1)}, u32[]{:S(2)}, u32[]{:S(2)}) collective-permute-start(f32[1096,128]{1,0:T(8,128)S(1)} %shard_map.189), channel_id=1, source_target_pairs={{0,4},{4,0},{8,12},{12,8},{16,20},{20,16},{24,28},{28,24},{32,36},... | collective-permute-start | bytes 1683464 | tf_op jit(solution)/shard_map/ppermute | solution.py:33
  11.3 0.1 pad_add_fusion.1.spot
  11.4 1.8 %shard_map.188 = f32[1096,128]{1,0:T(8,128)S(1)} custom-call(s32[2]{0:T(128)S(1)} %pad_add_fusion.1.spot, bf16[1024,128]{1,0:T(8,128)(2,1)} %bitcast.38, f32[1024,128]{1,0:T(8,128)} %bitcast.30, bf16[128,1024]{1,0:T(8,128)(2,1)} %bitcast.42, f32[128,1024]{1,0:T(8,128)} %bitcast.34, bf16[1,3584]{1,0:T(2,128)(2,1)} %refs_4_.3, f32[8,128]{1,0:T(8,128)} %refs_5_.3, ...), custom_call_target="tpu_custom_call" | custom-call | tf_op jit(solution)/shard_map/pallas_call | solution.py:316
  13.2 0.0 collective-permute-done
  13.2 0.9 slice_add_fusion
  14.1 3.5 %all-to-all-start = ((f32[8,136,128]{2,1,0:T(8,128)}), f32[8,136,128]{2,1,0:T(8,128)S(1)}, u32[]{:S(2)}, u32[]{:S(2)}) async-start(f32[8,136,128]{2,1,0:T(8,128)} %bitcast.11), calls=%async_computation | async-start | bytes 1114112 | tf_op jit(solution)/shard_map/all_to_all | solution.py:37
  17.7 12.4 %all-to-all-done = f32[8,136,128]{2,1,0:T(8,128)S(1)} async-done(((f32[8,136,128]{2,1,0:T(8,128)}), f32[8,136,128]{2,1,0:T(8,128)S(1)}, u32[]{:S(2)}, u32[]{:S(2)}) %all-to-all-start) | async-done | bytes 557088 | tf_op jit(solution)/shard_map/all_to_all | solution.py:37
  30.2 21.0 %all_to_all.25 = f32[8,152,128]{2,1,0:T(8,128)S(1)} all-to-all(f32[8,152,128]{2,1,0:T(8,128)S(1)} %broadcast_in_dim.27), channel_id=1, replica_groups={{0,64,128,192,256,320,384,448},{8,72,136,200,264,328,392,456},{16,80,14..., dimensions={0} | all-to-all | bytes 1245184 | tf_op jit(solution)/shard_map/all_to_all | solution.py:37
  51.2 0.1 copy.29
  51.4 0.1 broadcast_in_dim.28
  51.5 0.0 copy-start.4
  51.5 0.0 copy-start.7
  51.5 20.8 %all_to_all.26.recv = f32[8,264,128]{2,1,0:T(8,128)S(1)} all-to-all(f32[8,264,128]{2,1,0:T(8,128)S(1)} %broadcast_in_dim.28), channel_id=1, replica_groups={{0,8,16,24,32,40,48,56},{64,72,80,88,96,104,112,120},{128,136,144,152,1..., dimensions={0} | all-to-all | bytes 2162688 | tf_op jit(solution)/shard_map/all_to_all | solution.py:37
  72.2 0.0 copy-done.4
  72.3 0.0 copy-done.7
  72.3 1.2 %shard_map.190 = (f32[4,32,1152]{2,1,0:T(8,128)S(1)}, f32[32,128]{1,0:T(8,128)}) custom-call(s32[2]{0:T(128)S(1)} %pad_add_fusion.1.spot, f32[8,264,128]{2,1,0:T(8,128)S(1)} %all_to_all.26.recv, f32[32,128]{1,0:T(8,128)S(1)} %bitcast.50, f32[32,1024]{1,0:T(8,128)S(1)} %bitcast.45), custom_call_target="tpu_custom_call" | custom-call | tf_op jit(solution)/shard_map/pallas_call | solution.py:316
  73.4 11.1 %all_to_all.27.got = f32[4,32,1152]{2,1,0:T(8,128)S(1)} all-to-all(f32[4,32,1152]{2,1,0:T(8,128)S(1)} %get-tuple-element.30), channel_id=1, replica_groups=mesh['shard'=128,'tensor'=4] {'tensor'}, dimensions={0} | all-to-all | bytes 1179648 | tf_op jit(solution)/shard_map/all_to_all | solution.py:391
  84.5 4.3 %shard_map.191 = (f32[4,32,1152]{2,1,0:T(8,128)}, f32[32,128]{1,0:T(8,128)S(1)}) custom-call(s32[2]{0:T(128)S(1)} %pad_add_fusion.1.spot, f32[8,264,128]{2,1,0:T(8,128)S(1)} %all_to_all.26.recv, f32[4,32,1152]{2,1,0:T(8,128)S(1)} %all_to_all.27.got), custom_call_target="tpu_custom_call" | custom-call | tf_op jit(solution)/shard_map/pallas_call | solution.py:316
  88.9 3.5 %all-to-all-start.4 = ((f32[4,32,1152]{2,1,0:T(8,128)}), f32[4,32,1152]{2,1,0:T(8,128)S(1)}, u32[]{:S(2)}, u32[]{:S(2)}) async-start(f32[4,32,1152]{2,1,0:T(8,128)} %get-tuple-element.33), calls=%async_computation.4 | async-start | bytes 1179648 | tf_op jit(solution)/shard_map/all_to_all | solution.py:391
  92.5 0.0 copy-start.8
  92.5 0.2 copy.31
  92.7 0.9 bitcast_select_fusion
  93.5 7.3 %collective-permute-start.1 = (f32[1024,128]{1,0:T(8,128)}, f32[1024,128]{1,0:T(8,128)}, u32[]{:S(2)}, u32[]{:S(2)}) collective-permute-start(f32[1024,128]{1,0:T(8,128)} %bitcast.20.refs_0_), channel_id=1, source_target_pairs={{0,4},{4,0},{8,12},{12,8},{16,20},{20,16},{24,28},{28,24},{32,36},... | collective-permute-start | bytes 1572872 | tf_op jit(solution)/shard_map/ppermute | solution.py:33
  100.9 0.0 copy-done.8
  100.9 1.2 shard_map.192
  102.1 0.0 copy-start
  102.1 0.0 copy-start.1
  102.1 0.0 copy-start.2
  102.1 0.0 copy-start.3
  102.1 0.0 copy-start.5
  102.1 0.0 copy-start.6
  102.1 0.0 all-to-all-done.4.got
  102.1 3.5 %shard_map.193.refs_1_ = f32[32,1152]{1,0:T(8,128)S(1)} custom-call(s32[2]{0:T(128)S(1)} %pad_add_fusion.1.spot, f32[8,264,128]{2,1,0:T(8,128)S(1)} %all_to_all.26.recv, f32[4,32,1152]{2,1,0:T(8,128)S(1)} %all-to-all-done.4.got, f32[32,128]{1,0:T(8,128)S(1)} %get-tuple-element.37.narrow), custom_call_target="tpu_custom_call" | custom-call | tf_op jit(solution)/shard_map/pallas_call | solution.py:316
  105.6 5.8 %collective-permute-start.2 = (f32[32,1152]{1,0:T(8,128)S(1)}, f32[32,1152]{1,0:T(8,128)S(1)}, u32[]{:S(2)}, u32[]{:S(2)}) collective-permute-start(f32[32,1152]{1,0:T(8,128)S(1)} %shard_map.193.refs_1_), channel_id=1, source_target_pairs={{0,4},{4,0},{8,12},{12,8},{16,20},{20,16},{24,28},{28,24},{32,36},... | collective-permute-start | bytes 442376 | tf_op jit(solution)/shard_map/ppermute | solution.py:33
  111.3 0.0 copy-done
  111.4 0.0 copy-done.1
  111.4 0.0 copy-done.2
  111.4 0.0 copy-done.3
  111.4 0.0 copy-done.5
  111.4 0.0 copy-done.6
  111.4 2.6 %shard_map.194 = (f32[1024,128]{1,0:T(8,128)}, f32[128,1024]{1,0:T(8,128)}, f32[8,128]{1,0:T(8,128)}, f32[8,128]{1,0:T(8,128)}, f32[1024,128]{1,0:T(8,128)}, /*index=5*/f32[128,1024]{1,0:T(8,128)}) custom-call(s32[2]{0:T(128)S(1)} %pad_add_fusion.1.spot, f32[1024,128]{1,0:T(8,128)} %bitcast.20.refs_0_, f32[32,1152]{1,0:T(8,128)S(1)} %shard_map.193.refs_1_, ...), custom_call_target="tpu_custom_call" | custom-call | tf_op jit(solution)/shard_map/pallas_call | solution.py:316
  114.0 0.0 collective-permute-done.1.refs_6_
  114.0 0.0 collective-permute-done.2.refs_7_
  114.0 2.6 %shard_map.195 = (f32[1024,128]{1,0:T(8,128)}, f32[128,1024]{1,0:T(8,128)}, f32[8,128]{1,0:T(8,128)}, f32[8,128]{1,0:T(8,128)}, f32[1024,128]{1,0:T(8,128)}, /*index=5*/f32[128,1024]{1,0:T(8,128)}) custom-call(s32[2]{0:T(128)S(1)} %pad_add_fusion.spot, ...), custom_call_target="tpu_custom_call", output_to_operand_aliasing={{0}: (1, {}), {1}: (2, {}), {2}: (3, {}), {3}: (4, {}), {4}... | custom-call | tf_op jit(solution)/shard_map/pallas_call | solution.py:316
  (14 shorter events, 0.2 us)
Async XLA Ops:
  2.5 10.7 %collective-permute-start = (f32[1096,128]{1,0:T(8,128)S(1)}, f32[1096,128]{1,0:T(8,128)S(1)}, u32[]{:S(2)}, u32[]{:S(2)}) collective-permute-start(f32[1096,128]{1,0:T(8,128)S(1)} %shard_map.189), channel_id=1, source_target_pairs={{0,4},{4,0},{8,12},{12,8},{16,20},{20,16},{24,28},{28,24},{32,36},... | collective-permute-start | bytes 1683464 | tf_op jit(solution)/shard_map/ppermute | solution.py:33
  14.1 15.9 %all-to-all-start = ((f32[8,136,128]{2,1,0:T(8,128)}), f32[8,136,128]{2,1,0:T(8,128)S(1)}, u32[]{:S(2)}, u32[]{:S(2)}) async-start(f32[8,136,128]{2,1,0:T(8,128)} %bitcast.11), calls=%async_computation | async-start | bytes 1114112 | tf_op jit(solution)/shard_map/all_to_all | solution.py:37
  51.5 20.8 %copy-start.4 = (f32[1024,32]{0,1:T(8,128)S(1)}, f32[1024,32]{0,1:T(8,128)}, u32[]{:S(2)}) copy-start(f32[1024,32]{0,1:T(8,128)} %param.18) | copy-start | bytes 393220
  51.5 20.8 %copy-start.7 = (f32[128,32]{0,1:T(8,128)S(1)}, f32[128,32]{0,1:T(8,128)}, u32[]{:S(2)}) copy-start(f32[128,32]{0,1:T(8,128)} %param.17) | copy-start | bytes 49156
  88.9 13.2 %all-to-all-start.4 = ((f32[4,32,1152]{2,1,0:T(8,128)}), f32[4,32,1152]{2,1,0:T(8,128)S(1)}, u32[]{:S(2)}, u32[]{:S(2)}) async-start(f32[4,32,1152]{2,1,0:T(8,128)} %get-tuple-element.33), calls=%async_computation.4 | async-start | bytes 1179648 | tf_op jit(solution)/shard_map/all_to_all | solution.py:391
  92.5 8.4 %copy-start.8 = (f32[28]{0:T(128)S(1)}, f32[28]{0:T(128)}, u32[]{:S(2)}) copy-start(f32[28]{0:T(128)} %param.24) | copy-start | bytes 340
  93.5 20.5 %collective-permute-start.1 = (f32[1024,128]{1,0:T(8,128)}, f32[1024,128]{1,0:T(8,128)}, u32[]{:S(2)}, u32[]{:S(2)}) collective-permute-start(f32[1024,128]{1,0:T(8,128)} %bitcast.20.refs_0_), channel_id=1, source_target_pairs={{0,4},{4,0},{8,12},{12,8},{16,20},{20,16},{24,28},{28,24},{32,36},... | collective-permute-start | bytes 1572872 | tf_op jit(solution)/shard_map/ppermute | solution.py:33
  102.1 9.3 %copy-start = (f32[1,1024,128]{2,1,0:T(8,128)S(1)}, f32[1,1024,128]{2,1,0:T(8,128)}, u32[]{:S(2)}) copy-start(f32[1,1024,128]{2,1,0:T(8,128)} %param.14) | copy-start | bytes 1572868
  102.1 9.3 %copy-start.1 = (f32[1,128,1024]{2,1,0:T(8,128)S(1)}, f32[1,128,1024]{2,1,0:T(8,128)}, u32[]{:S(2)}) copy-start(f32[1,128,1024]{2,1,0:T(8,128)} %param.16) | copy-start | bytes 1572868
  102.1 9.3 %copy-start.2 = (bf16[1,1024,128]{2,1,0:T(8,128)(2,1)S(1)}, bf16[1,1024,128]{2,1,0:T(8,128)(2,1)}, u32[]{:S(2)}) copy-start(bf16[1,1024,128]{2,1,0:T(8,128)(2,1)} %param.13) | copy-start | bytes 786436
  102.1 9.3 %copy-start.3 = (bf16[1,128,1024]{2,1,0:T(8,128)(2,1)S(1)}, bf16[1,128,1024]{2,1,0:T(8,128)(2,1)}, u32[]{:S(2)}) copy-start(bf16[1,128,1024]{2,1,0:T(8,128)(2,1)} %param.15) | copy-start | bytes 786436
  102.1 9.3 %copy-start.5 = (f32[8,128]{1,0:T(8,128)S(1)}, f32[8,128]{1,0:T(8,128)}, u32[]{:S(2)}) copy-start(f32[8,128]{1,0:T(8,128)} %refs_12_.1) | copy-start | bytes 12292
  102.1 9.3 %copy-start.6 = (f32[128,8]{0,1:T(8,128)S(1)}, f32[128,8]{0,1:T(8,128)}, u32[]{:S(2)}) copy-start(f32[128,8]{0,1:T(8,128)} %param.22) | copy-start | bytes 12292
  105.6 8.4 %collective-permute-start.2 = (f32[32,1152]{1,0:T(8,128)S(1)}, f32[32,1152]{1,0:T(8,128)S(1)}, u32[]{:S(2)}, u32[]{:S(2)}) collective-permute-start(f32[32,1152]{1,0:T(8,128)S(1)} %shard_map.193.refs_1_), channel_id=1, source_target_pairs={{0,4},{4,0},{8,12},{12,8},{16,20},{20,16},{24,28},{28,24},{32,36},... | collective-permute-start | bytes 442376 | tf_op jit(solution)/shard_map/ppermute | solution.py:33

commit v8 on v7

--- a/solution.py
+++ b/solution.py
@@ -53,27 +53,26 @@
     ]
     done = [jnp.zeros((8, LANES), jnp.float32) for _ in range(tiles)]
     wide = (8, LANES)
-    for k in range(0, rank, 2):
+    panel = 8
+    for k in range(0, rank, panel):
         at, place = k // 8, k % 8
-        near = [jnp.broadcast_to(rows[t][:, k:k + 1], wide) for t in range(at, tiles)]
-        far = [jnp.broadcast_to(rows[t][:, k + 1:k + 2], wide) for t in range(at, tiles)]
-        upper = jnp.broadcast_to(rows[at][place:place + 1], wide)
-        lower = jnp.broadcast_to(rows[at][place + 1:place + 2], wide)
-        pivot = jnp.broadcast_to(near[0][place:place + 1], wide)
-        below = jnp.broadcast_to(near[0][place + 1:place + 2], wide)
-        corner = jnp.broadcast_to(far[0][place + 1:place + 2], wide)
-        inverse = 1.0 / pivot
-        ratio = below * inverse
-        second = corner - below * ratio
-        lower = lower - ratio * upper
-        done[at] = jnp.where(sub == place, upper * lax.rsqrt(pivot), done[at])
-        done[at] = jnp.where(sub == place + 1, lower * lax.rsqrt(second), done[at])
-        upper = upper * inverse
-        lower = lower * (1.0 / second)
-        for t in range(at, tiles):
-            one, two = near[t - at], far[t - at]
-            take = one * upper + (two - one * ratio) * lower
-            rows[t] = rows[t] - (jnp.where(sub > place + 1, take, 0.0) if t == at else take)
+        below = range(at, tiles)
+        columns = [[jnp.broadcast_to(rows[t][:, k + i:k + i + 1], wide) for t in below] for i in range(panel)]
+        lines = [jnp.broadcast_to(rows[at][place + i:place + i + 1], wide) for i in range(panel)]
+        for i in range(panel):
+            pivot = jnp.broadcast_to(columns[i][0][place + i:place + i + 1], wide)
+            inverse = 1.0 / pivot
+            done[at] = jnp.where(sub == place + i, lines[i] * lax.rsqrt(pivot), done[at])
+            scaled = lines[i] * inverse
+            for l in range(i + 1, panel):
+                entry = jnp.broadcast_to(columns[i][0][place + l:place + l + 1], wide)
+                ratio = entry * inverse
+                lines[l] = lines[l] - entry * scaled
+                columns[l] = [one - two * ratio for one, two in zip(columns[l], columns[i])]
+            lines[i] = scaled
+        for t in below:
+            take = sum(columns[i][t - at] * lines[i] for i in range(panel))
+            rows[t] = rows[t] - (jnp.where(sub >= place + panel, take, 0.0) if t == at else take)
     return pltpu.roll(jnp.concatenate(done), half, 1)
 
 
@@ -170,11 +169,13 @@
     scale = 1.0 / shards
     load = pltpu.make_async_copy(old, kept, sems.at[2, 0])
     load.start()
-    along = spot[0] * rows
-    base = pl.multiple_of(along // LANES * LANES, LANES)
-    picked = pltpu.roll(factors[:, pl.ds(base, LANES)], (LANES - along % LANES) % LANES, 1)
     narrow = factors[:, height:] * scale
-    change = dot(picked, narrow, ((0,), (0,)))[:rows]
+
+    def change():
+        along = spot[0] * rows
+        base = pl.multiple_of(along // LANES * LANES, LANES)
+        picked = pltpu.roll(factors[:, pl.ds(base, LANES)], (LANES - along % LANES) % LANES, 1)
+        return dot(picked, narrow, ((0,), (0,)))[:rows]
 
     def parts(j):
         down = pl.ds(j * block, block)
@@ -182,9 +183,7 @@
 
     @pl.when(spot[1] == 0)
     def _():
-        moment[...] = 0.9 * moment_query[...] + change
-        copies = [pltpu.make_async_copy(moment, new_moment_query, sems.at[2, 1])]
-        copies[0].start()
+        copies = []
         for j in range(ring):
             at, down = parts(j)
             approx = dot(factors[:, down], narrow, ((0,), (0,)))
@@ -192,6 +191,9 @@
             weight_q[down] = -0.01 * approx
             copies.append(pltpu.make_async_copy(error_q.at[at], new_error_query.at[at], sems.at[0, j]))
             copies[-1].start()
+        moment[...] = 0.9 * moment_query[...] + change()
+        copies.append(pltpu.make_async_copy(moment, new_moment_query, sems.at[2, 1]))
+        copies[-1].start()
         load.wait()
         for j in range(ring):
             at, down = parts(j)
@@ -203,9 +205,7 @@
 
     @pl.when(spot[1] == 1)
     def _():
-        moment[...] = 0.9 * moment_output[...] + change
-        copies = [pltpu.make_async_copy(moment, new_moment_output, sems.at[2, 1])]
-        copies[0].start()
+        copies = []
         for j in range(ring):
             at, down = parts(j)
             approx = dot(narrow, factors[:, down], ((0,), (0,)))
@@ -213,6 +213,9 @@
             weight_o[:, down] = -0.01 * approx
             copies.append(pltpu.make_async_copy(error_o.at[:, at], new_error_output.at[:, at], sems.at[0, j]))
             copies[-1].start()
+        moment[...] = 0.9 * moment_output[...] + change()
+        copies.append(pltpu.make_async_copy(moment, new_moment_output, sems.at[2, 1]))
+        copies[-1].start()
         load.wait()
         for j in range(ring):
             at, down = parts(j)
@@ -374,10 +377,12 @@
     got = swap_cores(prelude(swapped), shards)
     mine = prelude(spot)
     summed = (mine[:ring * tall] + got[:ring * tall]).reshape(ring, tall, LANES)
+    summed = exchange(summed, first)
+    summed, mine, got = lax.optimization_barrier((summed, mine, got))
     own_kept, got_kept = mine[ring * tall:], got[ring * tall:]
     pair_kept = jnp.where(asks, jnp.concatenate([got_kept, own_kept]), jnp.concatenate([own_kept, got_kept]))
 
-    part = exchange(summed, first).sum(0)
+    part = summed.sum(0)
     every = share(jnp.concatenate([part, pair_kept]), second, ring)
     whole = every[:, :tall].sum(0)
     square = jnp.where(asks, whole[:block], whole[:block].T)

time: 117 us -> 115 us (0.983)
  Pallas kernels: 19 us -> 16.3 us
    pallas_call x8, Pallas kernels: 19 us -> 16.3 us  [run(): pl.pallas_call(kernel, out_shape=out_shape, in_specs=specs, out_specs=out...]
  transfers between devices with their start and end apart: 5 -> 5, of which waited for: 1 -> 1; matrix products, arithmetic and copies ran while one was open for 1% -> 1% of each run, Pallas kernels for 8% -> 7%
where the time goes in v8:
time: 115 us; the launch traced here: 114 us
  blocking collectives  52.9 us (46%)
  starting transfers between devices  28.9 us (25%)
  Pallas kernels  16.3 us (14%)
  waiting for transfers between devices  12.4 us (11%)
  other arithmetic  1.98 us (2%)
    all_to_all x2, blocking collectives, exchange(): lax.all_to_all(value, 'shard', 0, 0, axis_index_groups=group, tiled=True)  41.8 us
    ppermute x3, starting transfers between devices, swap_cores(): return lax.ppermute(value, 'shard', [(s, s ^ 1) for s in range(shards)])  21.9 us
    pallas_call x8, Pallas kernels, run(): pl.pallas_call(kernel, out_shape=out_shape, in_specs=specs, out_specs=out...  16.3 us
    all_to_all x1, waiting for transfers between devices, exchange(): lax.all_to_all(value, 'shard', 0, 0, axis_index_groups=group, tiled=True)  12.4 us
    all_to_all x1, blocking collectives, gathered(): return lax.all_to_all(value, 'tensor', 0, 0, tiled=True)  11.1 us
    all_to_all x1, starting transfers between devices, exchange(): lax.all_to_all(value, 'shard', 0, 0, axis_index_groups=group, tiled=True)  3.54 us
    all_to_all x1, starting transfers between devices, gathered(): return lax.all_to_all(value, 'tensor', 0, 0, tiled=True)  3.49 us
  transfers between devices with their start and end apart: 5, of which 1 were waited for; matrix products, arithmetic and copies ran while one was open for 1% of the time, Pallas kernels for 7%

profile of v8, /device:TPU:1, one launch (start us, length us, event | category | flops | bytes accessed | tf_op | source)
XLA Modules:
  0.0 113.9 jit_solution(17345861967256092551)
XLA Ops:
  0.6 0.1 pad_add_fusion.spot
  0.7 1.8 %shard_map.189 = f32[1096,128]{1,0:T(8,128)S(1)} custom-call(s32[2]{0:T(128)S(1)} %pad_add_fusion.spot, bf16[1024,128]{1,0:T(8,128)(2,1)} %bitcast.37, f32[1024,128]{1,0:T(8,128)} %bitcast.29, bf16[128,1024]{1,0:T(8,128)(2,1)} %bitcast.41, f32[128,1024]{1,0:T(8,128)} %bitcast.33, bf16[1,3584]{1,0:T(2,128)(2,1)} %refs_4_.3, f32[8,128]{1,0:T(8,128)} %refs_5_.3, ...), custom_call_target="tpu_custom_call" | custom-call | tf_op jit(solution)/shard_map/pallas_call | solution.py:319
  2.5 8.8 %collective-permute-start = (f32[1096,128]{1,0:T(8,128)S(1)}, f32[1096,128]{1,0:T(8,128)S(1)}, u32[]{:S(2)}, u32[]{:S(2)}) collective-permute-start(f32[1096,128]{1,0:T(8,128)S(1)} %shard_map.189), channel_id=1, source_target_pairs={{0,4},{4,0},{8,12},{12,8},{16,20},{20,16},{24,28},{28,24},{32,36},... | collective-permute-start | bytes 1683464 | tf_op jit(solution)/shard_map/ppermute | solution.py:33
  11.3 0.1 pad_add_fusion.1.spot
  11.4 1.8 %shard_map.188 = f32[1096,128]{1,0:T(8,128)S(1)} custom-call(s32[2]{0:T(128)S(1)} %pad_add_fusion.1.spot, bf16[1024,128]{1,0:T(8,128)(2,1)} %bitcast.38, f32[1024,128]{1,0:T(8,128)} %bitcast.30, bf16[128,1024]{1,0:T(8,128)(2,1)} %bitcast.42, f32[128,1024]{1,0:T(8,128)} %bitcast.34, bf16[1,3584]{1,0:T(2,128)(2,1)} %refs_4_.3, f32[8,128]{1,0:T(8,128)} %refs_5_.3, ...), custom_call_target="tpu_custom_call" | custom-call | tf_op jit(solution)/shard_map/pallas_call | solution.py:319
  13.2 0.0 collective-permute-done
  13.2 0.9 slice_add_fusion
  14.1 3.5 %all-to-all-start = ((f32[8,136,128]{2,1,0:T(8,128)}), f32[8,136,128]{2,1,0:T(8,128)S(1)}, u32[]{:S(2)}, u32[]{:S(2)}) async-start(f32[8,136,128]{2,1,0:T(8,128)} %bitcast.11), calls=%async_computation | async-start | bytes 1114112 | tf_op jit(solution)/shard_map/all_to_all | solution.py:37
  17.7 12.4 %all-to-all-done = f32[8,136,128]{2,1,0:T(8,128)S(1)} async-done(((f32[8,136,128]{2,1,0:T(8,128)}), f32[8,136,128]{2,1,0:T(8,128)S(1)}, u32[]{:S(2)}, u32[]{:S(2)}) %all-to-all-start) | async-done | bytes 557088 | tf_op jit(solution)/shard_map/all_to_all | solution.py:37
  30.2 21.0 %all_to_all.25 = f32[8,152,128]{2,1,0:T(8,128)S(1)} all-to-all(f32[8,152,128]{2,1,0:T(8,128)S(1)} %broadcast_in_dim.27), channel_id=1, replica_groups={{0,64,128,192,256,320,384,448},{8,72,136,200,264,328,392,456},{16,80,14..., dimensions={0} | all-to-all | bytes 1245184 | tf_op jit(solution)/shard_map/all_to_all | solution.py:37
  51.3 0.1 copy.29
  51.4 0.1 broadcast_in_dim.28
  51.5 0.0 copy-start.4
  51.5 0.0 copy-start.7
  51.5 20.8 %all_to_all.26.recv = f32[8,264,128]{2,1,0:T(8,128)S(1)} all-to-all(f32[8,264,128]{2,1,0:T(8,128)S(1)} %broadcast_in_dim.28), channel_id=1, replica_groups={{0,8,16,24,32,40,48,56},{64,72,80,88,96,104,112,120},{128,136,144,152,1..., dimensions={0} | all-to-all | bytes 2162688 | tf_op jit(solution)/shard_map/all_to_all | solution.py:37
  72.3 0.0 copy-done.4
  72.3 0.0 copy-done.7
  72.3 1.2 %shard_map.190 = (f32[4,32,1152]{2,1,0:T(8,128)S(1)}, f32[32,128]{1,0:T(8,128)}) custom-call(s32[2]{0:T(128)S(1)} %pad_add_fusion.1.spot, f32[8,264,128]{2,1,0:T(8,128)S(1)} %all_to_all.26.recv, f32[32,128]{1,0:T(8,128)S(1)} %bitcast.50, f32[32,1024]{1,0:T(8,128)S(1)} %bitcast.45), custom_call_target="tpu_custom_call" | custom-call | tf_op jit(solution)/shard_map/pallas_call | solution.py:319
  73.5 11.1 %all_to_all.27.got = f32[4,32,1152]{2,1,0:T(8,128)S(1)} all-to-all(f32[4,32,1152]{2,1,0:T(8,128)S(1)} %get-tuple-element.36), channel_id=1, replica_groups=mesh['shard'=128,'tensor'=4] {'tensor'}, dimensions={0} | all-to-all | bytes 1179648 | tf_op jit(solution)/shard_map/all_to_all | solution.py:396
  84.6 3.2 %shard_map.191 = (f32[4,32,1152]{2,1,0:T(8,128)}, f32[32,128]{1,0:T(8,128)S(1)}) custom-call(s32[2]{0:T(128)S(1)} %pad_add_fusion.1.spot, f32[8,264,128]{2,1,0:T(8,128)S(1)} %all_to_all.26.recv, f32[4,32,1152]{2,1,0:T(8,128)S(1)} %all_to_all.27.got), custom_call_target="tpu_custom_call" | custom-call | tf_op jit(solution)/shard_map/pallas_call | solution.py:319
  87.7 3.5 %all-to-all-start.4 = ((f32[4,32,1152]{2,1,0:T(8,128)}), f32[4,32,1152]{2,1,0:T(8,128)S(1)}, u32[]{:S(2)}, u32[]{:S(2)}) async-start(f32[4,32,1152]{2,1,0:T(8,128)} %get-tuple-element.39), calls=%async_computation.4 | async-start | bytes 1179648 | tf_op jit(solution)/shard_map/all_to_all | solution.py:396
  91.3 0.0 copy-start.8
  91.3 0.2 copy.31
  91.5 0.9 bitcast_select_fusion
  92.4 7.3 %collective-permute-start.1 = (f32[1024,128]{1,0:T(8,128)}, f32[1024,128]{1,0:T(8,128)}, u32[]{:S(2)}, u32[]{:S(2)}) collective-permute-start(f32[1024,128]{1,0:T(8,128)} %bitcast.20.refs_0_), channel_id=1, source_target_pairs={{0,4},{4,0},{8,12},{12,8},{16,20},{20,16},{24,28},{28,24},{32,36},... | collective-permute-start | bytes 1572872 | tf_op jit(solution)/shard_map/ppermute | solution.py:33
  99.7 0.0 copy-done.8
  99.8 1.2 %shard_map.192 = (f32[1,28]{1,0:T(1,128)}, f32[28,128]{1,0:T(8,128)}) custom-call(s32[2]{0:T(128)S(1)} %pad_add_fusion.1.spot, f32[8,264,128]{2,1,0:T(8,128)S(1)} %all_to_all.26.recv, f32[1,28]{1,0:T(1,128)S(1)} %bitcast.53), custom_call_target="tpu_custom_call" | custom-call | tf_op jit(solution)/shard_map/pallas_call | solution.py:319
  100.9 0.0 copy-start
  100.9 0.0 copy-start.1
  100.9 0.0 copy-start.2
  100.9 0.0 copy-start.3
  100.9 0.0 copy-start.5
  100.9 0.0 copy-start.6
  101.0 0.0 all-to-all-done.4.got
  101.0 1.9 %shard_map.193.refs_1_ = f32[32,1152]{1,0:T(8,128)S(1)} custom-call(s32[2]{0:T(128)S(1)} %pad_add_fusion.1.spot, f32[8,264,128]{2,1,0:T(8,128)S(1)} %all_to_all.26.recv, f32[4,32,1152]{2,1,0:T(8,128)S(1)} %all-to-all-done.4.got, f32[32,128]{1,0:T(8,128)S(1)} %get-tuple-element.43.narrow), custom_call_target="tpu_custom_call" | custom-call | tf_op jit(solution)/shard_map/pallas_call | solution.py:319
  102.9 5.8 %collective-permute-start.2 = (f32[32,1152]{1,0:T(8,128)S(1)}, f32[32,1152]{1,0:T(8,128)S(1)}, u32[]{:S(2)}, u32[]{:S(2)}) collective-permute-start(f32[32,1152]{1,0:T(8,128)S(1)} %shard_map.193.refs_1_), channel_id=1, source_target_pairs={{0,4},{4,0},{8,12},{12,8},{16,20},{20,16},{24,28},{28,24},{32,36},... | collective-permute-start | bytes 442376 | tf_op jit(solution)/shard_map/ppermute | solution.py:33
  108.7 0.0 copy-done
  108.7 0.0 copy-done.1
  108.7 0.0 copy-done.2
  108.7 0.0 copy-done.3
  108.7 0.0 copy-done.5
  108.7 0.0 copy-done.6
  108.7 2.6 %shard_map.194 = (f32[1024,128]{1,0:T(8,128)}, f32[128,1024]{1,0:T(8,128)}, f32[8,128]{1,0:T(8,128)}, f32[8,128]{1,0:T(8,128)}, f32[1024,128]{1,0:T(8,128)}, /*index=5*/f32[128,1024]{1,0:T(8,128)}) custom-call(s32[2]{0:T(128)S(1)} %pad_add_fusion.1.spot, f32[1024,128]{1,0:T(8,128)} %bitcast.20.refs_0_, f32[32,1152]{1,0:T(8,128)S(1)} %shard_map.193.refs_1_, ...), custom_call_target="tpu_custom_call" | custom-call | tf_op jit(solution)/shard_map/pallas_call | solution.py:319
  111.3 0.0 collective-permute-done.1.refs_6_
  111.3 0.0 collective-permute-done.2.refs_7_
  111.3 2.6 %shard_map.195 = (f32[1024,128]{1,0:T(8,128)}, f32[128,1024]{1,0:T(8,128)}, f32[8,128]{1,0:T(8,128)}, f32[8,128]{1,0:T(8,128)}, f32[1024,128]{1,0:T(8,128)}, /*index=5*/f32[128,1024]{1,0:T(8,128)}) custom-call(s32[2]{0:T(128)S(1)} %pad_add_fusion.spot, ...), custom_call_target="tpu_custom_call", output_to_operand_aliasing={{0}: (1, {}), {1}: (2, {}), {2}: (3, {}), {3}: (4, {}), {4}... | custom-call | tf_op jit(solution)/shard_map/pallas_call | solution.py:319
  (14 shorter events, 0.2 us)
Async XLA Ops:
  2.5 10.7 %collective-permute-start = (f32[1096,128]{1,0:T(8,128)S(1)}, f32[1096,128]{1,0:T(8,128)S(1)}, u32[]{:S(2)}, u32[]{:S(2)}) collective-permute-start(f32[1096,128]{1,0:T(8,128)S(1)} %shard_map.189), channel_id=1, source_target_pairs={{0,4},{4,0},{8,12},{12,8},{16,20},{20,16},{24,28},{28,24},{32,36},... | collective-permute-start | bytes 1683464 | tf_op jit(solution)/shard_map/ppermute | solution.py:33
  14.1 15.9 %all-to-all-start = ((f32[8,136,128]{2,1,0:T(8,128)}), f32[8,136,128]{2,1,0:T(8,128)S(1)}, u32[]{:S(2)}, u32[]{:S(2)}) async-start(f32[8,136,128]{2,1,0:T(8,128)} %bitcast.11), calls=%async_computation | async-start | bytes 1114112 | tf_op jit(solution)/shard_map/all_to_all | solution.py:37
  51.5 20.8 %copy-start.4 = (f32[1024,32]{0,1:T(8,128)S(1)}, f32[1024,32]{0,1:T(8,128)}, u32[]{:S(2)}) copy-start(f32[1024,32]{0,1:T(8,128)} %param.18) | copy-start | bytes 393220
  51.5 20.8 %copy-start.7 = (f32[128,32]{0,1:T(8,128)S(1)}, f32[128,32]{0,1:T(8,128)}, u32[]{:S(2)}) copy-start(f32[128,32]{0,1:T(8,128)} %param.17) | copy-start | bytes 49156
  87.7 13.2 %all-to-all-start.4 = ((f32[4,32,1152]{2,1,0:T(8,128)}), f32[4,32,1152]{2,1,0:T(8,128)S(1)}, u32[]{:S(2)}, u32[]{:S(2)}) async-start(f32[4,32,1152]{2,1,0:T(8,128)} %get-tuple-element.39), calls=%async_computation.4 | async-start | bytes 1179648 | tf_op jit(solution)/shard_map/all_to_all | solution.py:396
  91.3 8.4 %copy-start.8 = (f32[28]{0:T(128)S(1)}, f32[28]{0:T(128)}, u32[]{:S(2)}) copy-start(f32[28]{0:T(128)} %param.24) | copy-start | bytes 340
  92.4 18.9 %collective-permute-start.1 = (f32[1024,128]{1,0:T(8,128)}, f32[1024,128]{1,0:T(8,128)}, u32[]{:S(2)}, u32[]{:S(2)}) collective-permute-start(f32[1024,128]{1,0:T(8,128)} %bitcast.20.refs_0_), channel_id=1, source_target_pairs={{0,4},{4,0},{8,12},{12,8},{16,20},{20,16},{24,28},{28,24},{32,36},... | collective-permute-start | bytes 1572872 | tf_op jit(solution)/shard_map/ppermute | solution.py:33
  100.9 7.8 %copy-start = (f32[1,1024,128]{2,1,0:T(8,128)S(1)}, f32[1,1024,128]{2,1,0:T(8,128)}, u32[]{:S(2)}) copy-start(f32[1,1024,128]{2,1,0:T(8,128)} %param.14) | copy-start | bytes 1572868
  100.9 7.8 %copy-start.1 = (f32[1,128,1024]{2,1,0:T(8,128)S(1)}, f32[1,128,1024]{2,1,0:T(8,128)}, u32[]{:S(2)}) copy-start(f32[1,128,1024]{2,1,0:T(8,128)} %param.16) | copy-start | bytes 1572868
  100.9 7.8 %copy-start.2 = (bf16[1,1024,128]{2,1,0:T(8,128)(2,1)S(1)}, bf16[1,1024,128]{2,1,0:T(8,128)(2,1)}, u32[]{:S(2)}) copy-start(bf16[1,1024,128]{2,1,0:T(8,128)(2,1)} %param.13) | copy-start | bytes 786436
  100.9 7.8 %copy-start.3 = (bf16[1,128,1024]{2,1,0:T(8,128)(2,1)S(1)}, bf16[1,128,1024]{2,1,0:T(8,128)(2,1)}, u32[]{:S(2)}) copy-start(bf16[1,128,1024]{2,1,0:T(8,128)(2,1)} %param.15) | copy-start | bytes 786436
  100.9 7.8 %copy-start.5 = (f32[8,128]{1,0:T(8,128)S(1)}, f32[8,128]{1,0:T(8,128)}, u32[]{:S(2)}) copy-start(f32[8,128]{1,0:T(8,128)} %refs_12_.1) | copy-start | bytes 12292
  100.9 7.8 %copy-start.6 = (f32[128,8]{0,1:T(8,128)S(1)}, f32[128,8]{0,1:T(8,128)}, u32[]{:S(2)}) copy-start(f32[128,8]{0,1:T(8,128)} %param.22) | copy-start | bytes 12292
  102.9 8.4 %collective-permute-start.2 = (f32[32,1152]{1,0:T(8,128)S(1)}, f32[32,1152]{1,0:T(8,128)S(1)}, u32[]{:S(2)}, u32[]{:S(2)}) collective-permute-start(f32[32,1152]{1,0:T(8,128)S(1)} %shard_map.193.refs_1_), channel_id=1, source_target_pairs={{0,4},{4,0},{8,12},{12,8},{16,20},{20,16},{24,28},{28,24},{32,36},... | collective-permute-start | bytes 442376 | tf_op jit(solution)/shard_map/ppermute | solution.py:33

commit v9 on v8

--- a/solution.py
+++ b/solution.py
@@ -183,52 +183,54 @@
 
     @pl.when(spot[1] == 0)
     def _():
-        copies = []
-        for j in range(ring):
-            at, down = parts(j)
-            approx = dot(factors[:, down], narrow, ((0,), (0,)))
-            error_q[down] = grad_query[down].astype(jnp.float32) + error_query[down] - approx
-            weight_q[down] = -0.01 * approx
-            copies.append(pltpu.make_async_copy(error_q.at[at], new_error_query.at[at], sems.at[0, j]))
-            copies[-1].start()
-        moment[...] = 0.9 * moment_query[...] + change()
-        copies.append(pltpu.make_async_copy(moment, new_moment_query, sems.at[2, 1]))
-        copies[-1].start()
-        load.wait()
-        for j in range(ring):
-            at, down = parts(j)
-            weight_q[down] = kept[down] + weight_q[down]
-            copies.append(pltpu.make_async_copy(weight_q.at[at], new_weight_query.at[at], sems.at[1, j]))
-            copies[-1].start()
+        copies = [pltpu.make_async_copy(moment, new_moment_query, sems.at[2, 1])]
+        for start in (0, ring // 2):
+            for j in range(start, start + ring // 2):
+                at, down = parts(j)
+                approx = dot(factors[:, down], narrow, ((0,), (0,)))
+                error_q[down] = grad_query[down].astype(jnp.float32) + error_query[down] - approx
+                weight_q[down] = -0.01 * approx
+                copies.append(pltpu.make_async_copy(error_q.at[at], new_error_query.at[at], sems.at[0, j]))
+                copies[-1].start()
+            if start == 0:
+                moment[...] = 0.9 * moment_query[...] + change()
+                copies[0].start()
+                load.wait()
+            for j in range(start, start + ring // 2):
+                at, down = parts(j)
+                weight_q[down] = kept[down] + weight_q[down]
+                copies.append(pltpu.make_async_copy(weight_q.at[at], new_weight_query.at[at], sems.at[1, j]))
+                copies[-1].start()
         for copy in copies:
             copy.wait()
 
     @pl.when(spot[1] == 1)
     def _():
-        copies = []
-        for j in range(ring):
-            at, down = parts(j)
-            approx = dot(narrow, factors[:, down], ((0,), (0,)))
-            error_o[:, down] = grad_output[:, down].astype(jnp.float32) + error_output[:, down] - approx
-            weight_o[:, down] = -0.01 * approx
-            copies.append(pltpu.make_async_copy(error_o.at[:, at], new_error_output.at[:, at], sems.at[0, j]))
-            copies[-1].start()
-        moment[...] = 0.9 * moment_output[...] + change()
-        copies.append(pltpu.make_async_copy(moment, new_moment_output, sems.at[2, 1]))
-        copies[-1].start()
-        load.wait()
-        for j in range(ring):
-            at, down = parts(j)
-            weight_o[:, down] = kept[down] + weight_o[:, down]
-            copies.append(pltpu.make_async_copy(weight_o.at[:, at], new_weight_output.at[:, at], sems.at[1, j]))
-            copies[-1].start()
+        copies = [pltpu.make_async_copy(moment, new_moment_output, sems.at[2, 1])]
+        for start in (0, ring // 2):
+            for j in range(start, start + ring // 2):
+                at, down = parts(j)
+                approx = dot(narrow, factors[:, down], ((0,), (0,)))
+                error_o[:, down] = grad_output[:, down].astype(jnp.float32) + error_output[:, down] - approx
+                weight_o[:, down] = -0.01 * approx
+                copies.append(pltpu.make_async_copy(error_o.at[:, at], new_error_output.at[:, at], sems.at[0, j]))
+                copies[-1].start()
+            if start == 0:
+                moment[...] = 0.9 * moment_output[...] + change()
+                copies[0].start()
+                load.wait()
+            for j in range(start, start + ring // 2):
+                at, down = parts(j)
+                weight_o[:, down] = kept[down] + weight_o[:, down]
+                copies.append(pltpu.make_async_copy(weight_o.at[:, at], new_weight_output.at[:, at], sems.at[1, j]))
+                copies[-1].start()
         for copy in copies:
             copy.wait()
 
 
 def prelude_kernel(ring, per, slot, vec, spot, *refs):
-    far, total, near, (line, sems) = refs[:11], refs[11], refs[12:23], refs[23:]
-    moves = [pltpu.make_async_copy(*pair, sems.at[n]) for n, pair in enumerate(zip(far, near))]
+    far, total, near, (line, sems, big) = refs[:11], refs[11], refs[12:23], refs[23:]
+    moves = [pltpu.make_async_copy(far[n], near[n], sems.at[n]) for n in range(4, 11)]
     grad_q, error_q, grad_o, error_o, grad_vector, weight_query, moment_query, weight_output, moment_output = near[:9]
     weight_vector, moment_vector = near[9:]
     height, width = grad_q.shape
@@ -238,19 +240,29 @@
     small = weight_vector.shape[1]
     index, which = spot[0], spot[1]
 
+    span = ring // 2 * block // max(ring // 4, 1)
+    pieces = [pl.ds(n * span, span) for n in range(height // span)]
+    down = [[pltpu.make_async_copy(far[a].at[p], near[a].at[p], big.at[a, n]) for a in (0, 1)] for n, p in enumerate(pieces)]
+    across = [
+        [pltpu.make_async_copy(far[a].at[:, p], near[a].at[:, p], big.at[a - 2, n]) for a in (2, 3)]
+        for n, p in enumerate(pieces)
+    ]
+
     @pl.when(which == 0)
     def _():
-        moves[0].start()
-        moves[1].start()
+        for pair in down:
+            for move in pair:
+                move.start()
 
     @pl.when(which == 1)
     def _():
-        moves[2].start()
-        moves[3].start()
-
-    for move in moves[4:]:
+        for pair in across:
+            for move in pair:
+                move.start()
+
+    for move in moves:
         move.start()
-    for move in moves[4:]:
+    for move in moves:
         move.wait()
     line[...] = jnp.zeros_like(line)
     line[0:1, :small] = weight_vector[...] - 0.009 * moment_vector[...]
@@ -271,20 +283,22 @@
     @pl.when(which == 0)
     def _():
         total[ring * tall:] = weight_query[...] - 0.009 * moment_query[...]
-        moves[0].wait()
-        moves[1].wait()
         for j in range(ring):
-            down = slice(j * block, (j + 1) * block)
-            total[j * tall:j * tall + block] = grad_q[down].astype(jnp.float32) + error_q[down]
+            if j * block % span == 0:
+                for move in down[j * block // span]:
+                    move.wait()
+            at = slice(j * block, (j + 1) * block)
+            total[j * tall:j * tall + block] = grad_q[at].astype(jnp.float32) + error_q[at]
 
     @pl.when(which == 1)
     def _():
         total[ring * tall:] = weight_output[...] - 0.009 * moment_output[...]
-        moves[2].wait()
-        moves[3].wait()
         for j in range(ring):
-            down = slice(j * block, (j + 1) * block)
-            total[j * tall:j * tall + block] = grad_o[:, down].astype(jnp.float32) + error_o[:, down]
+            if j * block % span == 0:
+                for move in across[j * block // span]:
+                    move.wait()
+            at = slice(j * block, (j + 1) * block)
+            total[j * tall:j * tall + block] = grad_o[:, at].astype(jnp.float32) + error_o[:, at]
 
 
 def vector_kernel(block, per, shards, spot, recv, moment_vector, new_moment, new_weight, mean, kept):
@@ -369,6 +383,7 @@
             [
                 *(pltpu.VMEM(value.shape, value.dtype) for value in given),
                 pltpu.VMEM((8, LANES), jnp.float32), pltpu.SemaphoreType.DMA((len(given),)),
+                pltpu.SemaphoreType.DMA((2, ring)),
             ],
             outside=len(given),
         )
@@ -377,12 +392,11 @@
     got = swap_cores(prelude(swapped), shards)
     mine = prelude(spot)
     summed = (mine[:ring * tall] + got[:ring * tall]).reshape(ring, tall, LANES)
-    summed = exchange(summed, first)
-    summed, mine, got = lax.optimization_barrier((summed, mine, got))
     own_kept, got_kept = mine[ring * tall:], got[ring * tall:]
     pair_kept = jnp.where(asks, jnp.concatenate([got_kept, own_kept]), jnp.concatenate([own_kept, got_kept]))
-
-    part = summed.sum(0)
+    summed, pair_kept = lax.optimization_barrier((summed, pair_kept))
+
+    part = exchange(summed, first).sum(0)
     every = share(jnp.concatenate([part, pair_kept]), second, ring)
     whole = every[:, :tall].sum(0)
     square = jnp.where(asks, whole[:block], whole[:block].T)

time: 115 us -> 115 us (level)
  blocking collectives: 52.9 us -> 68.7 us
  waiting for transfers between devices: 12.4 us -> 0.01 us
  starting transfers between devices: 28.9 us -> 25.3 us
    all_to_all x2 -> x3, blocking collectives: 41.8 us -> 57.6 us  [exchange(): lax.all_to_all(value, 'shard', 0, 0, axis_index_groups=group, tiled=True)]
    all_to_all x1 -> x0, waiting for transfers between devices: 12.4 us -> none  [exchange(): lax.all_to_all(value, 'shard', 0, 0, axis_index_groups=group, tiled=True)]
    all_to_all x1 -> x0, starting transfers between devices: 3.54 us -> none  [exchange(): lax.all_to_all(value, 'shard', 0, 0, axis_index_groups=group, tiled=True)]
    pallas_call x8, Pallas kernels: 16.3 us -> 17.4 us  [run(): pl.pallas_call(kernel, out_shape=out_shape, in_specs=specs, out_specs=out...]
  transfers between devices with their start and end apart: 5 -> 4, of which waited for: 1 -> 0; matrix products, arithmetic and copies ran while one was open for 1% -> 1% of each run, Pallas kernels for 7% -> 7%
where the time goes in v9:
time: 115 us; the launch traced here: 114 us
  blocking collectives  68.7 us (60%)
  starting transfers between devices  25.3 us (22%)
  Pallas kernels  17.4 us (15%)
  other arithmetic  1.17 us (1%)
    all_to_all x3, blocking collectives, exchange(): lax.all_to_all(value, 'shard', 0, 0, axis_index_groups=group, tiled=True)  57.6 us
    ppermute x3, starting transfers between devices, swap_cores(): return lax.ppermute(value, 'shard', [(s, s ^ 1) for s in range(shards)])  21.8 us
    pallas_call x8, Pallas kernels, run(): pl.pallas_call(kernel, out_shape=out_shape, in_specs=specs, out_specs=out...  17.4 us
    all_to_all x1, blocking collectives, gathered(): return lax.all_to_all(value, 'tensor', 0, 0, tiled=True)  11.1 us
    all_to_all x1, starting transfers between devices, gathered(): return lax.all_to_all(value, 'tensor', 0, 0, tiled=True)  3.49 us
  transfers between devices with their start and end apart: 4, of which 0 were waited for; matrix products, arithmetic and copies ran while one was open for 1% of the time, Pallas kernels for 7%

profile of v9, /device:TPU:1, one launch (start us, length us, event | category | flops | bytes accessed | tf_op | source)
XLA Modules:
  0.0 114.1 jit_solution(10685552244724365405)
XLA Ops:
  0.6 0.1 pad_add_fusion.spot
  0.7 2.1 %shard_map.189 = f32[1096,128]{1,0:T(8,128)S(1)} custom-call(s32[2]{0:T(128)S(1)} %pad_add_fusion.spot, bf16[1024,128]{1,0:T(8,128)(2,1)} %bitcast.37, f32[1024,128]{1,0:T(8,128)} %bitcast.29, bf16[128,1024]{1,0:T(8,128)(2,1)} %bitcast.41, f32[128,1024]{1,0:T(8,128)} %bitcast.33, bf16[1,3584]{1,0:T(2,128)(2,1)} %refs_4_.3, f32[8,128]{1,0:T(8,128)} %refs_5_.3, ...), custom_call_target="tpu_custom_call" | custom-call | tf_op jit(solution)/shard_map/pallas_call | solution.py:333
  2.8 8.7 %collective-permute-start = (f32[1096,128]{1,0:T(8,128)S(1)}, f32[1096,128]{1,0:T(8,128)S(1)}, u32[]{:S(2)}, u32[]{:S(2)}) collective-permute-start(f32[1096,128]{1,0:T(8,128)S(1)} %shard_map.189), channel_id=1, source_target_pairs={{0,4},{4,0},{8,12},{12,8},{16,20},{20,16},{24,28},{28,24},{32,36},... | collective-permute-start | bytes 1683464 | tf_op jit(solution)/shard_map/ppermute | solution.py:33
  11.5 0.1 pad_add_fusion.1.spot
  11.6 2.0 %shard_map.188 = f32[1096,128]{1,0:T(8,128)S(1)} custom-call(s32[2]{0:T(128)S(1)} %pad_add_fusion.1.spot, bf16[1024,128]{1,0:T(8,128)(2,1)} %bitcast.38, f32[1024,128]{1,0:T(8,128)} %bitcast.30, bf16[128,1024]{1,0:T(8,128)(2,1)} %bitcast.42, f32[128,1024]{1,0:T(8,128)} %bitcast.34, bf16[1,3584]{1,0:T(2,128)(2,1)} %refs_4_.3, f32[8,128]{1,0:T(8,128)} %refs_5_.3, ...), custom_call_target="tpu_custom_call" | custom-call | tf_op jit(solution)/shard_map/pallas_call | solution.py:333
  13.6 0.0 collective-permute-done
  13.7 0.1 slice_add_fusion
  13.7 14.9 %all_to_all.25 = f32[8,136,128]{2,1,0:T(8,128)S(1)} all-to-all(f32[8,136,128]{2,1,0:T(8,128)S(1)} %bitcast.54), channel_id=1, replica_groups={{0,8,16,24,32,40,48,56},{64,72,80,88,96,104,112,120},{128,136,144,152,1..., dimensions={0} | all-to-all | bytes 1114112 | tf_op jit(solution)/shard_map/all_to_all | solution.py:37
  28.7 21.9 %all_to_all.26 = f32[8,152,128]{2,1,0:T(8,128)S(1)} all-to-all(f32[8,152,128]{2,1,0:T(8,128)S(1)} %broadcast_in_dim.27), channel_id=1, replica_groups={{0,64,128,192,256,320,384,448},{8,72,136,200,264,328,392,456},{16,80,14..., dimensions={0} | all-to-all | bytes 1245184 | tf_op jit(solution)/shard_map/all_to_all | solution.py:37
  50.7 0.1 copy.29
  50.8 0.1 broadcast_in_dim.28
  50.9 0.0 copy-start.4
  50.9 0.0 copy-start.7
  50.9 20.8 %all_to_all.27.recv = f32[8,264,128]{2,1,0:T(8,128)S(1)} all-to-all(f32[8,264,128]{2,1,0:T(8,128)S(1)} %broadcast_in_dim.28), channel_id=1, replica_groups={{0,8,16,24,32,40,48,56},{64,72,80,88,96,104,112,120},{128,136,144,152,1..., dimensions={0} | all-to-all | bytes 2162688 | tf_op jit(solution)/shard_map/all_to_all | solution.py:37
  71.7 0.0 copy-done.4
  71.7 0.0 copy-done.7
  71.7 1.2 %shard_map.190 = (f32[4,32,1152]{2,1,0:T(8,128)S(1)}, f32[32,128]{1,0:T(8,128)}) custom-call(s32[2]{0:T(128)S(1)} %pad_add_fusion.1.spot, f32[8,264,128]{2,1,0:T(8,128)S(1)} %all_to_all.27.recv, f32[32,128]{1,0:T(8,128)S(1)} %bitcast.50, f32[32,1024]{1,0:T(8,128)S(1)} %bitcast.45), custom_call_target="tpu_custom_call" | custom-call | tf_op jit(solution)/shard_map/pallas_call | solution.py:333
  72.9 11.1 %all_to_all.28.got = f32[4,32,1152]{2,1,0:T(8,128)S(1)} all-to-all(f32[4,32,1152]{2,1,0:T(8,128)S(1)} %get-tuple-element.34), channel_id=1, replica_groups=mesh['shard'=128,'tensor'=4] {'tensor'}, dimensions={0} | all-to-all | bytes 1179648 | tf_op jit(solution)/shard_map/all_to_all | solution.py:410
  84.0 3.2 %shard_map.191 = (f32[4,32,1152]{2,1,0:T(8,128)}, f32[32,128]{1,0:T(8,128)S(1)}) custom-call(s32[2]{0:T(128)S(1)} %pad_add_fusion.1.spot, f32[8,264,128]{2,1,0:T(8,128)S(1)} %all_to_all.27.recv, f32[4,32,1152]{2,1,0:T(8,128)S(1)} %all_to_all.28.got), custom_call_target="tpu_custom_call" | custom-call | tf_op jit(solution)/shard_map/pallas_call | solution.py:333
  87.2 3.5 %all-to-all-start.4 = ((f32[4,32,1152]{2,1,0:T(8,128)}), f32[4,32,1152]{2,1,0:T(8,128)S(1)}, u32[]{:S(2)}, u32[]{:S(2)}) async-start(f32[4,32,1152]{2,1,0:T(8,128)} %get-tuple-element.37), calls=%async_computation.4 | async-start | bytes 1179648 | tf_op jit(solution)/shard_map/all_to_all | solution.py:410
  90.8 0.0 copy-start.8
  90.8 0.2 copy.31
  91.0 0.9 bitcast_select_fusion
  91.9 7.3 %collective-permute-start.1 = (f32[1024,128]{1,0:T(8,128)}, f32[1024,128]{1,0:T(8,128)}, u32[]{:S(2)}, u32[]{:S(2)}) collective-permute-start(f32[1024,128]{1,0:T(8,128)} %bitcast.20.refs_0_), channel_id=1, source_target_pairs={{0,4},{4,0},{8,12},{12,8},{16,20},{20,16},{24,28},{28,24},{32,36},... | collective-permute-start | bytes 1572872 | tf_op jit(solution)/shard_map/ppermute | solution.py:33
  99.2 0.0 copy-done.8
  99.2 1.2 %shard_map.192 = (f32[1,28]{1,0:T(1,128)}, f32[28,128]{1,0:T(8,128)}) custom-call(s32[2]{0:T(128)S(1)} %pad_add_fusion.1.spot, f32[8,264,128]{2,1,0:T(8,128)S(1)} %all_to_all.27.recv, f32[1,28]{1,0:T(1,128)S(1)} %bitcast.53), custom_call_target="tpu_custom_call" | custom-call | tf_op jit(solution)/shard_map/pallas_call | solution.py:333
  100.4 0.0 copy-start
  100.4 0.0 copy-start.1
  100.4 0.0 copy-start.2
  100.4 0.0 copy-start.3
  100.4 0.0 copy-start.5
  100.4 0.0 copy-start.6
  100.4 0.0 all-to-all-done.4.got
  100.5 1.9 %shard_map.193.refs_1_ = f32[32,1152]{1,0:T(8,128)S(1)} custom-call(s32[2]{0:T(128)S(1)} %pad_add_fusion.1.spot, f32[8,264,128]{2,1,0:T(8,128)S(1)} %all_to_all.27.recv, f32[4,32,1152]{2,1,0:T(8,128)S(1)} %all-to-all-done.4.got, f32[32,128]{1,0:T(8,128)S(1)} %get-tuple-element.41.narrow), custom_call_target="tpu_custom_call" | custom-call | tf_op jit(solution)/shard_map/pallas_call | solution.py:333
  102.4 5.8 %collective-permute-start.2 = (f32[32,1152]{1,0:T(8,128)S(1)}, f32[32,1152]{1,0:T(8,128)S(1)}, u32[]{:S(2)}, u32[]{:S(2)}) collective-permute-start(f32[32,1152]{1,0:T(8,128)S(1)} %shard_map.193.refs_1_), channel_id=1, source_target_pairs={{0,4},{4,0},{8,12},{12,8},{16,20},{20,16},{24,28},{28,24},{32,36},... | collective-permute-start | bytes 442376 | tf_op jit(solution)/shard_map/ppermute | solution.py:33
  108.2 0.0 copy-done
  108.2 0.0 copy-done.1
  108.2 0.0 copy-done.2
  108.2 0.0 copy-done.3
  108.2 0.0 copy-done.5
  108.2 0.0 copy-done.6
  108.2 3.0 %shard_map.194 = (f32[1024,128]{1,0:T(8,128)}, f32[128,1024]{1,0:T(8,128)}, f32[8,128]{1,0:T(8,128)}, f32[8,128]{1,0:T(8,128)}, f32[1024,128]{1,0:T(8,128)}, /*index=5*/f32[128,1024]{1,0:T(8,128)}) custom-call(s32[2]{0:T(128)S(1)} %pad_add_fusion.1.spot, f32[1024,128]{1,0:T(8,128)} %bitcast.20.refs_0_, f32[32,1152]{1,0:T(8,128)S(1)} %shard_map.193.refs_1_, ...), custom_call_target="tpu_custom_call" | custom-call | tf_op jit(solution)/shard_map/pallas_call | solution.py:333
  111.2 0.0 collective-permute-done.1.refs_6_
  111.2 0.0 collective-permute-done.2.refs_7_
  111.2 2.9 %shard_map.195 = (f32[1024,128]{1,0:T(8,128)}, f32[128,1024]{1,0:T(8,128)}, f32[8,128]{1,0:T(8,128)}, f32[8,128]{1,0:T(8,128)}, f32[1024,128]{1,0:T(8,128)}, /*index=5*/f32[128,1024]{1,0:T(8,128)}) custom-call(s32[2]{0:T(128)S(1)} %pad_add_fusion.spot, ...), custom_call_target="tpu_custom_call", output_to_operand_aliasing={{0}: (1, {}), {1}: (2, {}), {2}: (3, {}), {3}: (4, {}), {4}... | custom-call | tf_op jit(solution)/shard_map/pallas_call | solution.py:333
  (14 shorter events, 0.2 us)
Async XLA Ops:
  2.8 10.8 %collective-permute-start = (f32[1096,128]{1,0:T(8,128)S(1)}, f32[1096,128]{1,0:T(8,128)S(1)}, u32[]{:S(2)}, u32[]{:S(2)}) collective-permute-start(f32[1096,128]{1,0:T(8,128)S(1)} %shard_map.189), channel_id=1, source_target_pairs={{0,4},{4,0},{8,12},{12,8},{16,20},{20,16},{24,28},{28,24},{32,36},... | collective-permute-start | bytes 1683464 | tf_op jit(solution)/shard_map/ppermute | solution.py:33
  50.9 20.8 %copy-start.4 = (f32[1024,32]{0,1:T(8,128)S(1)}, f32[1024,32]{0,1:T(8,128)}, u32[]{:S(2)}) copy-start(f32[1024,32]{0,1:T(8,128)} %param.18) | copy-start | bytes 393220
  50.9 20.8 %copy-start.7 = (f32[128,32]{0,1:T(8,128)S(1)}, f32[128,32]{0,1:T(8,128)}, u32[]{:S(2)}) copy-start(f32[128,32]{0,1:T(8,128)} %param.17) | copy-start | bytes 49156
  87.2 13.2 %all-to-all-start.4 = ((f32[4,32,1152]{2,1,0:T(8,128)}), f32[4,32,1152]{2,1,0:T(8,128)S(1)}, u32[]{:S(2)}, u32[]{:S(2)}) async-start(f32[4,32,1152]{2,1,0:T(8,128)} %get-tuple-element.37), calls=%async_computation.4 | async-start | bytes 1179648 | tf_op jit(solution)/shard_map/all_to_all | solution.py:410
  90.8 8.4 %copy-start.8 = (f32[28]{0:T(128)S(1)}, f32[28]{0:T(128)}, u32[]{:S(2)}) copy-start(f32[28]{0:T(128)} %param.24) | copy-start | bytes 340
  91.9 19.3 %collective-permute-start.1 = (f32[1024,128]{1,0:T(8,128)}, f32[1024,128]{1,0:T(8,128)}, u32[]{:S(2)}, u32[]{:S(2)}) collective-permute-start(f32[1024,128]{1,0:T(8,128)} %bitcast.20.refs_0_), channel_id=1, source_target_pairs={{0,4},{4,0},{8,12},{12,8},{16,20},{20,16},{24,28},{28,24},{32,36},... | collective-permute-start | bytes 1572872 | tf_op jit(solution)/shard_map/ppermute | solution.py:33
  100.4 7.8 %copy-start = (f32[1,1024,128]{2,1,0:T(8,128)S(1)}, f32[1,1024,128]{2,1,0:T(8,128)}, u32[]{:S(2)}) copy-start(f32[1,1024,128]{2,1,0:T(8,128)} %param.14) | copy-start | bytes 1572868
  100.4 7.8 %copy-start.1 = (f32[1,128,1024]{2,1,0:T(8,128)S(1)}, f32[1,128,1024]{2,1,0:T(8,128)}, u32[]{:S(2)}) copy-start(f32[1,128,1024]{2,1,0:T(8,128)} %param.16) | copy-start | bytes 1572868
  100.4 7.8 %copy-start.2 = (bf16[1,1024,128]{2,1,0:T(8,128)(2,1)S(1)}, bf16[1,1024,128]{2,1,0:T(8,128)(2,1)}, u32[]{:S(2)}) copy-start(bf16[1,1024,128]{2,1,0:T(8,128)(2,1)} %param.13) | copy-start | bytes 786436
  100.4 7.8 %copy-start.3 = (bf16[1,128,1024]{2,1,0:T(8,128)(2,1)S(1)}, bf16[1,128,1024]{2,1,0:T(8,128)(2,1)}, u32[]{:S(2)}) copy-start(bf16[1,128,1024]{2,1,0:T(8,128)(2,1)} %param.15) | copy-start | bytes 786436
  100.4 7.8 %copy-start.5 = (f32[8,128]{1,0:T(8,128)S(1)}, f32[8,128]{1,0:T(8,128)}, u32[]{:S(2)}) copy-start(f32[8,128]{1,0:T(8,128)} %refs_12_.1) | copy-start | bytes 12292
  100.4 7.8 %copy-start.6 = (f32[128,8]{0,1:T(8,128)S(1)}, f32[128,8]{0,1:T(8,128)}, u32[]{:S(2)}) copy-start(f32[128,8]{0,1:T(8,128)} %param.22) | copy-start | bytes 12292
  102.4 8.8 %collective-permute-start.2 = (f32[32,1152]{1,0:T(8,128)S(1)}, f32[32,1152]{1,0:T(8,128)S(1)}, u32[]{:S(2)}, u32[]{:S(2)}) collective-permute-start(f32[32,1152]{1,0:T(8,128)S(1)} %shard_map.193.refs_1_), channel_id=1, source_target_pairs={{0,4},{4,0},{8,12},{12,8},{16,20},{20,16},{24,28},{28,24},{32,36},... | collective-permute-start | bytes 442376 | tf_op jit(solution)/shard_map/ppermute | solution.py:33

commit v10 on v8

--- a/solution.py
+++ b/solution.py
@@ -377,12 +377,11 @@
     got = swap_cores(prelude(swapped), shards)
     mine = prelude(spot)
     summed = (mine[:ring * tall] + got[:ring * tall]).reshape(ring, tall, LANES)
-    summed = exchange(summed, first)
-    summed, mine, got = lax.optimization_barrier((summed, mine, got))
     own_kept, got_kept = mine[ring * tall:], got[ring * tall:]
     pair_kept = jnp.where(asks, jnp.concatenate([got_kept, own_kept]), jnp.concatenate([own_kept, got_kept]))
-
-    part = summed.sum(0)
+    summed, pair_kept = lax.optimization_barrier((summed, pair_kept))
+
+    part = exchange(summed, first).sum(0)
     every = share(jnp.concatenate([part, pair_kept]), second, ring)
     whole = every[:, :tall].sum(0)
     square = jnp.where(asks, whole[:block], whole[:block].T)

time: 115 us -> 113 us (0.983)
  blocking collectives: 52.9 us -> 68.6 us
  waiting for transfers between devices: 12.4 us -> 0.01 us
  starting transfers between devices: 28.9 us -> 25.4 us
    all_to_all x2 -> x3, blocking collectives: 41.8 us -> 57.5 us  [exchange(): lax.all_to_all(value, 'shard', 0, 0, axis_index_groups=group, tiled=True)]
    all_to_all x1 -> x0, waiting for transfers between devices: 12.4 us -> none  [exchange(): lax.all_to_all(value, 'shard', 0, 0, axis_index_groups=group, tiled=True)]
    all_to_all x1 -> x0, starting transfers between devices: 3.54 us -> none  [exchange(): lax.all_to_all(value, 'shard', 0, 0, axis_index_groups=group, tiled=True)]
  transfers between devices with their start and end apart: 5 -> 4, of which waited for: 1 -> 0; matrix products, arithmetic and copies ran while one was open for 1% -> 1% of each run, Pallas kernels for 7% -> 7%
where the time goes in v10:
time: 113 us
  blocking collectives  68.6 us (61%)
  starting transfers between devices  25.4 us (22%)
  Pallas kernels  16.3 us (14%)
  other arithmetic  1.17 us (1%)
    all_to_all x3, blocking collectives, exchange(): lax.all_to_all(value, 'shard', 0, 0, axis_index_groups=group, tiled=True)  57.5 us
    ppermute x3, starting transfers between devices, swap_cores(): return lax.ppermute(value, 'shard', [(s, s ^ 1) for s in range(shards)])  21.9 us
    pallas_call x8, Pallas kernels, run(): pl.pallas_call(kernel, out_shape=out_shape, in_specs=specs, out_specs=out...  16.3 us
    all_to_all x1, blocking collectives, gathered(): return lax.all_to_all(value, 'tensor', 0, 0, tiled=True)  11.1 us
    all_to_all x1, starting transfers between devices, gathered(): return lax.all_to_all(value, 'tensor', 0, 0, tiled=True)  3.49 us
  transfers between devices with their start and end apart: 4, of which 0 were waited for; matrix products, arithmetic and copies ran while one was open for 1% of the time, Pallas kernels for 7%

profile of v10, /device:TPU:1, one launch (start us, length us, event | category | flops | bytes accessed | tf_op | source)
XLA Modules:
  0.0 113.0 jit_solution(8691961210755836800)
XLA Ops:
  0.6 0.1 pad_add_fusion.spot
  0.7 1.8 %shard_map.189 = f32[1096,128]{1,0:T(8,128)S(1)} custom-call(s32[2]{0:T(128)S(1)} %pad_add_fusion.spot, bf16[1024,128]{1,0:T(8,128)(2,1)} %bitcast.37, f32[1024,128]{1,0:T(8,128)} %bitcast.29, bf16[128,1024]{1,0:T(8,128)(2,1)} %bitcast.41, f32[128,1024]{1,0:T(8,128)} %bitcast.33, bf16[1,3584]{1,0:T(2,128)(2,1)} %refs_4_.3, f32[8,128]{1,0:T(8,128)} %refs_5_.3, ...), custom_call_target="tpu_custom_call" | custom-call | tf_op jit(solution)/shard_map/pallas_call | solution.py:319
  2.5 8.8 %collective-permute-start = (f32[1096,128]{1,0:T(8,128)S(1)}, f32[1096,128]{1,0:T(8,128)S(1)}, u32[]{:S(2)}, u32[]{:S(2)}) collective-permute-start(f32[1096,128]{1,0:T(8,128)S(1)} %shard_map.189), channel_id=1, source_target_pairs={{0,4},{4,0},{8,12},{12,8},{16,20},{20,16},{24,28},{28,24},{32,36},... | collective-permute-start | bytes 1683464 | tf_op jit(solution)/shard_map/ppermute | solution.py:33
  11.3 0.1 pad_add_fusion.1.spot
  11.4 1.8 %shard_map.188 = f32[1096,128]{1,0:T(8,128)S(1)} custom-call(s32[2]{0:T(128)S(1)} %pad_add_fusion.1.spot, bf16[1024,128]{1,0:T(8,128)(2,1)} %bitcast.38, f32[1024,128]{1,0:T(8,128)} %bitcast.30, bf16[128,1024]{1,0:T(8,128)(2,1)} %bitcast.42, f32[128,1024]{1,0:T(8,128)} %bitcast.34, bf16[1,3584]{1,0:T(2,128)(2,1)} %refs_4_.3, f32[8,128]{1,0:T(8,128)} %refs_5_.3, ...), custom_call_target="tpu_custom_call" | custom-call | tf_op jit(solution)/shard_map/pallas_call | solution.py:319
  13.2 0.0 collective-permute-done
  13.3 0.1 slice_add_fusion
  13.3 14.9 %all_to_all.25 = f32[8,136,128]{2,1,0:T(8,128)S(1)} all-to-all(f32[8,136,128]{2,1,0:T(8,128)S(1)} %bitcast.54), channel_id=1, replica_groups={{0,8,16,24,32,40,48,56},{64,72,80,88,96,104,112,120},{128,136,144,152,1..., dimensions={0} | all-to-all | bytes 1114112 | tf_op jit(solution)/shard_map/all_to_all | solution.py:37
  28.3 21.9 %all_to_all.26 = f32[8,152,128]{2,1,0:T(8,128)S(1)} all-to-all(f32[8,152,128]{2,1,0:T(8,128)S(1)} %broadcast_in_dim.27), channel_id=1, replica_groups={{0,64,128,192,256,320,384,448},{8,72,136,200,264,328,392,456},{16,80,14..., dimensions={0} | all-to-all | bytes 1245184 | tf_op jit(solution)/shard_map/all_to_all | solution.py:37
  50.3 0.1 copy.29
  50.4 0.1 broadcast_in_dim.28
  50.5 0.0 copy-start.4
  50.5 0.0 copy-start.7
  50.5 20.7 %all_to_all.27.recv = f32[8,264,128]{2,1,0:T(8,128)S(1)} all-to-all(f32[8,264,128]{2,1,0:T(8,128)S(1)} %broadcast_in_dim.28), channel_id=1, replica_groups={{0,8,16,24,32,40,48,56},{64,72,80,88,96,104,112,120},{128,136,144,152,1..., dimensions={0} | all-to-all | bytes 2162688 | tf_op jit(solution)/shard_map/all_to_all | solution.py:37
  71.3 0.0 copy-done.4
  71.3 0.0 copy-done.7
  71.3 1.2 %shard_map.190 = (f32[4,32,1152]{2,1,0:T(8,128)S(1)}, f32[32,128]{1,0:T(8,128)}) custom-call(s32[2]{0:T(128)S(1)} %pad_add_fusion.1.spot, f32[8,264,128]{2,1,0:T(8,128)S(1)} %all_to_all.27.recv, f32[32,128]{1,0:T(8,128)S(1)} %bitcast.50, f32[32,1024]{1,0:T(8,128)S(1)} %bitcast.45), custom_call_target="tpu_custom_call" | custom-call | tf_op jit(solution)/shard_map/pallas_call | solution.py:319
  72.5 11.1 %all_to_all.28.got = f32[4,32,1152]{2,1,0:T(8,128)S(1)} all-to-all(f32[4,32,1152]{2,1,0:T(8,128)S(1)} %get-tuple-element.34), channel_id=1, replica_groups=mesh['shard'=128,'tensor'=4] {'tensor'}, dimensions={0} | all-to-all | bytes 1179648 | tf_op jit(solution)/shard_map/all_to_all | solution.py:395
  83.6 3.2 %shard_map.191 = (f32[4,32,1152]{2,1,0:T(8,128)}, f32[32,128]{1,0:T(8,128)S(1)}) custom-call(s32[2]{0:T(128)S(1)} %pad_add_fusion.1.spot, f32[8,264,128]{2,1,0:T(8,128)S(1)} %all_to_all.27.recv, f32[4,32,1152]{2,1,0:T(8,128)S(1)} %all_to_all.28.got), custom_call_target="tpu_custom_call" | custom-call | tf_op jit(solution)/shard_map/pallas_call | solution.py:319
  86.7 3.5 %all-to-all-start.4 = ((f32[4,32,1152]{2,1,0:T(8,128)}), f32[4,32,1152]{2,1,0:T(8,128)S(1)}, u32[]{:S(2)}, u32[]{:S(2)}) async-start(f32[4,32,1152]{2,1,0:T(8,128)} %get-tuple-element.37), calls=%async_computation.4 | async-start | bytes 1179648 | tf_op jit(solution)/shard_map/all_to_all | solution.py:395
  90.3 0.0 copy-start.8
  90.3 0.2 copy.31
  90.5 0.9 bitcast_select_fusion
  91.4 7.3 %collective-permute-start.1 = (f32[1024,128]{1,0:T(8,128)}, f32[1024,128]{1,0:T(8,128)}, u32[]{:S(2)}, u32[]{:S(2)}) collective-permute-start(f32[1024,128]{1,0:T(8,128)} %bitcast.20.refs_0_), channel_id=1, source_target_pairs={{0,4},{4,0},{8,12},{12,8},{16,20},{20,16},{24,28},{28,24},{32,36},... | collective-permute-start | bytes 1572872 | tf_op jit(solution)/shard_map/ppermute | solution.py:33
  98.8 0.0 copy-done.8
  98.8 1.2 %shard_map.192 = (f32[1,28]{1,0:T(1,128)}, f32[28,128]{1,0:T(8,128)}) custom-call(s32[2]{0:T(128)S(1)} %pad_add_fusion.1.spot, f32[8,264,128]{2,1,0:T(8,128)S(1)} %all_to_all.27.recv, f32[1,28]{1,0:T(1,128)S(1)} %bitcast.53), custom_call_target="tpu_custom_call" | custom-call | tf_op jit(solution)/shard_map/pallas_call | solution.py:319
  99.9 0.0 copy-start
  99.9 0.0 copy-start.1
  99.9 0.0 copy-start.2
  99.9 0.0 copy-start.3
  99.9 0.0 copy-start.5
  100.0 0.0 copy-start.6
  100.0 0.0 all-to-all-done.4.got
  100.0 1.9 %shard_map.193.refs_1_ = f32[32,1152]{1,0:T(8,128)S(1)} custom-call(s32[2]{0:T(128)S(1)} %pad_add_fusion.1.spot, f32[8,264,128]{2,1,0:T(8,128)S(1)} %all_to_all.27.recv, f32[4,32,1152]{2,1,0:T(8,128)S(1)} %all-to-all-done.4.got, f32[32,128]{1,0:T(8,128)S(1)} %get-tuple-element.41.narrow), custom_call_target="tpu_custom_call" | custom-call | tf_op jit(solution)/shard_map/pallas_call | solution.py:319
  101.9 5.8 %collective-permute-start.2 = (f32[32,1152]{1,0:T(8,128)S(1)}, f32[32,1152]{1,0:T(8,128)S(1)}, u32[]{:S(2)}, u32[]{:S(2)}) collective-permute-start(f32[32,1152]{1,0:T(8,128)S(1)} %shard_map.193.refs_1_), channel_id=1, source_target_pairs={{0,4},{4,0},{8,12},{12,8},{16,20},{20,16},{24,28},{28,24},{32,36},... | collective-permute-start | bytes 442376 | tf_op jit(solution)/shard_map/ppermute | solution.py:33
  107.7 0.0 copy-done
  107.7 0.0 copy-done.1
  107.7 0.0 copy-done.2
  107.7 0.0 copy-done.3
  107.7 0.0 copy-done.5
  107.7 0.0 copy-done.6
  107.7 2.6 %shard_map.194 = (f32[1024,128]{1,0:T(8,128)}, f32[128,1024]{1,0:T(8,128)}, f32[8,128]{1,0:T(8,128)}, f32[8,128]{1,0:T(8,128)}, f32[1024,128]{1,0:T(8,128)}, /*index=5*/f32[128,1024]{1,0:T(8,128)}) custom-call(s32[2]{0:T(128)S(1)} %pad_add_fusion.1.spot, f32[1024,128]{1,0:T(8,128)} %bitcast.20.refs_0_, f32[32,1152]{1,0:T(8,128)S(1)} %shard_map.193.refs_1_, ...), custom_call_target="tpu_custom_call" | custom-call | tf_op jit(solution)/shard_map/pallas_call | solution.py:319
  110.3 0.0 collective-permute-done.1.refs_6_
  110.3 0.0 collective-permute-done.2.refs_7_
  110.4 2.6 %shard_map.195 = (f32[1024,128]{1,0:T(8,128)}, f32[128,1024]{1,0:T(8,128)}, f32[8,128]{1,0:T(8,128)}, f32[8,128]{1,0:T(8,128)}, f32[1024,128]{1,0:T(8,128)}, /*index=5*/f32[128,1024]{1,0:T(8,128)}) custom-call(s32[2]{0:T(128)S(1)} %pad_add_fusion.spot, ...), custom_call_target="tpu_custom_call", output_to_operand_aliasing={{0}: (1, {}), {1}: (2, {}), {2}: (3, {}), {3}: (4, {}), {4}... | custom-call | tf_op jit(solution)/shard_map/pallas_call | solution.py:319
  (14 shorter events, 0.2 us)
Async XLA Ops:
  2.5 10.7 %collective-permute-start = (f32[1096,128]{1,0:T(8,128)S(1)}, f32[1096,128]{1,0:T(8,128)S(1)}, u32[]{:S(2)}, u32[]{:S(2)}) collective-permute-start(f32[1096,128]{1,0:T(8,128)S(1)} %shard_map.189), channel_id=1, source_target_pairs={{0,4},{4,0},{8,12},{12,8},{16,20},{20,16},{24,28},{28,24},{32,36},... | collective-permute-start | bytes 1683464 | tf_op jit(solution)/shard_map/ppermute | solution.py:33
  50.5 20.8 %copy-start.4 = (f32[1024,32]{0,1:T(8,128)S(1)}, f32[1024,32]{0,1:T(8,128)}, u32[]{:S(2)}) copy-start(f32[1024,32]{0,1:T(8,128)} %param.18) | copy-start | bytes 393220
  50.5 20.8 %copy-start.7 = (f32[128,32]{0,1:T(8,128)S(1)}, f32[128,32]{0,1:T(8,128)}, u32[]{:S(2)}) copy-start(f32[128,32]{0,1:T(8,128)} %param.17) | copy-start | bytes 49156
  86.7 13.2 %all-to-all-start.4 = ((f32[4,32,1152]{2,1,0:T(8,128)}), f32[4,32,1152]{2,1,0:T(8,128)S(1)}, u32[]{:S(2)}, u32[]{:S(2)}) async-start(f32[4,32,1152]{2,1,0:T(8,128)} %get-tuple-element.37), calls=%async_computation.4 | async-start | bytes 1179648 | tf_op jit(solution)/shard_map/all_to_all | solution.py:395
  90.3 8.4 %copy-start.8 = (f32[28]{0:T(128)S(1)}, f32[28]{0:T(128)}, u32[]{:S(2)}) copy-start(f32[28]{0:T(128)} %param.24) | copy-start | bytes 340
  91.4 18.9 %collective-permute-start.1 = (f32[1024,128]{1,0:T(8,128)}, f32[1024,128]{1,0:T(8,128)}, u32[]{:S(2)}, u32[]{:S(2)}) collective-permute-start(f32[1024,128]{1,0:T(8,128)} %bitcast.20.refs_0_), channel_id=1, source_target_pairs={{0,4},{4,0},{8,12},{12,8},{16,20},{20,16},{24,28},{28,24},{32,36},... | collective-permute-start | bytes 1572872 | tf_op jit(solution)/shard_map/ppermute | solution.py:33
  99.9 7.8 %copy-start = (f32[1,1024,128]{2,1,0:T(8,128)S(1)}, f32[1,1024,128]{2,1,0:T(8,128)}, u32[]{:S(2)}) copy-start(f32[1,1024,128]{2,1,0:T(8,128)} %param.14) | copy-start | bytes 1572868
  99.9 7.8 %copy-start.1 = (f32[1,128,1024]{2,1,0:T(8,128)S(1)}, f32[1,128,1024]{2,1,0:T(8,128)}, u32[]{:S(2)}) copy-start(f32[1,128,1024]{2,1,0:T(8,128)} %param.16) | copy-start | bytes 1572868
  99.9 7.8 %copy-start.2 = (bf16[1,1024,128]{2,1,0:T(8,128)(2,1)S(1)}, bf16[1,1024,128]{2,1,0:T(8,128)(2,1)}, u32[]{:S(2)}) copy-start(bf16[1,1024,128]{2,1,0:T(8,128)(2,1)} %param.13) | copy-start | bytes 786436
  99.9 7.8 %copy-start.3 = (bf16[1,128,1024]{2,1,0:T(8,128)(2,1)S(1)}, bf16[1,128,1024]{2,1,0:T(8,128)(2,1)}, u32[]{:S(2)}) copy-start(bf16[1,128,1024]{2,1,0:T(8,128)(2,1)} %param.15) | copy-start | bytes 786436
  99.9 7.8 %copy-start.5 = (f32[8,128]{1,0:T(8,128)S(1)}, f32[8,128]{1,0:T(8,128)}, u32[]{:S(2)}) copy-start(f32[8,128]{1,0:T(8,128)} %refs_12_.1) | copy-start | bytes 12292
  100.0 7.8 %copy-start.6 = (f32[128,8]{0,1:T(8,128)S(1)}, f32[128,8]{0,1:T(8,128)}, u32[]{:S(2)}) copy-start(f32[128,8]{0,1:T(8,128)} %param.22) | copy-start | bytes 12292
  101.9 8.4 %collective-permute-start.2 = (f32[32,1152]{1,0:T(8,128)S(1)}, f32[32,1152]{1,0:T(8,128)S(1)}, u32[]{:S(2)}, u32[]{:S(2)}) collective-permute-start(f32[32,1152]{1,0:T(8,128)S(1)} %shard_map.193.refs_1_), channel_id=1, source_target_pairs={{0,4},{4,0},{8,12},{12,8},{16,20},{20,16},{24,28},{28,24},{32,36},... | collective-permute-start | bytes 442376 | tf_op jit(solution)/shard_map/ppermute | solution.py:33
